TPU v7x, 32 devices: a whole 2x2x4 slice. The times are simulated.
32 devices in a mesh: hx: 4 (over z), hy: 4 (over x, core), ga: 2 (over y).
Axes of the slice: x: 2, y: 2, z: 4, core: 2. Of those that a mesh axis runs over, the one named last changes fastest.
Arguments:
- density: float32 [32, 128, 256], P('hx', 'hy', 'ga'), may hold values from 0.5 to 2
- velocity: float32 [3, 32, 128, 256], P(None, 'hx', 'hy', 'ga'), may hold values from -3 to 3
- pressure: float32 [32, 128, 256], P('hx', 'hy', 'ga'), may hold values from 0.3 to 3
- species: float32 [9, 32, 128, 256], P(None, 'hx', 'hy', 'ga'), may hold values from 0.05 to 1
- newton_count: int32 [32, 128, 256], P('hx', 'hy', 'ga'), may hold values from 1 to 4
Outputs:
- new_density: float32 [32, 128, 256], P('hx', 'hy', 'ga')
- momentum: float32 [3, 32, 128, 256], P(None, 'hx', 'hy', 'ga')
- total_energy: float32 [32, 128, 256], P('hx', 'hy', 'ga')
- species_mass: float32 [9, 32, 128, 256], P(None, 'hx', 'hy', 'ga')
- potential: float32 [32, 128, 256], P('hx', 'hy', 'ga')
Inputs may be any that keep to these rules, and one draw needn't show every extreme that they name: `newton_count`: how many Newton iterations each cell takes.
All inputs are finite; a program needn't handle non-finite values.
Results may differ from a plain program's by a relative error of at most 0.0003.
Values sent between devices are 32-bit elements; how exact they have to be, the bound alone decides.
No kernel may reach another device: no remote copies, remote signals or barrier semaphores. Data moves between devices by JAX's collectives and lax.ppermute only.
A program may use at most 128 MiB of HBM per device.

v0:
```python
import jax
import jax.numpy as jnp
from jax import lax
from jax.sharding import PartitionSpec as P

NEWTON = 4


gamma_gas = 5.0 / 3.0
time_step = 0.1
cool_rates = (2.0, 5.0, 9.0, 14.0, 20.0, 3.0, 7.0, 11.0, 29.0)
highest = lax.Precision.HIGHEST


def extended(cells, sides, width):
    for axis, dim in sides:
        count = lax.axis_size(axis)
        head = lax.slice_in_dim(cells, 0, width, axis=dim)
        tail = lax.slice_in_dim(cells, cells.shape[dim] - width, cells.shape[dim], axis=dim)
        cells = jnp.concatenate(
            [
                lax.ppermute(tail, axis, [(i, (i + 1) % count) for i in range(count)]),
                cells,
                lax.ppermute(head, axis, [((i + 1) % count, i) for i in range(count)]),
            ],
            axis=dim,
        )
    return cells


def cooled_pressure(density, pressure, species, newton_count):
    cooling = cool_rates[0] * species[0]
    for species_index in range(1, 9):
        cooling = cooling + cool_rates[species_index] * species[species_index]
    stiffness = time_step * density * cooling
    initial = pressure / ((gamma_gas - 1.0) * density)
    energy = initial
    for newton_step in range(NEWTON):
        residual_value = energy - initial + stiffness * energy * energy / (1.0 + energy)
        derivative = 1.0 + stiffness * energy * (energy + 2.0) / ((1.0 + energy) * (1.0 + energy))
        energy = jnp.where(newton_count > newton_step, energy - residual_value / derivative, energy)
    return (gamma_gas - 1.0) * density * energy


def conserved(primitive):
    density = primitive[0]
    velocity = primitive[1:4]
    kinetic = (
        0.5
        * density
        * (velocity[0] * velocity[0] + velocity[1] * velocity[1] + velocity[2] * velocity[2])
    )
    energy = primitive[4] / (gamma_gas - 1.0) + kinetic
    return jnp.concatenate(
        [density[None], density[None] * velocity, energy[None], density[None] * primitive[5:14]],
        axis=0,
    )


def face_flux(lower_cells, upper_cells, direction):
    sides_data = []
    for side_cells in (lower_cells, upper_cells):
        amounts = conserved(side_cells)
        normal = side_cells[1 + direction]
        carried = amounts * normal[None]
        carried = carried.at[1 + direction].add(side_cells[4])
        carried = carried.at[4].add(side_cells[4] * normal)
        signal = jnp.abs(normal) + jnp.sqrt(gamma_gas * side_cells[4] / side_cells[0])
        sides_data.append((amounts, carried, signal))
    wave_speed = jnp.maximum(sides_data[0][2], sides_data[1][2])
    return 0.5 * (sides_data[0][1] + sides_data[1][1]) - 0.5 * wave_speed[None] * (
        sides_data[1][0] - sides_data[0][0]
    )


def window(padded, array_axis, offset, extent):
    selection = [slice(None), slice(1, -1), slice(1, -1), slice(1, -1)]
    selection[array_axis] = slice(offset, offset + extent)
    return padded[tuple(selection)]


def advance(padded):
    primitive = padded[0:14]
    current = conserved(primitive[:, 1:-1, 1:-1, 1:-1])
    change = jnp.zeros_like(current)
    accelerations = []
    for direction in range(3):
        array_axis = 1 + direction
        extent = current.shape[array_axis]
        across = face_flux(
            window(primitive, array_axis, 0, extent + 1),
            window(primitive, array_axis, 1, extent + 1),
            direction,
        )
        change = change + (
            lax.slice_in_dim(across, 1, extent + 1, axis=array_axis)
            - lax.slice_in_dim(across, 0, extent, axis=array_axis)
        )
        accelerations.append(
            -0.5
            * (
                window(padded[14:15], array_axis, 2, extent)
                - window(padded[14:15], array_axis, 0, extent)
            )[0]
        )
    updated = current - time_step * change
    density = current[0]
    momentum = jnp.concatenate(
        [
            (updated[1 + direction] + time_step * density * accelerations[direction])[None]
            for direction in range(3)
        ],
        axis=0,
    )
    energy = updated[4] + time_step * (
        current[1] * accelerations[0]
        + current[2] * accelerations[1]
        + current[3] * accelerations[2]
    )
    return (updated[0], momentum, energy, updated[5:14])


def hartley(row_keys, col_keys, length):
    phase = row_keys[:, None] * col_keys[None, :] % length
    angle = 2.0 * jnp.pi / length * phase.astype(jnp.float32)
    return jnp.cos(angle) + jnp.sin(angle)


def eigen_keys(keys, extent):
    return 2.0 * jnp.cos(2.0 * jnp.pi / extent * keys.astype(jnp.float32)) - 2.0


def spectral_solve(planes_data, wave_y, total_y):
    total_x = planes_data.shape[0]
    total_z = planes_data.shape[2]
    keys_x = jnp.arange(total_x, dtype=jnp.int32)
    keys_z = jnp.arange(total_z, dtype=jnp.int32)
    table_x = hartley(keys_x, keys_x, total_x)
    table_z = hartley(keys_z, keys_z, total_z)
    turned = jnp.einsum("ab,byz->ayz", table_x, planes_data, precision=highest)
    turned = jnp.einsum("ayz,zc->ayc", turned, table_z, precision=highest)
    total = (
        eigen_keys(keys_x, total_x)[:, None, None]
        + eigen_keys(wave_y, total_y)[None, :, None]
        + eigen_keys(keys_z, total_z)[None, None, :]
    )
    green = jnp.where(total < 0.0, 1.0 / jnp.where(total < 0.0, total, -1.0), 0.0) / (
        total_x * total_y * total_z
    )
    turned = turned * green
    turned = jnp.einsum("ab,byz->ayz", table_x, turned, precision=highest)
    return jnp.einsum("ayz,zc->ayc", turned, table_z, precision=highest)


def local(density, velocity, pressure, species, newton_count):
    size_x = lax.axis_size("hx")
    size_y = lax.axis_size("hy")
    size_g = lax.axis_size("ga")
    rank_x = lax.axis_index("hx")
    rank_y = lax.axis_index("hy")
    rank_g = lax.axis_index("ga")
    rows_y = density.shape[1]
    total_y = rows_y * size_y
    slab_share = rows_y // size_x
    thin_rows = slab_share // size_g
    keys_y = jnp.arange(total_y, dtype=jnp.int32)
    local_keys = jnp.arange(thin_rows, dtype=jnp.int32)
    table_y = hartley(keys_y, keys_y, total_y)
    gathered = lax.all_to_all(density, "hy", split_axis=0, concat_axis=1, tiled=True)
    turned = jnp.einsum("ab,xbz->xaz", table_y, gathered, precision=highest)
    planes_data = lax.all_to_all(
        lax.all_to_all(turned, ("hx", "hy"), split_axis=1, concat_axis=0, tiled=True),
        "ga",
        split_axis=1,
        concat_axis=2,
        tiled=True,
    )
    wave_y = (rank_x * size_y + rank_y) * slab_share + rank_g * thin_rows + local_keys
    solved = spectral_solve(planes_data, wave_y, total_y)
    returned = lax.all_to_all(
        lax.all_to_all(solved, ("hx", "hy"), split_axis=0, concat_axis=1, tiled=True),
        "ga",
        split_axis=2,
        concat_axis=1,
        tiled=True,
    )
    from_group = keys_y // (thin_rows * size_x * size_y)
    remainder = keys_y % (thin_rows * size_x * size_y)
    column_keys = (
        remainder // thin_rows * slab_share + from_group * thin_rows + remainder % thin_rows
    )
    inverted = jnp.einsum(
        "ab,xbz->xaz", hartley(keys_y, column_keys, total_y), returned, precision=highest
    )
    potential = lax.all_to_all(inverted, "hy", split_axis=1, concat_axis=0, tiled=True)
    cooled = cooled_pressure(density, pressure, species, newton_count)
    gas_stack = jnp.concatenate(
        [density[None], velocity, cooled[None], species, potential[None]], axis=0
    )
    padded = extended(gas_stack, (("hx", 1), ("hy", 2), ("ga", 3)), 1)
    new_density, momentum, total_energy, species_mass = advance(padded)
    return (new_density, momentum, total_energy, species_mass, potential)


def solution(mesh):
    in_specs = (
        P("hx", "hy", "ga"),
        P(None, "hx", "hy", "ga"),
        P("hx", "hy", "ga"),
        P(None, "hx", "hy", "ga"),
        P("hx", "hy", "ga"),
    )
    out_specs = (
        P("hx", "hy", "ga"),
        P(None, "hx", "hy", "ga"),
        P("hx", "hy", "ga"),
        P(None, "hx", "hy", "ga"),
        P("hx", "hy", "ga"),
    )
    return jax.shard_map(local, mesh=mesh, in_specs=in_specs, out_specs=out_specs, check_vma=False)
```

profile of v0, /device:TPU:0, one launch (start us, length us, event | category | flops | bytes accessed | tf_op | source)
XLA Modules:
  0.0 165.5 jit_solution(11811423332542547678)
XLA Ops:
  0.6 4.4 %all-to-all-start = ((f32[8,32,128]{2,1,0:T(8,128)}), f32[8,32,128]{2,1,0:T(8,128)S(1)}, u32[]{:S(2)}, u32[]{:S(2)}) async-start(f32[8,32,128]{2,1,0:T(8,128)} %param.29), calls=%async_computation | async-start | bytes 262144 | tf_op jit(solution)/shard_map/all_to_all | solution.py:169
  5.0 1.0 constant_dynamic-update-slice_fusion.2
  6.2 1.0 copy.232
  7.2 3.0 %copy.137 = f32[9,8,32,128]{3,1,2,0:T(8,128)} copy(f32[9,8,32,128]{3,2,1,0:T(8,128)} %param.32) | data formatting | bytes 2359296 | tf_op args[3]
  11.6 7.0 %all-to-all-start.1 = ((f32[2,128,128]{2,0,1:T(2,128)}), f32[2,128,128]{2,0,1:T(2,128)S(1)}, u32[]{:S(2)}, u32[]{:S(2)}) async-start(f32[2,128,128]{2,0,1:T(2,128)} %copy.153), calls=%async_computation.1 | async-start | bytes 262144 | tf_op jit(solution)/shard_map/all_to_all | solution.py:172
  18.6 1.1 broadcast_multiply_fusion.1
  19.7 6.8 %all-to-all-done.1 = f32[2,128,128]{2,0,1:T(2,128)S(1)} async-done(((f32[2,128,128]{2,0,1:T(2,128)}), f32[2,128,128]{2,0,1:T(2,128)S(1)}, u32[]{:S(2)}, u32[]{:S(2)}) %all-to-all-start.1) | async-done | bytes 131104 | tf_op jit(solution)/shard_map/all_to_all | solution.py:172
  27.2 3.4 %all-to-all-start.2 = ((f32[32,8,128]{2,0,1:T(8,128)}), f32[32,8,128]{2,0,1:T(8,128)S(1)}, u32[]{:S(2)}, u32[]{:S(2)}) async-start(f32[32,8,128]{2,0,1:T(8,128)} %copy.156), calls=%async_computation.2 | async-start | bytes 262144 | tf_op jit(solution)/shard_map/all_to_all | solution.py:171
  30.6 4.4 %all-to-all-done.2 = f32[32,8,128]{2,0,1:T(8,128)S(1)} async-done(((f32[32,8,128]{2,0,1:T(8,128)}), f32[32,8,128]{2,0,1:T(8,128)S(1)}, u32[]{:S(2)}, u32[]{:S(2)}) %all-to-all-start.2) | async-done | bytes 131104 | tf_op jit(solution)/shard_map/all_to_all | solution.py:171
  35.6 1.3 convolution_multiply_fusion
  37.3 1.3 fusion.57
  39.4 4.2 %all-to-all-start.3 = ((f32[32,4,256]{2,1,0:T(4,128)}), f32[32,4,256]{2,1,0:T(4,128)}, u32[]{:S(2)}, u32[]{:S(2)}) async-start(f32[32,4,256]{2,1,0:T(4,128)} %copy.158), calls=%async_computation.3 | async-start | bytes 262144 | tf_op jit(solution)/shard_map/all_to_all | solution.py:181
  43.6 2.9 %fusion.92 = (f32[1,8,32,128]{3,1,2,0:T(8,128)}, f32[8,32,128]{2,0,1:T(8,128)S(1)}) fusion(f32[3,8,32,128]{3,1,2,0:T(8,128)} %get-tuple-element.219, f32[8,32,128]{2,1,0:T(8,128)S(1)} %copy-done.8, f32[9,8,32,128]{3,1,2,0:T(8,128)} %copy.137, f32[8,32,128]{2,1,0:T(8,128)} %param.31, s32[8,32,128]{2,1,0:T(8,128)} %param.33), kind=kLoop, calls=%fused_computation.216 | loop fusion | flops 2981888 | bytes 2228224 | tf_op jit(solution)/shard_map/add | solution.py:53
  46.4 5.0 %all-to-all-done.3 = f32[32,4,256]{2,1,0:T(4,128)} async-done(((f32[32,4,256]{2,1,0:T(4,128)}), f32[32,4,256]{2,1,0:T(4,128)}, u32[]{:S(2)}, u32[]{:S(2)}) %all-to-all-start.3) | async-done | bytes 131104 | tf_op jit(solution)/shard_map/all_to_all | solution.py:181
  51.5 1.6 copy.159
  53.1 1.7 %copy.160 = f32[2,64,256]{1,0,2:T(2,128)} copy(f32[2,64,256]{2,0,1:T(2,128)} %bitcast.132) | data formatting | bytes 262144 | tf_op jit(solution)/shard_map/all_to_all | solution.py:181
  54.8 1.9 %reshape.556 = f32[2,1,16384]{2,1,0:T(1,128)} reshape(f32[256,2,64]{2,1,0:T(2,128)} %bitcast.130) | data formatting | bytes 262144
  56.7 4.0 %all-to-all-start.4 = ((f32[2,1,16384]{2,1,0:T(1,128)}), f32[2,1,16384]{2,1,0:T(1,128)}, u32[]{:S(2)}, u32[]{:S(2)}) async-start(f32[2,1,16384]{2,1,0:T(1,128)} %reshape.556), calls=%async_computation.4 | async-start | bytes 262144 | tf_op jit(solution)/shard_map/all_to_all | solution.py:180
  60.7 4.5 %all-to-all-done.4 = f32[2,1,16384]{2,1,0:T(1,128)} async-done(((f32[2,1,16384]{2,1,0:T(1,128)}), f32[2,1,16384]{2,1,0:T(1,128)}, u32[]{:S(2)}, u32[]{:S(2)}) %all-to-all-start.4) | async-done | bytes 131104 | tf_op jit(solution)/shard_map/all_to_all | solution.py:180
  65.8 2.6 %reduce.24 = f32[2,16384]{1,0:T(2,128)} reduce(f32[2,1,16384]{2,1,0:T(1,128)} %all-to-all-done.4, f32[]{:T(128)} %broadcast.581), dimensions={1}, to_apply=%all_to_all.94.reduce_sub_computation | reduce | bytes 262148 | tf_op jit(solution)/shard_map/all_to_all | solution.py:180
  68.4 1.9 %reshape.557 = f32[256,2,64]{2,1,0:T(2,128)} reshape(f32[2,16384]{1,0:T(2,128)} %reduce.24) | data formatting | bytes 262144
  70.2 1.7 %copy.162 = f32[2,2,64,128]{3,2,1,0:T(8,128)} copy(f32[2,2,64,128]{2,0,3,1:T(2,128)} %bitcast.131) | data formatting | bytes 262144 | tf_op jit(solution)/shard_map/all_to_all | solution.py:180
  72.0 2.1 %convolution_bitcast_fusion = f32[2,128,128]{1,2,0:T(8,128)} fusion(f32[2,128,128]{2,1,0:T(8,128)} %bitcast.141, s32[128]{0:T(128)S(1)} %fusion.156), kind=kOutput, calls=%fused_computation.54 | convolution fusion | flops 50577408 | bytes 262656 | tf_op jit(solution)/shard_map/ab,xbz->xaz/dot_general | solution.py:192
  74.1 1.7 %copy.164 = f32[2,128,128]{2,0,1:T(2,128)} copy(f32[2,128,128]{1,2,0:T(8,128)} %convolution_bitcast_fusion) | data formatting | bytes 262144 | tf_op jit(solution)/shard_map/ab,xbz->xaz/transpose | solution.py:192
  75.7 4.0 %all-to-all-start.5 = ((f32[2,128,128]{2,0,1:T(2,128)}), f32[2,128,128]{2,0,1:T(2,128)}, u32[]{:S(2)}, u32[]{:S(2)}) async-start(f32[2,128,128]{2,0,1:T(2,128)} %copy.164), calls=%async_computation.5 | async-start | bytes 262144 | tf_op jit(solution)/shard_map/all_to_all | solution.py:195
  79.7 1.8 %broadcast_multiply_fusion = (f32[9,8,32,128]{3,1,2,0:T(8,128)}, f32[15,8,32,128]{3,1,2,0:T(8,128)S(1)}) fusion(f32[8,32,128]{2,0,1:T(8,128)S(1)} %copy.232, f32[9,8,32,128]{3,2,1,0:T(8,128)S(1)} %copy-done.5, f32[15,8,32,128]{3,1,2,0:T(8,128)S(1)} %bitcast_dynamic-update-slice_fusion), kind=kLoop, calls=%fused_computation.64 | loop fusion | flops 294912 | bytes 3670016 | tf_op jit(solution)/shard_map/mul | solution.py:55
  81.5 2.8 %all-to-all-done.5 = f32[2,128,128]{2,0,1:T(2,128)} async-done(((f32[2,128,128]{2,0,1:T(2,128)}), f32[2,128,128]{2,0,1:T(2,128)}, u32[]{:S(2)}, u32[]{:S(2)}) %all-to-all-start.5) | async-done | bytes 131104 | tf_op jit(solution)/shard_map/all_to_all | solution.py:195
  86.6 3.8 %collective-permute-start.1 = (f32[15,1,32,128]{3,1,2,0:T(1,128)S(1)}, f32[15,1,32,128]{3,1,2,0:T(1,128)S(1)}, u32[]{:S(2)}, u32[]{:S(2)}) collective-permute-start(f32[15,1,32,128]{3,1,2,0:T(1,128)S(1)} %get-tuple-element.213), channel_id=1, source_target_pairs={{8,0},{16,8},{24,16},{0,24},{9,1},{17,9},{25,17},{1,25},{10,2},{18... | collective-permute-start | bytes 737288 | tf_op jit(solution)/shard_map/ppermute | solution.py:24
  90.4 6.8 %collective-permute-done = f32[15,1,32,128]{3,1,2,0:T(1,128)S(1)} collective-permute-done((f32[15,1,32,128]{3,1,2,0:T(1,128)S(1)}, f32[15,1,32,128]{3,1,2,0:T(1,128)S(1)}, u32[]{:S(2)}, u32[]{:S(2)}) %collective-permute-start) | collective-permute-done | bytes 245792 | tf_op jit(solution)/shard_map/ppermute | solution.py:22
  97.2 2.0 %collective-permute-done.1 = f32[15,1,32,128]{3,1,2,0:T(1,128)S(1)} collective-permute-done((f32[15,1,32,128]{3,1,2,0:T(1,128)S(1)}, f32[15,1,32,128]{3,1,2,0:T(1,128)S(1)}, u32[]{:S(2)}, u32[]{:S(2)}) %collective-permute-start.1) | collective-permute-done | bytes 245792 | tf_op jit(solution)/shard_map/ppermute | solution.py:24
  102.0 2.0 %collective-permute-start.3 = (f32[15,10,1,128]{3,0,2,1:T(8,128)S(1)}, f32[15,10,1,128]{3,0,2,1:T(8,128)S(1)}, u32[]{:S(2)}, u32[]{:S(2)}) collective-permute-start(f32[15,10,1,128]{3,0,2,1:T(8,128)S(1)} %copy.172), channel_id=1, source_target_pairs={{2,0},{4,2},{6,4},{0,6},{3,1},{5,3},{7,5},{1,7},{10,8},{12,10},{14... | collective-permute-start | bytes 230408 | tf_op jit(solution)/shard_map/ppermute | solution.py:24
  103.9 2.4 %multiply_subtract_fusion.1 = f32[14,9,32,128]{3,1,2,0:T(8,128)} fusion(f32[14,9,32,128]{3,1,2,0:T(8,128)S(1)} %fusion.55, f32[14,9,32,128]{3,1,2,0:T(8,128)S(1)} %fusion.53, f32[9,9,32,128]{3,1,2,0:T(8,128)S(1)} %get-tuple-element.210, f32[1,9,32,128]{3,1,2,0:T(8,128)S(1)} %get-tuple-element.208, f32[3,9,32,128]{3,1,2,0:T(8,128)S(1)} %get-tuple-element.206, ...), kind=kLoop, calls=%fused_computation.30 | loop fusion | flops 5677056 | bytes 10469376 | tf_op jit(solution)/shard_map/sub | solution.py:71
  109.0 1.7 %fusion.12 = (f32[14,8,33,128]{3,1,2,0:T(8,128)S(1)}, f32[14,8,33,128]{3,1,2,0:T(8,128)}) fusion(f32[9,8,33,128]{3,1,2,0:T(8,128)S(1)} %get-tuple-element.199, f32[1,8,33,128]{3,1,2,0:T(8,128)S(1)} %fusion.67, f32[3,8,33,128]{3,1,2,0:T(8,128)S(1)} %get-tuple-element.197, f32[1,8,33,128]{3,1,2,0:T(8,128)S(1)} %get-tuple-element.180, ...), kind=kLoop, calls=%fused_computation.56 | loop fusion | flops 3784704 | bytes 7839744 | tf_op jit(solution)/shard_map/mul | solution.py:65
  110.7 1.7 %fusion.70 = f32[14,8,33,128]{3,1,2,0:T(8,128)} fusion(f32[14,8,33,128]{3,1,2,0:T(8,128)} %get-tuple-element.225, f32[1,8,33,128]{3,1,2,0:T(8,128)S(1)} %get-tuple-element.181), kind=kLoop, calls=%fused_computation.162 | loop fusion | flops 33792 | bytes 405504 | tf_op jit(solution)/shard_map/scatter-add | solution.py:66
  112.5 1.6 fusion.69
  114.8 4.8 %fusion.185 = (f32[15,10,34,1]{3,1,2,0:T(8,128)}, f32[15,10,34,1]{3,1,2,0:T(8,128)}) fusion(f32[15,10,34,128]{3,1,2,0:T(8,128)S(1)} %pad_maximum_fusion), kind=kLoop, calls=%fused_computation.345 | loop fusion | bytes 81600 | tf_op jit(solution)/shard_map/slice | solution.py:18
  119.6 4.2 %copy.176 = f32[15,10,34,1]{2,0,3,1:T(8,128)} copy(f32[15,10,34,1]{3,1,2,0:T(8,128)} %get-tuple-element.192) | data formatting | bytes 40800 | tf_op jit(solution)/shard_map/slice | solution.py:19
  123.7 4.2 %copy.183 = f32[15,10,34,1]{2,0,3,1:T(8,128)} copy(f32[15,10,34,1]{3,1,2,0:T(8,128)} %get-tuple-element.191) | data formatting | bytes 40800 | tf_op jit(solution)/shard_map/slice | solution.py:18
  127.9 2.0 %collective-permute-start.5 = (f32[15,10,34,1]{2,0,3,1:T(8,128)}, f32[15,10,34,1]{2,0,3,1:T(8,128)}, u32[]{:S(2)}, u32[]{:S(2)}) collective-permute-start(f32[15,10,34,1]{2,0,3,1:T(8,128)} %copy.183), channel_id=1, source_target_pairs={{1,0},{0,1},{3,2},{2,3},{5,4},{4,5},{7,6},{6,7},{9,8},{8,9},{11,10... | collective-permute-start | bytes 61208 | tf_op jit(solution)/shard_map/ppermute | solution.py:24
  129.9 4.6 %multiply_subtract_fusion.2 = f32[14,8,33,128]{3,1,2,0:T(8,128)} fusion(f32[14,8,33,128]{3,1,2,0:T(8,128)} %fusion.69, f32[14,8,33,128]{3,1,2,0:T(8,128)} %copy-done.4, f32[9,8,33,128]{3,1,2,0:T(8,128)} %copy-done.2, f32[1,8,33,128]{3,1,2,0:T(8,128)} %copy-done.12, f32[3,8,33,128]{3,1,2,0:T(8,128)S(1)} %get-tuple-element.197, ...), kind=kLoop, calls=%fused_computation.43 | loop fusion | flops 5203968 | bytes 9596928 | tf_op jit(solution)/shard_map/sub | solution.py:71
  134.5 4.1 %copy.177 = f32[15,10,34,1]{3,1,2,0:T(8,128)} copy(f32[15,10,34,1]{2,0,3,1:T(8,128)} %collective-permute-done.4) | data formatting | bytes 40800 | tf_op jit(solution)/shard_map/ppermute | solution.py:22
  138.7 4.1 %copy.184 = f32[15,10,34,1]{3,1,2,0:T(8,128)} copy(f32[15,10,34,1]{2,0,3,1:T(8,128)} %collective-permute-done.5) | data formatting | bytes 40800 | tf_op jit(solution)/shard_map/ppermute | solution.py:24
  142.8 2.0 %multiply_bitcast_fusion = (f32[8,32,129]{2,0,1:T(8,128)S(1)}, f32[1,8,32,129]{3,1,2,0:T(8,128)S(1)}, f32[1,8,32,129]{3,1,2,0:T(8,128)S(1)}, f32[1,8,32,129]{3,1...) fusion(f32[15,10,34,1]{3,1,2,0:T(8,128)} %copy.184, ...), kind=kLoop, calls=%fused_computation.133 | loop fusion | flops 1320960 | bytes 3576672 | tf_op jit(solution)/shard_map/mul | solution.py:71
  145.4 1.3 copy-done.1
  147.3 2.9 %maximum_multiply_fusion = (f32[9,8,32,129]{3,1,2,0:T(8,128)S(1)}, f32[9,8,32,129]{3,1,2,0:T(8,128)S(1)}) fusion(f32[15,10,34,1]{3,1,2,0:T(8,128)S(1)} %copy-done.1, f32[15,10,1,128]{3,1,2,0:T(8,128)S(1)} %copy.173, f32[15,10,1,128]{3,1,2,0:T(8,128)S(1)} %copy.171, f32[15,1,32,128]{3,1,2,0:T(1,128)S(1)} %collective-permute-done.1, ...), kind=kLoop, calls=%fused_computation.35 | loop fusion | flops 3566592 | bytes 5293920 | tf_op jit(solution)/shard_map/mul | solution.py:55
  152.0 2.8 %multiply_subtract_fusion = f32[14,8,32,129]{3,1,2,0:T(8,128)} fusion(f32[14,8,32,129]{3,1,2,0:T(8,128)S(1)} %fusion.47, f32[14,8,32,129]{3,1,2,0:T(8,128)S(1)} %fusion.41, f32[9,8,32,129]{3,1,2,0:T(8,128)S(1)} %get-tuple-element.195, f32[1,8,32,129]{3,1,2,0:T(8,128)S(1)} %fusion.46, f32[3,8,32,129]{3,1,2,0:T(8,128)S(1)} %get-tuple-element.193, ...), kind=kLoop, calls=%fused_computation.29 | loop fusion | flops 5085696 | bytes 9378816 | tf_op jit(solution)/shard_map/sub | solution.py:71
  154.8 6.7 %fusion.10 = f32[14,8,32,128]{3,1,2,0:T(8,128)S(1)} fusion(f32[14,8,32,129]{3,1,2,0:T(8,128)} %multiply_subtract_fusion, f32[14,8,33,128]{3,1,2,0:T(8,128)} %multiply_subtract_fusion.2, f32[14,9,32,128]{3,1,2,0:T(8,128)} %multiply_subtract_fusion.1, f32[9,8,32,128]{3,1,2,0:T(8,128)} %get-tuple-element.215, f32[1,8,32,128]{3,1,2,0:T(8,128)S(1)} %copy-done.13, ...), kind=kLoop, calls=%fused_computation.47 | loop fusion | flops 4587520 | bytes 14680064 | tf_op jit(solution)/shard_map/sub | solution.py:106
  161.6 1.2 copy.196
  (98 shorter events, 18.3 us)
Async XLA Ops:
  0.6 17.9 %copy-start.15 = (f32[3,8,32,128]{3,2,1,0:T(8,128)S(1)}, f32[3,8,32,128]{3,2,1,0:T(8,128)}, u32[]{:S(2)}) copy-start(f32[3,8,32,128]{3,2,1,0:T(8,128)} %param.30) | copy-start | bytes 1179652
  0.6 9.6 %all-to-all-start = ((f32[8,32,128]{2,1,0:T(8,128)}), f32[8,32,128]{2,1,0:T(8,128)S(1)}, u32[]{:S(2)}, u32[]{:S(2)}) async-start(f32[8,32,128]{2,1,0:T(8,128)} %param.29), calls=%async_computation | async-start | bytes 262144 | tf_op jit(solution)/shard_map/all_to_all | solution.py:169
  7.2 72.5 %copy-start.9 = (f32[8,32,128]{2,0,1:T(8,128)}, f32[8,32,128]{2,0,1:T(8,128)S(1)}, u32[]{:S(2)}) copy-start(f32[8,32,128]{2,0,1:T(8,128)S(1)} %copy.232) | copy-start | bytes 393220
  11.6 14.9 %all-to-all-start.1 = ((f32[2,128,128]{2,0,1:T(2,128)}), f32[2,128,128]{2,0,1:T(2,128)S(1)}, u32[]{:S(2)}, u32[]{:S(2)}) async-start(f32[2,128,128]{2,0,1:T(2,128)} %copy.153), calls=%async_computation.1 | async-start | bytes 262144 | tf_op jit(solution)/shard_map/all_to_all | solution.py:172
  27.2 7.8 %all-to-all-start.2 = ((f32[32,8,128]{2,0,1:T(8,128)}), f32[32,8,128]{2,0,1:T(8,128)S(1)}, u32[]{:S(2)}, u32[]{:S(2)}) async-start(f32[32,8,128]{2,0,1:T(8,128)} %copy.156), calls=%async_computation.2 | async-start | bytes 262144 | tf_op jit(solution)/shard_map/all_to_all | solution.py:171
  30.6 13.0 %copy-start.8 = (f32[8,32,128]{2,1,0:T(8,128)S(1)}, f32[8,32,128]{2,1,0:T(8,128)}, u32[]{:S(2)}) copy-start(f32[8,32,128]{2,1,0:T(8,128)} %param.29) | copy-start | bytes 393220
  39.4 12.1 %all-to-all-start.3 = ((f32[32,4,256]{2,1,0:T(4,128)}), f32[32,4,256]{2,1,0:T(4,128)}, u32[]{:S(2)}, u32[]{:S(2)}) async-start(f32[32,4,256]{2,1,0:T(4,128)} %copy.158), calls=%async_computation.3 | async-start | bytes 262144 | tf_op jit(solution)/shard_map/all_to_all | solution.py:181
  43.6 36.2 %copy-start.5 = (f32[9,8,32,128]{3,2,1,0:T(8,128)S(1)}, f32[9,8,32,128]{3,2,1,0:T(8,128)}, u32[]{:S(2)}) copy-start(f32[9,8,32,128]{3,2,1,0:T(8,128)} %param.32) | copy-start | bytes 3538948
  56.7 8.6 %all-to-all-start.4 = ((f32[2,1,16384]{2,1,0:T(1,128)}), f32[2,1,16384]{2,1,0:T(1,128)}, u32[]{:S(2)}, u32[]{:S(2)}) async-start(f32[2,1,16384]{2,1,0:T(1,128)} %reshape.556), calls=%async_computation.4 | async-start | bytes 262144 | tf_op jit(solution)/shard_map/all_to_all | solution.py:180
  75.7 8.6 %all-to-all-start.5 = ((f32[2,128,128]{2,0,1:T(2,128)}), f32[2,128,128]{2,0,1:T(2,128)}, u32[]{:S(2)}, u32[]{:S(2)}) async-start(f32[2,128,128]{2,0,1:T(2,128)} %copy.164), calls=%async_computation.5 | async-start | bytes 262144 | tf_op jit(solution)/shard_map/all_to_all | solution.py:195
  85.3 0.7 copy-start.14
  86.5 10.7 %collective-permute-start = (f32[15,1,32,128]{3,1,2,0:T(1,128)S(1)}, f32[15,1,32,128]{3,1,2,0:T(1,128)S(1)}, u32[]{:S(2)}, u32[]{:S(2)}) collective-permute-start(f32[15,1,32,128]{3,1,2,0:T(1,128)S(1)} %get-tuple-element.212), channel_id=1, source_target_pairs={{0,8},{8,16},{16,24},{24,0},{1,9},{9,17},{17,25},{25,1},{2,10},{10... | collective-permute-start | bytes 737288 | tf_op jit(solution)/shard_map/ppermute | solution.py:22
  86.6 12.6 %collective-permute-start.1 = (f32[15,1,32,128]{3,1,2,0:T(1,128)S(1)}, f32[15,1,32,128]{3,1,2,0:T(1,128)S(1)}, u32[]{:S(2)}, u32[]{:S(2)}) collective-permute-start(f32[15,1,32,128]{3,1,2,0:T(1,128)S(1)} %get-tuple-element.213), channel_id=1, source_target_pairs={{8,0},{16,8},{24,16},{0,24},{9,1},{17,9},{25,17},{1,25},{10,2},{18... | collective-permute-start | bytes 737288 | tf_op jit(solution)/shard_map/ppermute | solution.py:24
  101.9 4.5 %collective-permute-start.2 = (f32[15,10,1,128]{3,0,2,1:T(8,128)S(1)}, f32[15,10,1,128]{3,0,2,1:T(8,128)S(1)}, u32[]{:S(2)}, u32[]{:S(2)}) collective-permute-start(f32[15,10,1,128]{3,0,2,1:T(8,128)S(1)} %copy.170), channel_id=1, source_target_pairs={{0,2},{2,4},{4,6},{6,0},{1,3},{3,5},{5,7},{7,1},{8,10},{10,12},{12... | collective-permute-start | bytes 230408 | tf_op jit(solution)/shard_map/ppermute | solution.py:22
  102.0 4.4 %collective-permute-start.3 = (f32[15,10,1,128]{3,0,2,1:T(8,128)S(1)}, f32[15,10,1,128]{3,0,2,1:T(8,128)S(1)}, u32[]{:S(2)}, u32[]{:S(2)}) collective-permute-start(f32[15,10,1,128]{3,0,2,1:T(8,128)S(1)} %copy.172), channel_id=1, source_target_pairs={{2,0},{4,2},{6,4},{0,6},{3,1},{5,3},{7,5},{1,7},{10,8},{12,10},{14... | collective-permute-start | bytes 230408 | tf_op jit(solution)/shard_map/ppermute | solution.py:24
  107.3 0.7 copy-start.6
  107.6 1.0 copy-start.2
  107.6 1.4 copy-start.3
  107.7 3.0 %copy-start.11 = (f32[1,8,33,128]{3,1,2,0:T(8,128)}, f32[1,8,33,128]{3,1,2,0:T(8,128)S(1)}, u32[]{:S(2)}) copy-start(f32[1,8,33,128]{3,1,2,0:T(8,128)S(1)} %fusion.73) | copy-start | bytes 405508
  107.8 2.9 %copy-start.12 = (f32[1,8,33,128]{3,1,2,0:T(8,128)}, f32[1,8,33,128]{3,1,2,0:T(8,128)S(1)}, u32[]{:S(2)}) copy-start(f32[1,8,33,128]{3,1,2,0:T(8,128)S(1)} %fusion.67) | copy-start | bytes 405508
  110.7 1.7 %copy-start.4 = (f32[14,8,33,128]{3,1,2,0:T(8,128)}, f32[14,8,33,128]{3,1,2,0:T(8,128)S(1)}, u32[]{:S(2)}) copy-start(f32[14,8,33,128]{3,1,2,0:T(8,128)S(1)} %fusion.63) | copy-start | bytes 5677060
  123.7 10.8 %collective-permute-start.4 = (f32[15,10,34,1]{2,0,3,1:T(8,128)}, f32[15,10,34,1]{2,0,3,1:T(8,128)}, u32[]{:S(2)}, u32[]{:S(2)}) collective-permute-start(f32[15,10,34,1]{2,0,3,1:T(8,128)} %copy.176), channel_id=1, source_target_pairs={{0,1},{1,0},{2,3},{3,2},{4,5},{5,4},{6,7},{7,6},{8,9},{9,8},{10,11... | collective-permute-start | bytes 61208 | tf_op jit(solution)/shard_map/ppermute | solution.py:22
  127.9 10.8 %collective-permute-start.5 = (f32[15,10,34,1]{2,0,3,1:T(8,128)}, f32[15,10,34,1]{2,0,3,1:T(8,128)}, u32[]{:S(2)}, u32[]{:S(2)}) collective-permute-start(f32[15,10,34,1]{2,0,3,1:T(8,128)} %copy.183), channel_id=1, source_target_pairs={{1,0},{0,1},{3,2},{2,3},{5,4},{4,5},{7,6},{6,7},{9,8},{8,9},{11,10... | collective-permute-start | bytes 61208 | tf_op jit(solution)/shard_map/ppermute | solution.py:24
  142.8 2.7 %copy-start = (f32[15,10,34,1]{3,1,2,0:T(8,128)S(1)}, f32[15,10,34,1]{3,1,2,0:T(8,128)}, u32[]{:S(2)}) copy-start(f32[15,10,34,1]{3,1,2,0:T(8,128)} %copy.177) | copy-start | bytes 61204
  142.8 3.9 %copy-start.1 = (f32[15,10,34,1]{3,1,2,0:T(8,128)S(1)}, f32[15,10,34,1]{3,1,2,0:T(8,128)}, u32[]{:S(2)}) copy-start(f32[15,10,34,1]{3,1,2,0:T(8,128)} %copy.184) | copy-start | bytes 61204
  151.9 2.8 %copy-start.7 = (f32[3,8,32,128]{3,1,2,0:T(8,128)S(1)}, f32[3,8,32,128]{3,1,2,0:T(8,128)}, u32[]{:S(2)}) copy-start(f32[3,8,32,128]{3,1,2,0:T(8,128)} %get-tuple-element.217) | copy-start | bytes 1179652
  152.0 2.8 %copy-start.10 = (f32[8,32,128]{2,0,1:T(8,128)S(1)}, f32[8,32,128]{2,0,1:T(8,128)}, u32[]{:S(2)}) copy-start(f32[8,32,128]{2,0,1:T(8,128)} %copy-done.9) | copy-start | bytes 393220
  152.0 2.8 %copy-start.13 = (f32[1,8,32,128]{3,1,2,0:T(8,128)S(1)}, f32[1,8,32,128]{3,1,2,0:T(8,128)}, u32[]{:S(2)}) copy-start(f32[1,8,32,128]{3,1,2,0:T(8,128)} %get-tuple-element.168) | copy-start | bytes 393220
where the time goes:
time: 167 us; the launch traced here: 165 us
  local copies, waits for them, and re-layouts  48.6 us (29%)
  other arithmetic  42.5 us (25%)
  starting transfers between devices  34.8 us (21%)
  waiting for transfers between devices  32.4 us (19%)
  matrix products  6.03 us (4%)
    unnamed x42, local copies, waits for them, and re-layouts  15.9 us
    sub x3, other arithmetic, face_flux(): 0.5 * (sides_data[0][1] + sides_data[1][1])  9.84 us
    slice x3, local copies, waits for them, and re-layouts, extended(): head = lax.slice_in_dim(cells, 0, width, axis=dim)  8.95 us
    ppermute x3, starting transfers between devices, extended(): lax.ppermute(head, axis, [((i + 1) % count, i) for i in range(count)])  7.78 us
    all_to_all x1, starting transfers between devices, local(): lax.all_to_all(turned, ('hx', 'hy'), split_axis=1, concat_axis=0, tiled=T...  6.98 us
    ppermute x3, waiting for transfers between devices, extended(): lax.ppermute(tail, axis, [(i, (i + 1) % count) for i in range(count)])  6.81 us
    all_to_all x1, waiting for transfers between devices, local(): lax.all_to_all(turned, ('hx', 'hy'), split_axis=1, concat_axis=0, tiled=T...  6.75 us
    sub x1, other arithmetic, advance(): updated = current - time_step * change  6.74 us
  transfers between devices with their start and end apart: 12, of which 7 were waited for; matrix products, arithmetic and copies ran while one was open for 16% of the time, Pallas kernels for 0%

commit v1 on v0

v1 whole, which is shorter than its diff:
```python
import functools
import math

import jax
import jax.numpy as jnp
import numpy as np
from jax import lax
from jax.experimental import pallas as pl
from jax.experimental.pallas import tpu as pltpu
from jax.sharding import PartitionSpec as P

NEWTON = 4
gamma_gas = 5.0 / 3.0
time_step = 0.1
cool_rates = (2.0, 5.0, 9.0, 14.0, 20.0, 3.0, 7.0, 11.0, 29.0)
species_n = len(cool_rates)
prim_n = 5 + species_n
half_step = 0.5 * time_step
highest = lax.Precision.HIGHEST
LANES = 128
P_AT = prim_n
C_AT = prim_n + 1
V_AT = prim_n + 2
field_n = prim_n + 5
face_n = prim_n + 3
HIGH_FACE = 64


def fields_of(primitive):
    density, v0, v1, v2, pressure = primitive[:5]
    energy = pressure * (1.0 / (gamma_gas - 1.0)) + 0.5 * density * (v0 * v0 + v1 * v1 + v2 * v2)
    sound = jnp.sqrt(gamma_gas * pressure / density)
    return (
        [density, density * v0, density * v1, density * v2, energy]
        + list(primitive[5:])
        + [pressure, sound, v0, v1, v2]
    )


def cooled_plane(density, pressure, species, count):
    cooling = cool_rates[0] * species[0]
    for s in range(1, species_n):
        cooling = cooling + cool_rates[s] * species[s]
    stiffness = time_step * density * cooling
    initial = pressure / ((gamma_gas - 1.0) * density)
    energy = initial
    for step in range(NEWTON):
        above = 1.0 + energy
        residual = ((energy - initial) * above + stiffness * energy * energy) * above
        derivative = above * above + stiffness * energy * (energy + 2.0)
        energy = jnp.where(count > step, energy - residual / derivative, energy)
    return (gamma_gas - 1.0) * density * energy


def pack_kernel(den, vel, pre, spe, cnt, cooled, xlo, xhi, ylo, yhi, zface):
    nx, ny, nz = den.shape
    lane = lax.broadcasted_iota(jnp.int32, (ny, LANES), 1)

    def plane(x, _):
        density = den[x]
        species = [spe[s, x] for s in range(species_n)]
        pressure = cooled_plane(density, pre[x], species, cnt[x])
        cooled[x] = pressure
        primitive = [density, vel[0, x], vel[1, x], vel[2, x], pressure] + [density * s for s in species]
        for c in range(prim_n):
            ylo[c, pl.ds(x, 1), :] = primitive[c][0:1, :]
            yhi[c, pl.ds(x, 1), :] = primitive[c][ny - 1 : ny, :]

        @pl.when(x == 0)
        def _():
            for c in range(prim_n):
                xlo[c] = primitive[c]

        @pl.when(x == nx - 1)
        def _():
            for c in range(prim_n):
                xhi[c] = primitive[c]

        fields = fields_of(primitive)
        carried = fields[: C_AT + 1] + [fields[V_AT + 2]]
        packed = jnp.zeros((ny, LANES), jnp.float32)
        for c in range(face_n):
            first, last = carried[c][:, :LANES], carried[c][:, nz - LANES :]
            packed = jnp.where(lane == c, pltpu.roll(first, c, 1) if c else first, packed)
            packed = jnp.where(lane == HIGH_FACE + c, pltpu.roll(last, HIGH_FACE + c + 1, 1), packed)
        zface[x] = packed
        return 0

    lax.fori_loop(0, nx, plane, 0)


def flux_kernel(den, vel, cooled, spe, xbelow, xabove, ybelow, yabove, zbelow, zabove,
                new_density, momentum, energy, mass, ext, yedge):
    nx, ny, nz = den.shape
    row = lax.broadcasted_iota(jnp.int32, (ny, nz), 0)
    lane = lax.broadcasted_iota(jnp.int32, (ny, nz), 1)

    for side, (at, face) in enumerate(((0, xbelow), (nx + 1, xabove))):
        for f, value in enumerate(fields_of([face[c] for c in range(prim_n)])):
            ext[f, at] = value
    for side, face in enumerate((ybelow, yabove)):
        for f, value in enumerate(fields_of([face[c] for c in range(prim_n)])):
            yedge[side, f] = value

    def derive(x, _):
        density = den[x]
        primitive = [density, vel[0, x], vel[1, x], vel[2, x], cooled[x]]
        primitive += [density * spe[s, x] for s in range(species_n)]
        for f, value in enumerate(fields_of(primitive)):
            ext[f, x + 1] = value
        return 0

    lax.fori_loop(0, nx, derive, 0)

    def plane(x, _):
        from_below = zbelow[x]
        from_above = zabove[x]

        def beside(f, direction, up):
            if direction == 0:
                return ext[f, x + 2] if up else ext[f, x]
            here = ext[f, x + 1]
            if direction == 1:
                edge = yedge[1 if up else 0, f, pl.ds(x, 1), :]
                if up:
                    return jnp.where(row == ny - 1, edge, pltpu.roll(here, ny - 1, 0))
                return jnp.where(row == 0, edge, pltpu.roll(here, 1, 0))
            slot = f if f < V_AT else prim_n + 2
            if up:
                edge = pltpu.roll(from_above, LANES - 1 - slot, 1)
                return jnp.where(lane == nz - 1, edge, pltpu.roll(here, nz - 1, 1))
            edge = pltpu.roll(from_below, LANES - HIGH_FACE - slot, 1)
            return jnp.where(lane == 0, edge, pltpu.roll(here, 1, 1))

        sound = ext[C_AT, x + 1]
        centre = 1.0
        above, below, push, work = [], [], [], 0.0
        for d in range(3):
            speed = jnp.abs(ext[V_AT + d, x + 1]) + sound
            v_up, v_lo = beside(V_AT + d, d, True), beside(V_AT + d, d, False)
            p_up, p_lo = beside(P_AT, d, True), beside(P_AT, d, False)
            s_up = jnp.maximum(speed, jnp.abs(v_up) + beside(C_AT, d, True))
            s_lo = jnp.maximum(speed, jnp.abs(v_lo) + beside(C_AT, d, False))
            centre = centre - half_step * (s_up + s_lo)
            above.append(half_step * (s_up - v_up))
            below.append(half_step * (s_lo + v_lo))
            push.append(half_step * (p_lo - p_up))
            work = work + half_step * (p_lo * v_lo - p_up * v_up)

        def updated(f):
            total = centre * ext[f, x + 1]
            for d in range(3):
                total = total + above[d] * beside(f, d, True)
                total = total + below[d] * beside(f, d, False)
            return total

        new_density[x] = updated(0)
        for d in range(3):
            momentum[d, x] = updated(1 + d) + push[d]
        energy[x] = updated(4) + work
        for s in range(species_n):
            mass[s, x] = updated(5 + s)
        return 0

    lax.fori_loop(0, nx, plane, 0)


def vmem_call(kernel, out_shape, **more):
    return pl.pallas_call(
        kernel,
        out_shape=[jax.ShapeDtypeStruct(s, jnp.float32) for s in out_shape],
        **more,
    )


def shifted(value, axis, step):
    count = lax.axis_size(axis)
    return lax.ppermute(value, axis, [(i, (i + step) % count) for i in range(count)])


def hartley(row_keys, col_keys, length):
    phase = row_keys[:, None] * col_keys[None, :] % length
    angle = 2.0 * jnp.pi / length * phase.astype(jnp.float32)
    return jnp.cos(angle) + jnp.sin(angle)


def eigen_keys(keys, extent):
    return 2.0 * jnp.cos(2.0 * jnp.pi / extent * keys.astype(jnp.float32)) - 2.0


def spectral_solve(planes_data, wave_y, total_y):
    total_x = planes_data.shape[0]
    total_z = planes_data.shape[2]
    keys_x = jnp.arange(total_x, dtype=jnp.int32)
    keys_z = jnp.arange(total_z, dtype=jnp.int32)
    table_x = hartley(keys_x, keys_x, total_x)
    table_z = hartley(keys_z, keys_z, total_z)
    turned = jnp.einsum("ab,byz->ayz", table_x, planes_data, precision=highest)
    turned = jnp.einsum("ayz,zc->ayc", turned, table_z, precision=highest)
    total = (
        eigen_keys(keys_x, total_x)[:, None, None]
        + eigen_keys(wave_y, total_y)[None, :, None]
        + eigen_keys(keys_z, total_z)[None, None, :]
    )
    green = jnp.where(total < 0.0, 1.0 / jnp.where(total < 0.0, total, -1.0), 0.0) / (
        total_x * total_y * total_z
    )
    turned = turned * green
    turned = jnp.einsum("ab,byz->ayz", table_x, turned, precision=highest)
    return jnp.einsum("ayz,zc->ayc", turned, table_z, precision=highest)


def local(density, velocity, pressure, species, newton_count):
    size_x = lax.axis_size("hx")
    size_y = lax.axis_size("hy")
    size_g = lax.axis_size("ga")
    rank_x = lax.axis_index("hx")
    rank_y = lax.axis_index("hy")
    rank_g = lax.axis_index("ga")
    rows_y = density.shape[1]
    total_y = rows_y * size_y
    slab_share = rows_y // size_x
    thin_rows = slab_share // size_g
    keys_y = jnp.arange(total_y, dtype=jnp.int32)
    local_keys = jnp.arange(thin_rows, dtype=jnp.int32)
    table_y = hartley(keys_y, keys_y, total_y)
    gathered = lax.all_to_all(density, "hy", split_axis=0, concat_axis=1, tiled=True)
    turned = jnp.einsum("ab,xbz->xaz", table_y, gathered, precision=highest)
    planes_data = lax.all_to_all(
        lax.all_to_all(turned, ("hx", "hy"), split_axis=1, concat_axis=0, tiled=True),
        "ga",
        split_axis=1,
        concat_axis=2,
        tiled=True,
    )
    wave_y = (rank_x * size_y + rank_y) * slab_share + rank_g * thin_rows + local_keys
    solved = spectral_solve(planes_data, wave_y, total_y)
    returned = lax.all_to_all(
        lax.all_to_all(solved, ("hx", "hy"), split_axis=0, concat_axis=1, tiled=True),
        "ga",
        split_axis=2,
        concat_axis=1,
        tiled=True,
    )
    from_group = keys_y // (thin_rows * size_x * size_y)
    remainder = keys_y % (thin_rows * size_x * size_y)
    column_keys = (
        remainder // thin_rows * slab_share + from_group * thin_rows + remainder % thin_rows
    )
    inverted = jnp.einsum(
        "ab,xbz->xaz", hartley(keys_y, column_keys, total_y), returned, precision=highest
    )
    potential = lax.all_to_all(inverted, "hy", split_axis=1, concat_axis=0, tiled=True)
    nx, ny, nz = density.shape
    cooled, xlo, xhi, ylo, yhi, zface = vmem_call(
        pack_kernel,
        [(nx, ny, nz)] + [(prim_n, ny, nz)] * 2 + [(prim_n, nx, nz)] * 2 + [(nx, ny, LANES)],
    )(density, velocity, pressure, species, newton_count)
    xbelow, xabove = shifted(xhi, "hx", 1), shifted(xlo, "hx", -1)
    ybelow, yabove = shifted(yhi, "hy", 1), shifted(ylo, "hy", -1)
    zbelow = shifted(zface, "ga", 1)
    zabove = zbelow if size_g == 2 else shifted(zface, "ga", -1)
    new_density, momentum, total_energy, species_mass = vmem_call(
        flux_kernel,
        [(nx, ny, nz), (3, nx, ny, nz), (nx, ny, nz), (species_n, nx, ny, nz)],
        scratch_shapes=[
            pltpu.VMEM((field_n, nx + 2, ny, nz), jnp.float32),
            pltpu.VMEM((2, field_n, nx, nz), jnp.float32),
        ],
    )(density, velocity, cooled, species, xbelow, xabove, ybelow, yabove, zbelow, zabove)
    gravity = []
    for d, axis in enumerate(("hx", "hy", "ga")):
        n = potential.shape[d]
        first = lax.slice_in_dim(potential, 0, 1, axis=d)
        last = lax.slice_in_dim(potential, n - 1, n, axis=d)
        wide = jnp.concatenate([shifted(last, axis, 1), potential, shifted(first, axis, -1)], axis=d)
        gravity.append(
            -0.5 * (lax.slice_in_dim(wide, 2, n + 2, axis=d) - lax.slice_in_dim(wide, 0, n, axis=d))
        )
    kick = time_step * density * jnp.stack(gravity)
    return (
        new_density,
        momentum + kick,
        total_energy + jnp.sum(kick * velocity, axis=0),
        species_mass,
        potential,
    )


def solution(mesh):
    in_specs = (
        P("hx", "hy", "ga"),
        P(None, "hx", "hy", "ga"),
        P("hx", "hy", "ga"),
        P(None, "hx", "hy", "ga"),
        P("hx", "hy", "ga"),
    )
    out_specs = (
        P("hx", "hy", "ga"),
        P(None, "hx", "hy", "ga"),
        P("hx", "hy", "ga"),
        P(None, "hx", "hy", "ga"),
        P("hx", "hy", "ga"),
    )
    return jax.shard_map(local, mesh=mesh, in_specs=in_specs, out_specs=out_specs, check_vma=False)
```

time: 167 us -> 92.2 us (0.55)
  local copies, waits for them, and re-layouts: 48.6 us -> 4.72 us
  other arithmetic: 42.5 us -> 3.98 us
  Pallas kernels: 0 us -> 10.6 us
  blocking collectives: 0 us -> 10.5 us
  starting transfers between devices: 34.8 us -> 28.5 us
  waiting for transfers between devices: 32.4 us -> 27.7 us
    sub x4 -> x0, other arithmetic: 16.6 us -> none  [the longest x3 9.84 us: face_flux(): 0.5 * (sides_data[0][1] + sides_data[1][1])]
    unnamed x42 -> x20, local copies, waits for them, and re-layouts: 15.9 us -> 1.22 us
    mul x14 -> x1, other arithmetic: 14.1 us -> 0.01 us  [local(): kick = time_step * density * jnp.stack(gravity)]
    slice x7 -> x3, local copies, waits for them, and re-layouts: 13.7 us -> 0.1 us  [local(): first = lax.slice_in_dim(potential, 0, 1, axis=d)]
    pallas_call x0 -> x2, Pallas kernels: none -> 10.6 us  [the longest x1 6.13 us: local(): vmem_call(flux_kernel, [(nx, ny, nz), (3, nx, ny, nz), (nx, ny, nz), (spe...]
    all_to_all x0 -> x1, blocking collectives: none -> 10.5 us  [local(): lax.all_to_all(solved, ('hx', 'hy'), split_axis=0, concat_axis=1, tiled=T...]
    ppermute x4 -> x0, local copies, waits for them, and re-layouts: 8.29 us -> none  [the longest x2 4.15 us: extended(): lax.ppermute(tail, axis, [(i, (i + 1) % count) for i in range(count)])]
    all_to_all x1 -> x0, waiting for transfers between devices: 5.02 us -> none  [local(): lax.all_to_all(solved, ('hx', 'hy'), split_axis=0, concat_axis=1, tiled=T...]
  transfers between devices with their start and end apart: 12 -> 16, of which waited for: 7 -> 7; matrix products, arithmetic and copies ran while one was open for 16% -> 0% of each run, Pallas kernels for 0% -> 12%
where the time goes in v1:
time: 92.2 us; the launch traced here: 91.5 us
  starting transfers between devices  28.5 us (31%)
  waiting for transfers between devices  27.7 us (30%)
  Pallas kernels  10.6 us (11%)
  blocking collectives  10.5 us (11%)
  local copies, waits for them, and re-layouts  4.72 us (5%)
  matrix products  4.47 us (5%)
  other arithmetic  3.98 us (4%)
  between operations  0.96 us (1%)
    all_to_all x1, blocking collectives, local(): lax.all_to_all(solved, ('hx', 'hy'), split_axis=0, concat_axis=1, tiled=T...  10.5 us
    ppermute x11, starting transfers between devices, shifted(): lax.ppermute(value, axis, [(i, (i + step) % count) for i in range(count)])  8.64 us
    all_to_all x1, waiting for transfers between devices, local(): lax.all_to_all(turned, ('hx', 'hy'), split_axis=1, concat_axis=0, tiled=T...  7.78 us
    ppermute x11, waiting for transfers between devices, shifted(): lax.ppermute(value, axis, [(i, (i + step) % count) for i in range(count)])  6.49 us
    pallas_call x1, Pallas kernels, local(): vmem_call(flux_kernel, [(nx, ny, nz), (3, nx, ny, nz), (nx, ny, nz), (spe...  6.13 us
    all_to_all x1, starting transfers between devices, local(): lax.all_to_all(turned, ('hx', 'hy'), split_axis=1, concat_axis=0, tiled=T...  5.52 us
    all_to_all x1, waiting for transfers between devices, local(): lax.all_to_all(density, 'hy', split_axis=0, concat_axis=1, tiled=True)  4.56 us
    pallas_call x1, Pallas kernels, local(): vmem_call(pack_kernel, [(nx, ny, nz)] + [(prim_n, ny, nz)] * 2 + [(prim_n...  4.52 us
  transfers between devices with their start and end apart: 16, of which 7 were waited for; matrix products, arithmetic and copies ran while one was open for 0% of the time, Pallas kernels for 12%

profile of v1, /device:TPU:0, one launch (start us, length us, event | category | flops | bytes accessed | tf_op | source)
XLA Modules:
  0.0 91.5 jit_solution(2668095033406565633)
XLA Ops:
  0.6 4.2 %all-to-all-start = ((f32[8,32,128]{2,1,0:T(8,128)}), f32[8,32,128]{2,1,0:T(8,128)S(1)}, u32[]{:S(2)}, u32[]{:S(2)}) async-start(f32[8,32,128]{2,1,0:T(8,128)} %den.3), calls=%async_computation | async-start | bytes 262144 | tf_op jit(solution)/shard_map/all_to_all | solution.py:227
  4.9 4.6 %all-to-all-done = f32[8,32,128]{2,1,0:T(8,128)S(1)} async-done(((f32[8,32,128]{2,1,0:T(8,128)}), f32[8,32,128]{2,1,0:T(8,128)S(1)}, u32[]{:S(2)}, u32[]{:S(2)}) %all-to-all-start) | async-done | bytes 131104 | tf_op jit(solution)/shard_map/all_to_all | solution.py:227
  9.5 0.5 convolution_bitcast_fusion.1
  10.0 0.8 copy.49
  10.8 5.5 %all-to-all-start.1 = ((f32[2,128,128]{2,0,1:T(2,128)}), f32[2,128,128]{2,0,1:T(2,128)S(1)}, u32[]{:S(2)}, u32[]{:S(2)}) async-start(f32[2,128,128]{2,0,1:T(2,128)} %copy.49), calls=%async_computation.1 | async-start | bytes 262144 | tf_op jit(solution)/shard_map/all_to_all | solution.py:230
  16.4 0.1 broadcast_add_fusion
  16.4 7.8 %all-to-all-done.1 = f32[2,128,128]{2,0,1:T(2,128)S(1)} async-done(((f32[2,128,128]{2,0,1:T(2,128)}), f32[2,128,128]{2,0,1:T(2,128)S(1)}, u32[]{:S(2)}, u32[]{:S(2)}) %all-to-all-start.1) | async-done | bytes 131104 | tf_op jit(solution)/shard_map/all_to_all | solution.py:230
  24.2 0.7 copy.52
  24.9 3.4 %all-to-all-start.2 = ((f32[32,8,128]{2,0,1:T(8,128)}), f32[32,8,128]{2,0,1:T(8,128)S(1)}, u32[]{:S(2)}, u32[]{:S(2)}) async-start(f32[32,8,128]{2,0,1:T(8,128)} %copy.52), calls=%async_computation.2 | async-start | bytes 262144 | tf_op jit(solution)/shard_map/all_to_all | solution.py:229
  28.4 4.4 %all-to-all-done.2 = f32[32,8,128]{2,0,1:T(8,128)S(1)} async-done(((f32[32,8,128]{2,0,1:T(8,128)}), f32[32,8,128]{2,0,1:T(8,128)S(1)}, u32[]{:S(2)}, u32[]{:S(2)}) %all-to-all-start.2) | async-done | bytes 131104 | tf_op jit(solution)/shard_map/all_to_all | solution.py:229
  32.8 0.1 copy.68
  32.9 0.1 all_to_all.89
  33.0 0.3 fusion.62
  33.3 1.3 %convolution_multiply_fusion = f32[32,4,256]{2,0,1:T(8,128)S(1)} fusion(f32[32,4,256]{2,0,1:T(8,128)S(1)} %fusion.62, f32[256]{0:T(256)S(1)} %multiply_add_fusion, f32[32,4]{0,1:T(4,128)S(1)} %broadcast_add_fusion), kind=kOutput, calls=%fused_computation | convolution fusion | flops 101875712 | bytes 263680 | tf_op jit(solution)/shard_map/ayz,zc->ayc/dot_general | solution.py:199
  34.7 0.3 fusion.60
  35.0 1.3 %fusion.3 = f32[32,4,256]{2,0,1:T(8,128)S(1)} fusion(f32[32,4,256]{2,0,1:T(8,128)S(1)} %fusion.60), kind=kOutput, calls=%fused_computation.11 | convolution fusion | flops 101646336 | bytes 262144 | tf_op jit(solution)/shard_map/ayz,zc->ayc/dot_general | solution.py:210
  36.4 0.1 copy.54
  36.5 10.5 %all_to_all.108 = f32[32,4,256]{2,1,0:T(4,128)S(1)} all-to-all(f32[32,4,256]{2,1,0:T(4,128)S(1)} %copy.54), channel_id=1, replica_groups=mesh['hx'=4,'hy'=4,'ga'=2] {'hx','hy'}, dimensions={0} | all-to-all | bytes 262144 | tf_op jit(solution)/shard_map/all_to_all | solution.py:239
  47.0 0.1 copy.55
  47.1 0.2 copy.56
  47.2 0.9 %reshape.122 = f32[2,1,16384]{2,1,0:T(1,128)} reshape(f32[256,2,64]{2,1,0:T(2,128)S(1)} %bitcast.68) | data formatting | bytes 262144
  48.1 3.4 %all-to-all-start.4 = ((f32[2,1,16384]{2,1,0:T(1,128)}), f32[2,1,16384]{2,1,0:T(1,128)S(1)}, u32[]{:S(2)}, u32[]{:S(2)}) async-start(f32[2,1,16384]{2,1,0:T(1,128)} %reshape.122), calls=%async_computation.4 | async-start | bytes 262144 | tf_op jit(solution)/shard_map/all_to_all | solution.py:238
  51.5 4.4 %all-to-all-done.4 = f32[2,1,16384]{2,1,0:T(1,128)S(1)} async-done(((f32[2,1,16384]{2,1,0:T(1,128)}), f32[2,1,16384]{2,1,0:T(1,128)S(1)}, u32[]{:S(2)}, u32[]{:S(2)}) %all-to-all-start.4) | async-done | bytes 131104 | tf_op jit(solution)/shard_map/all_to_all | solution.py:238
  56.0 0.5 broadcast.279
  56.5 1.0 %reduce = f32[2,16384]{1,0:T(2,128)S(1)} reduce(f32[2,1,16384]{2,1,0:T(1,128)S(1)} %all-to-all-done.4, f32[]{:T(128)} %broadcast.279), dimensions={1}, to_apply=%all_to_all.94.reduce_sub_computation | reduce | bytes 262148 | tf_op jit(solution)/shard_map/all_to_all | solution.py:238
  57.5 0.3 reshape.123
  57.8 0.1 copy.58
  57.9 0.6 convolution_bitcast_fusion
  58.5 0.8 copy.60
  59.2 3.3 %all-to-all-start.5 = ((f32[2,128,128]{2,0,1:T(2,128)}), f32[2,128,128]{2,0,1:T(2,128)S(1)}, u32[]{:S(2)}, u32[]{:S(2)}) async-start(f32[2,128,128]{2,0,1:T(2,128)} %copy.60), calls=%async_computation.5 | async-start | bytes 262144 | tf_op jit(solution)/shard_map/all_to_all | solution.py:253
  62.6 0.0 copy-start.2
  62.6 4.5 %shard_map.92 = (f32[8,32,128]{2,1,0:T(8,128)}, f32[14,32,128]{2,1,0:T(8,128)}, f32[14,32,128]{2,1,0:T(8,128)}, f32[14,8,128]{2,1,0:T(8,128)}, f32[14,8,128]{2,1,0:T(8,128)}, /*index=5*/f32[8,32,128]{2,1,0:T(8,128)}) custom-call(f32[8,32,128]{2,1,0:T(8,128)} %den.3, f32[3,8,32,128]{3,2,1,0:T(8,128)} %vel.3, f32[8,32,128]{2,1,0:T(8,128)} %pre.1, ...), custom_call_target="tpu_custom_call" | custom-call | tf_op jit(solution)/shard_map/pallas_call | solution.py:255
  67.1 3.8 %collective-permute-start.1 = (f32[14,32,128]{2,1,0:T(8,128)}, f32[14,32,128]{2,1,0:T(8,128)S(1)}, u32[]{:S(2)}, u32[]{:S(2)}) collective-permute-start(f32[14,32,128]{2,1,0:T(8,128)} %get-tuple-element.17), channel_id=1, source_target_pairs={{0,24},{8,0},{16,8},{24,16},{1,25},{9,1},{17,9},{25,17},{2,26},{10... | collective-permute-start | bytes 688136 | tf_op jit(solution)/shard_map/ppermute | solution.py:178
  70.9 1.7 %collective-permute-start.3 = (f32[14,8,128]{2,1,0:T(8,128)}, f32[14,8,128]{2,1,0:T(8,128)S(1)}, u32[]{:S(2)}, u32[]{:S(2)}) collective-permute-start(f32[14,8,128]{2,1,0:T(8,128)} %get-tuple-element.19), channel_id=1, source_target_pairs={{0,6},{2,0},{4,2},{6,4},{1,7},{3,1},{5,3},{7,5},{8,14},{10,8},{12,... | collective-permute-start | bytes 172040 | tf_op jit(solution)/shard_map/ppermute | solution.py:178
  72.7 0.0 collective-permute-start.4
  72.7 0.1 fusion.96
  72.8 1.9 %collective-permute-done.2.ybelow = f32[14,8,128]{2,1,0:T(8,128)S(1)} collective-permute-done((f32[14,8,128]{2,1,0:T(8,128)}, f32[14,8,128]{2,1,0:T(8,128)S(1)}, u32[]{:S(2)}, u32[]{:S(2)}) %collective-permute-start.2) | collective-permute-done | bytes 57376 | tf_op jit(solution)/shard_map/ppermute | solution.py:178
  74.7 0.2 collective-permute-start.10
  75.0 0.1 collective-permute-start.6
  75.0 4.2 %collective-permute-done.4.zbelow.zabove = f32[8,32,128]{2,1,0:T(8,128)S(1)} collective-permute-done((f32[8,32,128]{2,1,0:T(8,128)}, f32[8,32,128]{2,1,0:T(8,128)S(1)}, u32[]{:S(2)}, u32[]{:S(2)}) %collective-permute-start.4) | collective-permute-done | bytes 131104 | tf_op jit(solution)/shard_map/ppermute | solution.py:178
  79.3 1.1 %collective-permute-start.8 = (f32[8,1,128]{2,1,0:T(1,128)S(1)}, f32[8,1,128]{2,1,0:T(1,128)S(1)}, u32[]{:S(2)}, u32[]{:S(2)}) collective-permute-start(f32[8,1,128]{2,1,0:T(1,128)S(1)} %get-tuple-element.33), channel_id=1, source_target_pairs={{0,2},{2,4},{4,6},{6,0},{1,3},{3,5},{5,7},{7,1},{8,10},{10,12},{12... | collective-permute-start | bytes 12296 | tf_op jit(solution)/shard_map/ppermute | solution.py:178
  80.4 0.7 collective-permute-start.7
  81.1 0.4 collective-permute-done.10
  81.4 1.0 %collective-permute-start.9 = (f32[8,32,1]{2,1,0:T(8,128)S(1)}, f32[8,32,1]{2,1,0:T(8,128)S(1)}, u32[]{:S(2)}, u32[]{:S(2)}) collective-permute-start(f32[8,32,1]{2,1,0:T(8,128)S(1)} %get-tuple-element.34), channel_id=1, source_target_pairs={{0,1},{1,0},{2,3},{3,2},{4,5},{5,4},{6,7},{7,6},{8,9},{9,8},{10,11... | collective-permute-start | bytes 3080 | tf_op jit(solution)/shard_map/ppermute | solution.py:178
  82.5 6.1 %shard_map.93 = (f32[8,32,128]{2,1,0:T(8,128)}, f32[3,8,32,128]{3,2,1,0:T(8,128)}, f32[8,32,128]{2,1,0:T(8,128)}, f32[9,8,32,128]{3,2,1,0:T(8,128)}) custom-call(f32[8,32,128]{2,1,0:T(8,128)} %den.3, f32[3,8,32,128]{3,2,1,0:T(8,128)} %vel.3, f32[8,32,128]{2,1,0:T(8,128)} %get-tuple-element.15.cooled, f32[9,8,32,128]{3,2,1,0:T(8,128)} %spe.3, ...), custom_call_target="tpu_custom_call" | custom-call | tf_op jit(solution)/shard_map/pallas_call | solution.py:263
  88.7 0.2 fusion.21
  88.9 1.9 %multiply_reduce_fusion = (f32[8,32,128]{2,1,0:T(8,128)S(1)}, f32[3,8,32,128]{3,2,1,0:T(8,128)}) fusion(f32[3,8,32,128]{3,2,1,0:T(8,128)S(1)} %copy-done, f32[1,8,32,128]{3,2,1,0:T(8,128)S(1)} %get-tuple-element.29, f32[1,8,32,128]{3,2,1,0:T(8,128)S(1)} %get-tuple-element.28, f32[1,8,32,128]{3,2,1,0:T(8,128)S(1)} %get-tuple-element.27, ...), kind=kLoop, calls=%fused_computation.4 | loop fusion | flops 557056 | bytes 1835008 | tf_op jit(solution)/shard_map/reduce_sum | solution.py:284
  90.8 0.7 add.175
  (41 shorter events, 0.3 us)
Async XLA Ops:
  0.6 8.8 %all-to-all-start = ((f32[8,32,128]{2,1,0:T(8,128)}), f32[8,32,128]{2,1,0:T(8,128)S(1)}, u32[]{:S(2)}, u32[]{:S(2)}) async-start(f32[8,32,128]{2,1,0:T(8,128)} %den.3), calls=%async_computation | async-start | bytes 262144 | tf_op jit(solution)/shard_map/all_to_all | solution.py:227
  10.8 13.4 %all-to-all-start.1 = ((f32[2,128,128]{2,0,1:T(2,128)}), f32[2,128,128]{2,0,1:T(2,128)S(1)}, u32[]{:S(2)}, u32[]{:S(2)}) async-start(f32[2,128,128]{2,0,1:T(2,128)} %copy.49), calls=%async_computation.1 | async-start | bytes 262144 | tf_op jit(solution)/shard_map/all_to_all | solution.py:230
  24.9 7.8 %all-to-all-start.2 = ((f32[32,8,128]{2,0,1:T(8,128)}), f32[32,8,128]{2,0,1:T(8,128)S(1)}, u32[]{:S(2)}, u32[]{:S(2)}) async-start(f32[32,8,128]{2,0,1:T(8,128)} %copy.52), calls=%async_computation.2 | async-start | bytes 262144 | tf_op jit(solution)/shard_map/all_to_all | solution.py:229
  48.1 7.8 %all-to-all-start.4 = ((f32[2,1,16384]{2,1,0:T(1,128)}), f32[2,1,16384]{2,1,0:T(1,128)S(1)}, u32[]{:S(2)}, u32[]{:S(2)}) async-start(f32[2,1,16384]{2,1,0:T(1,128)} %reshape.122), calls=%async_computation.4 | async-start | bytes 262144 | tf_op jit(solution)/shard_map/all_to_all | solution.py:238
  59.2 13.5 %all-to-all-start.5 = ((f32[2,128,128]{2,0,1:T(2,128)}), f32[2,128,128]{2,0,1:T(2,128)S(1)}, u32[]{:S(2)}, u32[]{:S(2)}) async-start(f32[2,128,128]{2,0,1:T(2,128)} %copy.60), calls=%async_computation.5 | async-start | bytes 262144 | tf_op jit(solution)/shard_map/all_to_all | solution.py:253
  62.6 19.9 %copy-start.2 = (f32[8,32,128]{2,1,0:T(8,128)S(1)}, f32[8,32,128]{2,1,0:T(8,128)}, u32[]{:S(2)}) copy-start(f32[8,32,128]{2,1,0:T(8,128)} %den.3) | copy-start | bytes 393220
  67.1 12.2 %collective-permute-start = (f32[14,32,128]{2,1,0:T(8,128)}, f32[14,32,128]{2,1,0:T(8,128)S(1)}, u32[]{:S(2)}, u32[]{:S(2)}) collective-permute-start(f32[14,32,128]{2,1,0:T(8,128)} %get-tuple-element.16), channel_id=1, source_target_pairs={{0,8},{8,16},{16,24},{24,0},{1,9},{9,17},{17,25},{25,1},{2,10},{10... | collective-permute-start | bytes 688136 | tf_op jit(solution)/shard_map/ppermute | solution.py:178
  67.1 13.3 %collective-permute-start.1 = (f32[14,32,128]{2,1,0:T(8,128)}, f32[14,32,128]{2,1,0:T(8,128)S(1)}, u32[]{:S(2)}, u32[]{:S(2)}) collective-permute-start(f32[14,32,128]{2,1,0:T(8,128)} %get-tuple-element.17), channel_id=1, source_target_pairs={{0,24},{8,0},{16,8},{24,16},{1,25},{9,1},{17,9},{25,17},{2,26},{10... | collective-permute-start | bytes 688136 | tf_op jit(solution)/shard_map/ppermute | solution.py:178
  70.9 3.8 %collective-permute-start.2 = (f32[14,8,128]{2,1,0:T(8,128)}, f32[14,8,128]{2,1,0:T(8,128)S(1)}, u32[]{:S(2)}, u32[]{:S(2)}) collective-permute-start(f32[14,8,128]{2,1,0:T(8,128)} %get-tuple-element.18), channel_id=1, source_target_pairs={{0,2},{2,4},{4,6},{6,0},{1,3},{3,5},{5,7},{7,1},{8,10},{10,12},{12... | collective-permute-start | bytes 172040 | tf_op jit(solution)/shard_map/ppermute | solution.py:178
  70.9 4.0 %collective-permute-start.3 = (f32[14,8,128]{2,1,0:T(8,128)}, f32[14,8,128]{2,1,0:T(8,128)S(1)}, u32[]{:S(2)}, u32[]{:S(2)}) collective-permute-start(f32[14,8,128]{2,1,0:T(8,128)} %get-tuple-element.19), channel_id=1, source_target_pairs={{0,6},{2,0},{4,2},{6,4},{1,7},{3,1},{5,3},{7,5},{8,14},{10,8},{12,... | collective-permute-start | bytes 172040 | tf_op jit(solution)/shard_map/ppermute | solution.py:178
  72.7 6.6 %collective-permute-start.4 = (f32[8,32,128]{2,1,0:T(8,128)}, f32[8,32,128]{2,1,0:T(8,128)S(1)}, u32[]{:S(2)}, u32[]{:S(2)}) collective-permute-start(f32[8,32,128]{2,1,0:T(8,128)} %get-tuple-element.20), channel_id=1, source_target_pairs={{0,1},{1,0},{2,3},{3,2},{4,5},{5,4},{6,7},{7,6},{8,9},{9,8},{10,11... | collective-permute-start | bytes 393224 | tf_op jit(solution)/shard_map/ppermute | solution.py:178
  72.7 16.0 %copy-start.1 = (f32[4,2,32,128]{3,2,1,0:T(8,128)}, f32[4,2,32,128]{3,2,1,0:T(8,128)S(1)}, u32[]{:S(2)}) copy-start(f32[4,2,32,128]{3,2,1,0:T(8,128)S(1)} %copy.62) | copy-start | bytes 393220
  74.7 7.7 %copy-start.7 = (f32[14,8,128]{2,1,0:T(8,128)}, f32[14,8,128]{2,1,0:T(8,128)S(1)}, u32[]{:S(2)}) copy-start(f32[14,8,128]{2,1,0:T(8,128)S(1)} %collective-permute-done.2.ybelow) | copy-start | bytes 172036
  74.7 6.7 %collective-permute-start.10 = (f32[8,32,1]{2,1,0:T(8,128)S(1)}, f32[8,32,1]{2,1,0:T(8,128)S(1)}, u32[]{:S(2)}, u32[]{:S(2)}) collective-permute-start(f32[8,32,1]{2,1,0:T(8,128)S(1)} %get-tuple-element.35), channel_id=1, source_target_pairs={{0,1},{1,0},{2,3},{3,2},{4,5},{5,4},{6,7},{7,6},{8,9},{9,8},{10,11... | collective-permute-start | bytes 3080 | tf_op jit(solution)/shard_map/ppermute | solution.py:178
  75.0 7.5 %copy-start.8 = (f32[14,8,128]{2,1,0:T(8,128)}, f32[14,8,128]{2,1,0:T(8,128)S(1)}, u32[]{:S(2)}) copy-start(f32[14,8,128]{2,1,0:T(8,128)S(1)} %collective-permute-done.3.yabove) | copy-start | bytes 172036
  75.0 13.7 %collective-permute-start.6 = (f32[1,32,128]{2,1,0:T(8,128)S(1)}, f32[1,32,128]{2,1,0:T(8,128)S(1)}, u32[]{:S(2)}, u32[]{:S(2)}) collective-permute-start(f32[1,32,128]{2,1,0:T(8,128)S(1)} %get-tuple-element.31), channel_id=1, source_target_pairs={{0,8},{8,16},{16,24},{24,0},{1,9},{9,17},{17,25},{25,1},{2,10},{10... | collective-permute-start | bytes 49160 | tf_op jit(solution)/shard_map/ppermute | solution.py:178
  79.3 3.2 %copy-start.3 = (f32[8,32,128]{2,1,0:T(8,128)}, f32[8,32,128]{2,1,0:T(8,128)S(1)}, u32[]{:S(2)}) copy-start(f32[8,32,128]{2,1,0:T(8,128)S(1)} %collective-permute-done.4.zbelow.zabove) | copy-start | bytes 393220
  79.3 9.4 %collective-permute-start.5 = (f32[1,32,128]{2,1,0:T(8,128)S(1)}, f32[1,32,128]{2,1,0:T(8,128)S(1)}, u32[]{:S(2)}, u32[]{:S(2)}) collective-permute-start(f32[1,32,128]{2,1,0:T(8,128)S(1)} %get-tuple-element.30), channel_id=1, source_target_pairs={{0,24},{8,0},{16,8},{24,16},{1,25},{9,1},{17,9},{25,17},{2,26},{10... | collective-permute-start | bytes 49160 | tf_op jit(solution)/shard_map/ppermute | solution.py:178
  79.3 3.2 %copy-start.4 = (f32[14,32,128]{2,1,0:T(8,128)}, f32[14,32,128]{2,1,0:T(8,128)S(1)}, u32[]{:S(2)}) copy-start(f32[14,32,128]{2,1,0:T(8,128)S(1)} %collective-permute-done.xbelow) | copy-start | bytes 688132
  79.3 9.4 %collective-permute-start.8 = (f32[8,1,128]{2,1,0:T(1,128)S(1)}, f32[8,1,128]{2,1,0:T(1,128)S(1)}, u32[]{:S(2)}, u32[]{:S(2)}) collective-permute-start(f32[8,1,128]{2,1,0:T(1,128)S(1)} %get-tuple-element.33), channel_id=1, source_target_pairs={{0,2},{2,4},{4,6},{6,0},{1,3},{3,5},{5,7},{7,1},{8,10},{10,12},{12... | collective-permute-start | bytes 12296 | tf_op jit(solution)/shard_map/ppermute | solution.py:178
  80.4 2.1 %copy-start.5 = (f32[14,32,128]{2,1,0:T(8,128)}, f32[14,32,128]{2,1,0:T(8,128)S(1)}, u32[]{:S(2)}) copy-start(f32[14,32,128]{2,1,0:T(8,128)S(1)} %collective-permute-done.1.xabove) | copy-start | bytes 688132
  80.4 8.3 %collective-permute-start.7 = (f32[8,1,128]{2,1,0:T(1,128)S(1)}, f32[8,1,128]{2,1,0:T(1,128)S(1)}, u32[]{:S(2)}, u32[]{:S(2)}) collective-permute-start(f32[8,1,128]{2,1,0:T(1,128)S(1)} %get-tuple-element.32), channel_id=1, source_target_pairs={{0,6},{2,0},{4,2},{6,4},{1,7},{3,1},{5,3},{7,5},{8,14},{10,8},{12,... | collective-permute-start | bytes 12296 | tf_op jit(solution)/shard_map/ppermute | solution.py:178
  81.4 7.2 %collective-permute-start.9 = (f32[8,32,1]{2,1,0:T(8,128)S(1)}, f32[8,32,1]{2,1,0:T(8,128)S(1)}, u32[]{:S(2)}, u32[]{:S(2)}) collective-permute-start(f32[8,32,1]{2,1,0:T(8,128)S(1)} %get-tuple-element.34), channel_id=1, source_target_pairs={{0,1},{1,0},{2,3},{3,2},{4,5},{5,4},{6,7},{7,6},{8,9},{9,8},{10,11... | collective-permute-start | bytes 3080 | tf_op jit(solution)/shard_map/ppermute | solution.py:178
  82.5 6.4 %copy-start = (f32[3,8,32,128]{3,2,1,0:T(8,128)S(1)}, f32[3,8,32,128]{3,2,1,0:T(8,128)}, u32[]{:S(2)}) copy-start(f32[3,8,32,128]{3,2,1,0:T(8,128)} %vel.3) | copy-start | bytes 1179652
  88.7 2.1 %copy-start.6 = (f32[8,32,128]{2,1,0:T(8,128)S(1)}, f32[8,32,128]{2,1,0:T(8,128)}, u32[]{:S(2)}) copy-start(f32[8,32,128]{2,1,0:T(8,128)} %get-tuple-element.23) | copy-start | bytes 393220

commit v2 on v1

--- a/solution.py
+++ b/solution.py
@@ -178,80 +178,234 @@
     return lax.ppermute(value, axis, [(i, (i + step) % count) for i in range(count)])
 
 
-def hartley(row_keys, col_keys, length):
-    phase = row_keys[:, None] * col_keys[None, :] % length
-    angle = 2.0 * jnp.pi / length * phase.astype(jnp.float32)
-    return jnp.cos(angle) + jnp.sin(angle)
-
-
-def eigen_keys(keys, extent):
-    return 2.0 * jnp.cos(2.0 * jnp.pi / extent * keys.astype(jnp.float32)) - 2.0
-
-
-def spectral_solve(planes_data, wave_y, total_y):
-    total_x = planes_data.shape[0]
-    total_z = planes_data.shape[2]
-    keys_x = jnp.arange(total_x, dtype=jnp.int32)
-    keys_z = jnp.arange(total_z, dtype=jnp.int32)
-    table_x = hartley(keys_x, keys_x, total_x)
-    table_z = hartley(keys_z, keys_z, total_z)
-    turned = jnp.einsum("ab,byz->ayz", table_x, planes_data, precision=highest)
-    turned = jnp.einsum("ayz,zc->ayc", turned, table_z, precision=highest)
-    total = (
-        eigen_keys(keys_x, total_x)[:, None, None]
-        + eigen_keys(wave_y, total_y)[None, :, None]
-        + eigen_keys(keys_z, total_z)[None, None, :]
-    )
-    green = jnp.where(total < 0.0, 1.0 / jnp.where(total < 0.0, total, -1.0), 0.0) / (
-        total_x * total_y * total_z
-    )
-    turned = turned * green
-    turned = jnp.einsum("ab,byz->ayz", table_x, turned, precision=highest)
-    return jnp.einsum("ayz,zc->ayc", turned, table_z, precision=highest)
+def hartley(rows, columns, length):
+    angle = 2.0 * np.pi / length * (np.outer(rows, columns) % length)
+    return np.cos(angle) + np.sin(angle)
+
+
+def curvature(length):
+    return 4.0 * np.sin(np.pi / length * np.arange(length)) ** 2
+
+
+def decay_tables(nx, ny, nz):
+    mu = curvature(nz)[:, None] + curvature(ny)[None, :]
+    mu[0, 0] = 1.0
+    root = np.sqrt(mu * (4.0 + mu))
+    decay = 2.0 / (2.0 + mu + root)
+    return np.stack([decay, 1.0 / (1.0 - decay**nx), -1.0 / (root * ny * nz)]).astype(np.float32)
+
+
+def flat_mode_table(block, nx, ny, nz):
+    rows = -(-(block + 2) // 8) * 8
+    cell = np.arange(-1, rows - 1)[:, None]
+    segment = np.arange(nx // block)[:, None]
+    source = (np.arange(block)[None, :] - block * segment).reshape(1, -1)
+    gap = (cell - source) % nx
+    table = gap * (nx - gap) / (2.0 * nx) - (nx * nx - 1.0) / (12.0 * nx)
+    return (table / (ny * nz)).astype(np.float32)
+
+
+def along_z_kernel(part, den, table, out):
+    nx, ny, nz = den.shape
+    out[...] = lax.dot_general(
+        table[part[0]], den[...].reshape(nx * ny, nz), (((1,), (1,)), ((), ())),
+        precision=highest, preferred_element_type=jnp.float32,
+    )
+
+
+def segments(kz, width):
+    return lax.broadcasted_iota(jnp.int32, (kz, LANES), 1) // width
+
+
+def turned(value, lanes):
+    lanes = lanes % LANES
+    return pltpu.roll(value, lanes, 1) if lanes else value
+
+
+def along_y_kernel(size_g, block, parts, lines, table_y, tables, modes, sums, grid_rows):
+    groups, kz, _ = lines.shape
+    nx, _, ny = modes.shape
+    width = block
+    per = LANES // width
+    place = segments(kz, width)
+    for column in range(ny // LANES):
+        for high in range(nx // per):
+            source = []
+            for s in range(per):
+                first = (column * per + s) * size_g
+                total = lines[first, :, high * LANES : (high + 1) * LANES]
+                for g in range(1, size_g):
+                    total = total + lines[first + g, :, high * LANES : (high + 1) * LANES]
+                source.append(total)
+            for low in range(per):
+                line = turned(source[0], -low * width)
+                for s in range(1, per):
+                    line = jnp.where(place == s, turned(source[s], (s - low) * width), line)
+                x = high * per + low
+                grid_rows[x * kz : (x + 1) * kz, column * LANES : (column + 1) * LANES] = line
+    spectrum = jnp.dot(
+        grid_rows[...], table_y[...], precision=highest, preferred_element_type=jnp.float32
+    )
+    modes[...] = spectrum.reshape(nx, kz, ny)
+    decay = tables[0, pl.ds(parts[0] * kz, kz), :]
+    forward, backward = modes[0], modes[nx - 1]
+    for x in range(1, nx):
+        forward = forward * decay + modes[x]
+        backward = backward * decay + modes[nx - 1 - x]
+    sums[0:kz] = forward
+    sums[kz : 2 * kz] = backward
+    for x in range(nx):
+        sums[2 * kz + x : 2 * kz + x + 1] = modes[x, 0:1, :]
+
+
+def along_x_kernel(count, size_g, block, parts, modes, own, *rest):
+    others = rest[: count - 1]
+    table_y, tables, flat_table, out, gathered, potential, lines = rest[count - 1 :]
+    nx, kz, ny = modes.shape
+    width = block
+    per = LANES // width
+    for s in range(count):
+        seen = own if s == 0 else others[s - 1]
+        gathered[s * nx : (s + 1) * nx] = seen[2 * kz : 2 * kz + nx]
+    flat = jnp.dot(
+        flat_table[...], gathered[...], precision=highest, preferred_element_type=jnp.float32
+    )
+    for tile in range(0, kz, 8):
+        rows = slice(tile, tile + 8)
+        at = pl.ds(parts[0] * kz + tile, 8)
+        decay, closing, scale = tables[0, at, :], tables[1, at, :], tables[2, at, :]
+        far = decay
+        for _ in range(int(math.log2(nx))):
+            far = far * far
+        left = own[tile : tile + 8]
+        right = own[kz + tile : kz + tile + 8]
+        for s in range(count - 1, 0, -1):
+            left = left * far + others[s - 1][tile : tile + 8]
+            right = right * far + others[count - s - 1][kz + tile : kz + tile + 8]
+        left, right = left * closing, right * closing
+        from_left = [left]
+        for x in range(nx):
+            from_left.append(from_left[-1] * decay + modes[x, rows])
+        result = [None] * (nx + 2)
+        result[nx + 1] = from_left[nx] * decay + right
+        behind = right
+        for x in range(nx - 1, -1, -1):
+            result[x + 1] = behind * decay + from_left[x + 1]
+            behind = behind * decay + modes[x, rows]
+        result[0] = from_left[0] + behind * decay
+        if tile == 0:
+            first = lax.broadcasted_iota(jnp.int32, (8, ny), 0) + lax.broadcasted_iota(jnp.int32, (8, ny), 1)
+            first = first + parts[0] == 0
+        for x in range(nx + 2):
+            value = result[x] * scale
+            if tile == 0:
+                value = jnp.where(first, flat[x : x + 1, :], value)
+            potential[x * kz + tile : x * kz + tile + 8] = value
+    lines[...] = jnp.dot(
+        potential[...], table_y[...], precision=highest, preferred_element_type=jnp.float32
+    )
+    place = segments(kz, width)
+    lane = lax.broadcasted_iota(jnp.int32, (kz, LANES), 1)
+
+    def line(x, column):
+        return lines[(x + 1) * kz : (x + 2) * kz, column * LANES : (column + 1) * LANES]
+
+    for target in range(ny // width):
+        column, s = target // per, target % per
+        pieces = []
+        for high in range(nx // per):
+            piece = turned(line(high * per, column), -s * width)
+            for low in range(1, per):
+                piece = jnp.where(place == low, turned(line(high * per + low, column), (low - s) * width), piece)
+            pieces.append(piece)
+        edge = turned(line(-1, column), -s * width)
+        edge = jnp.where(place == 1, turned(line(nx, column), (1 - s) * width), edge)
+        for side, y in enumerate((target * width - 1, (target + 1) * width)):
+            y = y % ny
+            for x in range(nx):
+                slot = 2 * width + side * nx + x
+                edge = jnp.where(lane == slot, turned(line(x, y // LANES), slot - y % LANES), edge)
+        pieces.append(edge)
+        for g in range(size_g):
+            for p, piece in enumerate(pieces):
+                out[target * size_g + g, :, p * LANES : (p + 1) * LANES] = piece
+
+
+def gravity_kernel(part, planes, table, den, vel, momentum_in, energy_in, potential, momentum, energy, solved, edges):
+    nx, ny, nz = den.shape
+    groups, kz, width = planes.shape
+    main = nx * ny
+    flat = planes[...].reshape(groups * kz, width)
+    here = table[part[0]]
+    contract = (((0,), (0,)), ((), ()))
+    solved[...] = lax.dot_general(
+        flat[:, :main], here, contract, precision=highest, preferred_element_type=jnp.float32
+    )
+    edges[...] = lax.dot_general(
+        flat[:, main:], here[:, :nz], contract, precision=highest, preferred_element_type=jnp.float32
+    )
+    row = lax.broadcasted_iota(jnp.int32, (ny, nz), 0)
+    for x in range(nx):
+        value = solved[x * ny : (x + 1) * ny, :nz]
+        potential[x] = value
+        above = solved[(x + 1) * ny : (x + 2) * ny, :nz] if x < nx - 1 else edges[ny : 2 * ny]
+        below = solved[(x - 1) * ny : x * ny, :nz] if x > 0 else edges[:ny]
+        at = 2 * ny + x
+        right = jnp.where(row == ny - 1, edges[at + nx : at + nx + 1], pltpu.roll(value, ny - 1, 0))
+        left = jnp.where(row == 0, edges[at : at + 1], pltpu.roll(value, 1, 0))
+        pull = time_step * den[x]
+        kicks = [
+            pull * (-0.5 * (above - below)),
+            pull * (-0.5 * (right - left)),
+            pull * solved[x * ny : (x + 1) * ny, nz:],
+        ]
+        work = energy_in[x]
+        for d in range(3):
+            momentum[d, x] = momentum_in[d, x] + kicks[d]
+            work = work + kicks[d] * vel[d, x]
+        energy[x] = work
 
 
 def local(density, velocity, pressure, species, newton_count):
-    size_x = lax.axis_size("hx")
-    size_y = lax.axis_size("hy")
-    size_g = lax.axis_size("ga")
-    rank_x = lax.axis_index("hx")
-    rank_y = lax.axis_index("hy")
-    rank_g = lax.axis_index("ga")
-    rows_y = density.shape[1]
-    total_y = rows_y * size_y
-    slab_share = rows_y // size_x
-    thin_rows = slab_share // size_g
-    keys_y = jnp.arange(total_y, dtype=jnp.int32)
-    local_keys = jnp.arange(thin_rows, dtype=jnp.int32)
-    table_y = hartley(keys_y, keys_y, total_y)
-    gathered = lax.all_to_all(density, "hy", split_axis=0, concat_axis=1, tiled=True)
-    turned = jnp.einsum("ab,xbz->xaz", table_y, gathered, precision=highest)
-    planes_data = lax.all_to_all(
-        lax.all_to_all(turned, ("hx", "hy"), split_axis=1, concat_axis=0, tiled=True),
-        "ga",
-        split_axis=1,
-        concat_axis=2,
-        tiled=True,
-    )
-    wave_y = (rank_x * size_y + rank_y) * slab_share + rank_g * thin_rows + local_keys
-    solved = spectral_solve(planes_data, wave_y, total_y)
-    returned = lax.all_to_all(
-        lax.all_to_all(solved, ("hx", "hy"), split_axis=0, concat_axis=1, tiled=True),
-        "ga",
-        split_axis=2,
-        concat_axis=1,
-        tiled=True,
-    )
-    from_group = keys_y // (thin_rows * size_x * size_y)
-    remainder = keys_y % (thin_rows * size_x * size_y)
-    column_keys = (
-        remainder // thin_rows * slab_share + from_group * thin_rows + remainder % thin_rows
-    )
-    inverted = jnp.einsum(
-        "ab,xbz->xaz", hartley(keys_y, column_keys, total_y), returned, precision=highest
-    )
-    potential = lax.all_to_all(inverted, "hy", split_axis=1, concat_axis=0, tiled=True)
+    size_x, size_y, size_g = (lax.axis_size(a) for a in ("hx", "hy", "ga"))
     nx, ny, nz = density.shape
+    all_x, all_y, all_z = nx * size_x, ny * size_y, nz * size_g
+    groups = size_y * size_g
+    kz = all_z // groups
+    in_g = lax.axis_index("ga").astype(jnp.int32).reshape(1)
+    in_plane = (lax.axis_index("hy") * size_g + lax.axis_index("ga")).astype(jnp.int32).reshape(1)
+    main = nx * ny
+    width = main + LANES
+
+    keys_z = np.arange(all_z)
+    table_z = hartley(keys_z, keys_z, all_z)
+    ahead = hartley(keys_z, keys_z + 1, all_z)
+    behind = hartley(keys_z, keys_z - 1, all_z)
+    into_z = jnp.asarray(table_z.reshape(all_z, size_g, nz).transpose(1, 0, 2), jnp.float32)
+    pull_z = -0.5 * (ahead - behind)
+    from_z = np.concatenate(
+        [t.reshape(all_z, size_g, nz).transpose(1, 0, 2) for t in (table_z, pull_z)], axis=2
+    )
+    from_z = jnp.asarray(from_z, jnp.float32)
+    keys_y = np.arange(all_y)
+    table_y = jnp.asarray(hartley(keys_y, keys_y, all_y), jnp.float32)
+    tables = jnp.asarray(decay_tables(all_x, all_y, all_z))
+    flat_table = jnp.asarray(flat_mode_table(nx, all_x, all_y, all_z))
+
+    scalar = pl.BlockSpec(memory_space=pltpu.SMEM)
+
+    def call(kernel, inputs, out_shape, scratch=(), **more):
+        specs = [scalar] + [pl.BlockSpec(memory_space=pltpu.VMEM)] * (len(inputs) - 1)
+        return vmem_call(
+            kernel, out_shape, in_specs=specs,
+            scratch_shapes=[pltpu.VMEM(s, jnp.float32) for s in scratch], **more,
+        )(*inputs)
+
+    (spectral,) = call(along_z_kernel, (in_g, density, into_z), [(all_z, main)])
+    spectral = lax.all_to_all(
+        spectral.reshape(groups, kz, main), ("hy", "ga"), split_axis=0, concat_axis=0, tiled=True
+    )
+
     cooled, xlo, xhi, ylo, yhi, zface = vmem_call(
         pack_kernel,
         [(nx, ny, nz)] + [(prim_n, ny, nz)] * 2 + [(prim_n, nx, nz)] * 2 + [(nx, ny, LANES)],
@@ -260,6 +414,22 @@
     ybelow, yabove = shifted(yhi, "hy", 1), shifted(ylo, "hy", -1)
     zbelow = shifted(zface, "ga", 1)
     zabove = zbelow if size_g == 2 else shifted(zface, "ga", -1)
+
+    modes, sums = call(
+        functools.partial(along_y_kernel, size_g, ny),
+        (in_plane, spectral, table_y, tables),
+        [(nx, kz, all_y), (2 * kz + nx, all_y)],
+        [(nx * kz, all_y)],
+    )
+    others = [shifted(sums, "hx", s) for s in range(1, size_x)]
+    (planes,) = call(
+        functools.partial(along_x_kernel, size_x, size_g, ny),
+        (in_plane, modes, sums, *others, table_y, tables, flat_table),
+        [(groups, kz, width)],
+        [(all_x, all_y), ((nx + 2) * kz, all_y), ((nx + 2) * kz, all_y)],
+    )
+    planes = lax.all_to_all(planes, ("hy", "ga"), split_axis=0, concat_axis=0, tiled=True)
+
     new_density, momentum, total_energy, species_mass = vmem_call(
         flux_kernel,
         [(nx, ny, nz), (3, nx, ny, nz), (nx, ny, nz), (species_n, nx, ny, nz)],
@@ -268,38 +438,23 @@
             pltpu.VMEM((2, field_n, nx, nz), jnp.float32),
         ],
     )(density, velocity, cooled, species, xbelow, xabove, ybelow, yabove, zbelow, zabove)
-    gravity = []
-    for d, axis in enumerate(("hx", "hy", "ga")):
-        n = potential.shape[d]
-        first = lax.slice_in_dim(potential, 0, 1, axis=d)
-        last = lax.slice_in_dim(potential, n - 1, n, axis=d)
-        wide = jnp.concatenate([shifted(last, axis, 1), potential, shifted(first, axis, -1)], axis=d)
-        gravity.append(
-            -0.5 * (lax.slice_in_dim(wide, 2, n + 2, axis=d) - lax.slice_in_dim(wide, 0, n, axis=d))
-        )
-    kick = time_step * density * jnp.stack(gravity)
-    return (
-        new_density,
-        momentum + kick,
-        total_energy + jnp.sum(kick * velocity, axis=0),
-        species_mass,
-        potential,
-    )
+
+    potential, momentum, total_energy = call(
+        gravity_kernel,
+        (in_g, planes, from_z, density, velocity, momentum, total_energy),
+        [(nx, ny, nz), (3, nx, ny, nz), (nx, ny, nz)],
+        [(main, 2 * nz), (LANES, nz)],
+    )
+    return (new_density, momentum, total_energy, species_mass, potential)
 
 
 def solution(mesh):
-    in_specs = (
-        P("hx", "hy", "ga"),
-        P(None, "hx", "hy", "ga"),
-        P("hx", "hy", "ga"),
-        P(None, "hx", "hy", "ga"),
-        P("hx", "hy", "ga"),
-    )
-    out_specs = (
-        P("hx", "hy", "ga"),
-        P(None, "hx", "hy", "ga"),
-        P("hx", "hy", "ga"),
-        P(None, "hx", "hy", "ga"),
-        P("hx", "hy", "ga"),
-    )
-    return jax.shard_map(local, mesh=mesh, in_specs=in_specs, out_specs=out_specs, check_vma=False)
+    cells = P("hx", "hy", "ga")
+    fields = P(None, "hx", "hy", "ga")
+    return jax.shard_map(
+        local,
+        mesh=mesh,
+        in_specs=(cells, fields, cells, fields, cells),
+        out_specs=(cells, fields, cells, fields, cells),
+        check_vma=False,
+    )

time: 92.2 us -> 60.5 us (0.66)
  waiting for transfers between devices: 27.7 us -> 14.5 us
  blocking collectives: 10.5 us -> 0 us
  Pallas kernels: 10.6 us -> 20.4 us
  starting transfers between devices: 28.5 us -> 21.6 us
  matrix products: 4.47 us -> 0 us
  other arithmetic: 3.98 us -> 0 us
  local copies, waits for them, and re-layouts: 4.72 us -> 2.73 us
    all_to_all x5 -> x2, waiting for transfers between devices: 21.2 us -> 6.01 us  [the longest x1 6 us: local(): lax.all_to_all(spectral.reshape(groups, kz, main), ('hy', 'ga'), split_ax...]
    all_to_all x5 -> x2, starting transfers between devices: 19.9 us -> 8.65 us  [the longest x1 5.2 us: local(): lax.all_to_all(spectral.reshape(groups, kz, main), ('hy', 'ga'), split_ax...]
    all_to_all x1 -> x0, blocking collectives: 10.5 us -> none  [local(): lax.all_to_all(solved, ('hx', 'hy'), split_axis=0, concat_axis=1, tiled=T...]
    pallas_call x0 -> x4, Pallas kernels: none -> 9.89 us  [call(): vmem_call(kernel, out_shape, in_specs=specs, scratch_shapes=[pltpu.VMEM(s...]
    dot_general x6 -> x0, matrix products: 4.47 us -> none  [the longest x1 1.34 us: spectral_solve(): turned = jnp.einsum('ayz,zc->ayc', turned, table_z, precision=highest)]
    ppermute x11 -> x8, starting transfers between devices: 8.64 us -> 13 us  [shifted(): lax.ppermute(value, axis, [(i, (i + step) % count) for i in range(count)])]
    ppermute x11 -> x8, waiting for transfers between devices: 6.49 us -> 8.53 us  [shifted(): lax.ppermute(value, axis, [(i, (i + step) % count) for i in range(count)])]
    reduce_sum x1 -> x0, other arithmetic: 1.88 us -> none  [local(): jnp.sum(kick * velocity, axis=0)]
  transfers between devices with their start and end apart: 16 -> 10, of which waited for: 7 -> 8; matrix products, arithmetic and copies ran while one was open for 0% -> 0% of each run, Pallas kernels for 12% -> 18%
where the time goes in v2:
time: 60.5 us; the launch traced here: 60 us
  starting transfers between devices  21.6 us (36%)
  Pallas kernels  20.4 us (34%)
  waiting for transfers between devices  14.5 us (24%)
  local copies, waits for them, and re-layouts  2.73 us (5%)
  between operations  0.68 us (1%)
    ppermute x8, starting transfers between devices, shifted(): lax.ppermute(value, axis, [(i, (i + step) % count) for i in range(count)])  13 us
    pallas_call x4, Pallas kernels, call(): vmem_call(kernel, out_shape, in_specs=specs, scratch_shapes=[pltpu.VMEM(s...  9.89 us
    ppermute x8, waiting for transfers between devices, shifted(): lax.ppermute(value, axis, [(i, (i + step) % count) for i in range(count)])  8.53 us
    pallas_call x1, Pallas kernels, local(): vmem_call(flux_kernel, [(nx, ny, nz), (3, nx, ny, nz), (nx, ny, nz), (spe...  6.06 us
    all_to_all x1, waiting for transfers between devices, local(): lax.all_to_all(spectral.reshape(groups, kz, main), ('hy', 'ga'), split_ax...  6 us
    all_to_all x1, starting transfers between devices, local(): lax.all_to_all(spectral.reshape(groups, kz, main), ('hy', 'ga'), split_ax...  5.2 us
    pallas_call x1, Pallas kernels, local(): vmem_call(pack_kernel, [(nx, ny, nz)] + [(prim_n, ny, nz)] * 2 + [(prim_n...  4.49 us
    all_to_all x1, starting transfers between devices, local(): lax.all_to_all(planes, ('hy', 'ga'), split_axis=0, concat_axis=0, tiled=T...  3.45 us
  transfers between devices with their start and end apart: 10, of which 8 were waited for; matrix products, arithmetic and copies ran while one was open for 0% of the time, Pallas kernels for 18%

profile of v2, /device:TPU:0, one launch (start us, length us, event | category | flops | bytes accessed | tf_op | source)
XLA Modules:
  0.0 60.0 jit_solution(8303599416731623208)
XLA Ops:
  0.6 2.1 %shard_map.139 = f32[256,256]{1,0:T(8,128)} custom-call(s32[1]{0:T(128)} %bitcast.part, f32[8,32,128]{2,1,0:T(8,128)} %den.7, f32[2,256,128]{2,1,0:T(8,128)} %constant.20.clone.table), custom_call_target="tpu_custom_call" | custom-call | tf_op jit(solution)/shard_map/pallas_call | solution.py:399
  2.7 5.2 %all-to-all-start = ((f32[8,32,256]{2,1,0:T(8,128)}), f32[8,32,256]{2,1,0:T(8,128)S(1)}, u32[]{:S(2)}, u32[]{:S(2)}) async-start(f32[8,32,256]{2,1,0:T(8,128)} %bitcast.3), calls=%async_computation | async-start | bytes 524288 | tf_op jit(solution)/shard_map/all_to_all | solution.py:405
  7.9 6.0 %all-to-all-done.lines = f32[8,32,256]{2,1,0:T(8,128)S(1)} async-done(((f32[8,32,256]{2,1,0:T(8,128)}), f32[8,32,256]{2,1,0:T(8,128)S(1)}, u32[]{:S(2)}, u32[]{:S(2)}) %all-to-all-start) | async-done | bytes 262176 | tf_op jit(solution)/shard_map/all_to_all | solution.py:405
  13.9 0.0 copy-start.1
  13.9 0.7 %copy-done.1 = f32[8,32,256]{2,1,0:T(8,128)} copy-done((f32[8,32,256]{2,1,0:T(8,128)}, f32[8,32,256]{2,1,0:T(8,128)S(1)}, u32[]{:S(2)}) %copy-start.1) | copy-done | bytes 262168
  14.6 2.1 %shard_map.140 = (f32[8,32,128]{2,1,0:T(8,128)}, f32[72,128]{1,0:T(8,128)}) custom-call(s32[1]{0:T(128)} %bitcast.1.parts, f32[8,32,256]{2,1,0:T(8,128)} %copy-done.1, f32[128,128]{1,0:T(8,128)} %constant.22.clone.table_y.rest_3_, f32[3,256,128]{2,1,0:T(8,128)} %constant.23.clone.tables.rest_4_), custom_call_target="tpu_custom_call" | custom-call | tf_op jit(solution)/shard_map/pallas_call | solution.py:399
  16.8 1.6 %collective-permute-start.5 = (f32[72,128]{1,0:T(8,128)}, f32[72,128]{1,0:T(8,128)S(1)}, u32[]{:S(2)}, u32[]{:S(2)}) collective-permute-start(f32[72,128]{1,0:T(8,128)} %get-tuple-element.28.own), channel_id=1, source_target_pairs={{0,8},{8,16},{16,24},{24,0},{1,9},{9,17},{17,25},{25,1},{2,10},{10... | collective-permute-start | bytes 110600 | tf_op jit(solution)/shard_map/ppermute | solution.py:178
  18.4 2.6 %collective-permute-start.6 = (f32[72,128]{1,0:T(8,128)}, f32[72,128]{1,0:T(8,128)S(1)}, u32[]{:S(2)}, u32[]{:S(2)}) collective-permute-start(f32[72,128]{1,0:T(8,128)} %get-tuple-element.28.own), channel_id=1, source_target_pairs={{0,16},{8,24},{16,0},{24,8},{1,17},{9,25},{17,1},{25,9},{2,18},{10... | collective-permute-start | bytes 110600 | tf_op jit(solution)/shard_map/ppermute | solution.py:178
  21.0 1.3 %collective-permute-start.7 = (f32[72,128]{1,0:T(8,128)}, f32[72,128]{1,0:T(8,128)S(1)}, u32[]{:S(2)}, u32[]{:S(2)}) collective-permute-start(f32[72,128]{1,0:T(8,128)} %get-tuple-element.28.own), channel_id=1, source_target_pairs={{0,24},{8,0},{16,8},{24,16},{1,25},{9,1},{17,9},{25,17},{2,26},{10... | collective-permute-start | bytes 110600 | tf_op jit(solution)/shard_map/ppermute | solution.py:178
  22.3 0.5 collective-permute-done.5.rest_0_
  22.8 0.0 copy-start.7
  22.8 1.3 %collective-permute-done.6.rest_1_ = f32[72,128]{1,0:T(8,128)S(1)} collective-permute-done((f32[72,128]{1,0:T(8,128)}, f32[72,128]{1,0:T(8,128)S(1)}, u32[]{:S(2)}, u32[]{:S(2)}) %collective-permute-start.6) | collective-permute-done | bytes 36896 | tf_op jit(solution)/shard_map/ppermute | solution.py:178
  24.1 0.0 copy-start.8
  24.1 1.0 %collective-permute-done.7.rest_2_ = f32[72,128]{1,0:T(8,128)S(1)} collective-permute-done((f32[72,128]{1,0:T(8,128)}, f32[72,128]{1,0:T(8,128)S(1)}, u32[]{:S(2)}, u32[]{:S(2)}) %collective-permute-start.7) | collective-permute-done | bytes 36896 | tf_op jit(solution)/shard_map/ppermute | solution.py:178
  25.1 0.0 copy-start.9
  25.1 0.0 copy-done.7
  25.1 0.0 copy-done.8
  25.1 0.6 copy-done.9
  25.7 2.8 %shard_map.141 = f32[8,32,384]{2,1,0:T(8,128)} custom-call(s32[1]{0:T(128)} %bitcast.1.parts, f32[8,32,128]{2,1,0:T(8,128)} %get-tuple-element.27.modes, f32[72,128]{1,0:T(8,128)} %get-tuple-element.28.own, f32[72,128]{1,0:T(8,128)} %copy-done.7, f32[72,128]{1,0:T(8,128)} %copy-done.8, f32[72,128]{1,0:T(8,128)} %copy-done.9, ...), custom_call_target="tpu_custom_call" | custom-call | tf_op jit(solution)/shard_map/pallas_call | solution.py:399
  28.5 3.5 %all-to-all-start.1 = ((f32[8,32,384]{2,1,0:T(8,128)}), f32[8,32,384]{2,1,0:T(8,128)S(1)}, u32[]{:S(2)}, u32[]{:S(2)}) async-start(f32[8,32,384]{2,1,0:T(8,128)} %shard_map.141), calls=%async_computation.1 | async-start | bytes 786432 | tf_op jit(solution)/shard_map/all_to_all | solution.py:431
  32.0 4.5 %shard_map.137 = (f32[8,32,128]{2,1,0:T(8,128)}, f32[14,32,128]{2,1,0:T(8,128)}, f32[14,32,128]{2,1,0:T(8,128)}, f32[14,8,128]{2,1,0:T(8,128)}, f32[14,8,128]{2,1,0:T(8,128)}, /*index=5*/f32[8,32,128]{2,1,0:T(8,128)}) custom-call(f32[8,32,128]{2,1,0:T(8,128)} %den.7, f32[3,8,32,128]{3,2,1,0:T(8,128)} %vel.5, f32[8,32,128]{2,1,0:T(8,128)} %pre.1, ...), custom_call_target="tpu_custom_call" | custom-call | tf_op jit(solution)/shard_map/pallas_call | solution.py:409
  36.5 0.5 collective-permute-start
  36.9 3.4 %collective-permute-start.1 = (f32[14,32,128]{2,1,0:T(8,128)}, f32[14,32,128]{2,1,0:T(8,128)S(1)}, u32[]{:S(2)}, u32[]{:S(2)}) collective-permute-start(f32[14,32,128]{2,1,0:T(8,128)} %get-tuple-element.22), channel_id=1, source_target_pairs={{0,24},{8,0},{16,8},{24,16},{1,25},{9,1},{17,9},{25,17},{2,26},{10... | collective-permute-start | bytes 688136 | tf_op jit(solution)/shard_map/ppermute | solution.py:178
  40.3 1.9 %collective-permute-start.4 = (f32[8,32,128]{2,1,0:T(8,128)}, f32[8,32,128]{2,1,0:T(8,128)S(1)}, u32[]{:S(2)}, u32[]{:S(2)}) collective-permute-start(f32[8,32,128]{2,1,0:T(8,128)} %get-tuple-element.25), channel_id=1, source_target_pairs={{0,1},{1,0},{2,3},{3,2},{4,5},{5,4},{6,7},{7,6},{8,9},{9,8},{10,11... | collective-permute-start | bytes 393224 | tf_op jit(solution)/shard_map/ppermute | solution.py:178
  42.2 0.0 collective-permute-start.2
  42.2 1.7 %collective-permute-start.3 = (f32[14,8,128]{2,1,0:T(8,128)}, f32[14,8,128]{2,1,0:T(8,128)S(1)}, u32[]{:S(2)}, u32[]{:S(2)}) collective-permute-start(f32[14,8,128]{2,1,0:T(8,128)} %get-tuple-element.24), channel_id=1, source_target_pairs={{0,6},{2,0},{4,2},{6,4},{1,7},{3,1},{5,3},{7,5},{8,14},{10,8},{12,... | collective-permute-start | bytes 172040 | tf_op jit(solution)/shard_map/ppermute | solution.py:178
  44.0 2.1 %collective-permute-done.2.ybelow = f32[14,8,128]{2,1,0:T(8,128)S(1)} collective-permute-done((f32[14,8,128]{2,1,0:T(8,128)}, f32[14,8,128]{2,1,0:T(8,128)S(1)}, u32[]{:S(2)}, u32[]{:S(2)}) %collective-permute-start.2) | collective-permute-done | bytes 57376 | tf_op jit(solution)/shard_map/ppermute | solution.py:178
  46.0 0.0 copy-start.5
  46.0 0.1 collective-permute-done.3.yabove
  46.1 0.0 copy-start.6
  46.1 0.0 collective-permute-done.4.zbelow.zabove
  46.1 0.0 copy-start.2
  46.1 0.9 %collective-permute-done.xbelow = f32[14,32,128]{2,1,0:T(8,128)S(1)} collective-permute-done((f32[14,32,128]{2,1,0:T(8,128)}, f32[14,32,128]{2,1,0:T(8,128)S(1)}, u32[]{:S(2)}, u32[]{:S(2)}) %collective-permute-start) | collective-permute-done | bytes 229408 | tf_op jit(solution)/shard_map/ppermute | solution.py:178
  47.0 0.0 copy-start.3
  47.0 2.7 %collective-permute-done.1.xabove = f32[14,32,128]{2,1,0:T(8,128)S(1)} collective-permute-done((f32[14,32,128]{2,1,0:T(8,128)}, f32[14,32,128]{2,1,0:T(8,128)S(1)}, u32[]{:S(2)}, u32[]{:S(2)}) %collective-permute-start.1) | collective-permute-done | bytes 229408 | tf_op jit(solution)/shard_map/ppermute | solution.py:178
  49.7 0.0 copy-start.4
  49.7 0.0 copy-done.5
  49.7 0.0 copy-done.6
  49.7 0.0 copy-done.2
  49.7 0.0 copy-done.3
  49.7 0.7 %copy-done.4 = f32[14,32,128]{2,1,0:T(8,128)} copy-done((f32[14,32,128]{2,1,0:T(8,128)}, f32[14,32,128]{2,1,0:T(8,128)S(1)}, u32[]{:S(2)}) %copy-start.4) | copy-done | bytes 229400
  50.4 6.1 %shard_map.138 = (f32[8,32,128]{2,1,0:T(8,128)}, f32[3,8,32,128]{3,2,1,0:T(8,128)}, f32[8,32,128]{2,1,0:T(8,128)}, f32[9,8,32,128]{3,2,1,0:T(8,128)}) custom-call(f32[8,32,128]{2,1,0:T(8,128)} %den.7, f32[3,8,32,128]{3,2,1,0:T(8,128)} %vel.5, f32[8,32,128]{2,1,0:T(8,128)} %get-tuple-element.20.cooled, f32[9,8,32,128]{3,2,1,0:T(8,128)} %spe.3, ...), custom_call_target="tpu_custom_call" | custom-call | tf_op jit(solution)/shard_map/pallas_call | solution.py:433
  56.4 0.0 all-to-all-done.1.planes
  56.5 0.0 copy-start
  56.5 0.7 %copy-done = f32[8,32,384]{2,1,0:T(8,128)} copy-done((f32[8,32,384]{2,1,0:T(8,128)}, f32[8,32,384]{2,1,0:T(8,128)S(1)}, u32[]{:S(2)}) %copy-start) | copy-done | bytes 393240
  57.2 2.9 %shard_map.142 = (f32[8,32,128]{2,1,0:T(8,128)}, f32[3,8,32,128]{3,2,1,0:T(8,128)}, f32[8,32,128]{2,1,0:T(8,128)}) custom-call(s32[1]{0:T(128)} %bitcast.part, f32[8,32,384]{2,1,0:T(8,128)} %copy-done, f32[2,256,256]{2,1,0:T(8,128)} %constant.21.clone.table, f32[8,32,128]{2,1,0:T(8,128)} %den.7, f32[3,8,32,128]{3,2,1,0:T(8,128)} %vel.5, ...), custom_call_target="tpu_custom_call" | custom-call | tf_op jit(solution)/shard_map/pallas_call | solution.py:399
Async XLA Ops:
  2.7 11.2 %all-to-all-start = ((f32[8,32,256]{2,1,0:T(8,128)}), f32[8,32,256]{2,1,0:T(8,128)S(1)}, u32[]{:S(2)}, u32[]{:S(2)}) async-start(f32[8,32,256]{2,1,0:T(8,128)} %bitcast.3), calls=%async_computation | async-start | bytes 524288 | tf_op jit(solution)/shard_map/all_to_all | solution.py:405
  13.9 0.7 %copy-start.1 = (f32[8,32,256]{2,1,0:T(8,128)}, f32[8,32,256]{2,1,0:T(8,128)S(1)}, u32[]{:S(2)}) copy-start(f32[8,32,256]{2,1,0:T(8,128)S(1)} %all-to-all-done.lines) | copy-start | bytes 786436
  16.8 6.0 %collective-permute-start.5 = (f32[72,128]{1,0:T(8,128)}, f32[72,128]{1,0:T(8,128)S(1)}, u32[]{:S(2)}, u32[]{:S(2)}) collective-permute-start(f32[72,128]{1,0:T(8,128)} %get-tuple-element.28.own), channel_id=1, source_target_pairs={{0,8},{8,16},{16,24},{24,0},{1,9},{9,17},{17,25},{25,1},{2,10},{10... | collective-permute-start | bytes 110600 | tf_op jit(solution)/shard_map/ppermute | solution.py:178
  18.4 5.7 %collective-permute-start.6 = (f32[72,128]{1,0:T(8,128)}, f32[72,128]{1,0:T(8,128)S(1)}, u32[]{:S(2)}, u32[]{:S(2)}) collective-permute-start(f32[72,128]{1,0:T(8,128)} %get-tuple-element.28.own), channel_id=1, source_target_pairs={{0,16},{8,24},{16,0},{24,8},{1,17},{9,25},{17,1},{25,9},{2,18},{10... | collective-permute-start | bytes 110600 | tf_op jit(solution)/shard_map/ppermute | solution.py:178
  21.0 4.2 %collective-permute-start.7 = (f32[72,128]{1,0:T(8,128)}, f32[72,128]{1,0:T(8,128)S(1)}, u32[]{:S(2)}, u32[]{:S(2)}) collective-permute-start(f32[72,128]{1,0:T(8,128)} %get-tuple-element.28.own), channel_id=1, source_target_pairs={{0,24},{8,0},{16,8},{24,16},{1,25},{9,1},{17,9},{25,17},{2,26},{10... | collective-permute-start | bytes 110600 | tf_op jit(solution)/shard_map/ppermute | solution.py:178
  22.8 2.4 %copy-start.7 = (f32[72,128]{1,0:T(8,128)}, f32[72,128]{1,0:T(8,128)S(1)}, u32[]{:S(2)}) copy-start(f32[72,128]{1,0:T(8,128)S(1)} %collective-permute-done.5.rest_0_) | copy-start | bytes 110596
  24.1 1.0 %copy-start.8 = (f32[72,128]{1,0:T(8,128)}, f32[72,128]{1,0:T(8,128)S(1)}, u32[]{:S(2)}) copy-start(f32[72,128]{1,0:T(8,128)S(1)} %collective-permute-done.6.rest_1_) | copy-start | bytes 110596
  25.1 0.6 %copy-start.9 = (f32[72,128]{1,0:T(8,128)}, f32[72,128]{1,0:T(8,128)S(1)}, u32[]{:S(2)}) copy-start(f32[72,128]{1,0:T(8,128)S(1)} %collective-permute-done.7.rest_2_) | copy-start | bytes 110596
  28.5 27.9 %all-to-all-start.1 = ((f32[8,32,384]{2,1,0:T(8,128)}), f32[8,32,384]{2,1,0:T(8,128)S(1)}, u32[]{:S(2)}, u32[]{:S(2)}) async-start(f32[8,32,384]{2,1,0:T(8,128)} %shard_map.141), calls=%async_computation.1 | async-start | bytes 786432 | tf_op jit(solution)/shard_map/all_to_all | solution.py:431
  36.5 10.5 %collective-permute-start = (f32[14,32,128]{2,1,0:T(8,128)}, f32[14,32,128]{2,1,0:T(8,128)S(1)}, u32[]{:S(2)}, u32[]{:S(2)}) collective-permute-start(f32[14,32,128]{2,1,0:T(8,128)} %get-tuple-element.21), channel_id=1, source_target_pairs={{0,8},{8,16},{16,24},{24,0},{1,9},{9,17},{17,25},{25,1},{2,10},{10... | collective-permute-start | bytes 688136 | tf_op jit(solution)/shard_map/ppermute | solution.py:178
  36.9 12.8 %collective-permute-start.1 = (f32[14,32,128]{2,1,0:T(8,128)}, f32[14,32,128]{2,1,0:T(8,128)S(1)}, u32[]{:S(2)}, u32[]{:S(2)}) collective-permute-start(f32[14,32,128]{2,1,0:T(8,128)} %get-tuple-element.22), channel_id=1, source_target_pairs={{0,24},{8,0},{16,8},{24,16},{1,25},{9,1},{17,9},{25,17},{2,26},{10... | collective-permute-start | bytes 688136 | tf_op jit(solution)/shard_map/ppermute | solution.py:178
  40.3 5.8 %collective-permute-start.4 = (f32[8,32,128]{2,1,0:T(8,128)}, f32[8,32,128]{2,1,0:T(8,128)S(1)}, u32[]{:S(2)}, u32[]{:S(2)}) collective-permute-start(f32[8,32,128]{2,1,0:T(8,128)} %get-tuple-element.25), channel_id=1, source_target_pairs={{0,1},{1,0},{2,3},{3,2},{4,5},{5,4},{6,7},{7,6},{8,9},{9,8},{10,11... | collective-permute-start | bytes 393224 | tf_op jit(solution)/shard_map/ppermute | solution.py:178
  42.2 3.8 %collective-permute-start.2 = (f32[14,8,128]{2,1,0:T(8,128)}, f32[14,8,128]{2,1,0:T(8,128)S(1)}, u32[]{:S(2)}, u32[]{:S(2)}) collective-permute-start(f32[14,8,128]{2,1,0:T(8,128)} %get-tuple-element.23), channel_id=1, source_target_pairs={{0,2},{2,4},{4,6},{6,0},{1,3},{3,5},{5,7},{7,1},{8,10},{10,12},{12... | collective-permute-start | bytes 172040 | tf_op jit(solution)/shard_map/ppermute | solution.py:178
  42.2 3.9 %collective-permute-start.3 = (f32[14,8,128]{2,1,0:T(8,128)}, f32[14,8,128]{2,1,0:T(8,128)S(1)}, u32[]{:S(2)}, u32[]{:S(2)}) collective-permute-start(f32[14,8,128]{2,1,0:T(8,128)} %get-tuple-element.24), channel_id=1, source_target_pairs={{0,6},{2,0},{4,2},{6,4},{1,7},{3,1},{5,3},{7,5},{8,14},{10,8},{12,... | collective-permute-start | bytes 172040 | tf_op jit(solution)/shard_map/ppermute | solution.py:178
  46.0 3.7 %copy-start.5 = (f32[14,8,128]{2,1,0:T(8,128)}, f32[14,8,128]{2,1,0:T(8,128)S(1)}, u32[]{:S(2)}) copy-start(f32[14,8,128]{2,1,0:T(8,128)S(1)} %collective-permute-done.2.ybelow) | copy-start | bytes 172036
  46.1 3.6 %copy-start.6 = (f32[14,8,128]{2,1,0:T(8,128)}, f32[14,8,128]{2,1,0:T(8,128)S(1)}, u32[]{:S(2)}) copy-start(f32[14,8,128]{2,1,0:T(8,128)S(1)} %collective-permute-done.3.yabove) | copy-start | bytes 172036
  46.1 3.6 %copy-start.2 = (f32[8,32,128]{2,1,0:T(8,128)}, f32[8,32,128]{2,1,0:T(8,128)S(1)}, u32[]{:S(2)}) copy-start(f32[8,32,128]{2,1,0:T(8,128)S(1)} %collective-permute-done.4.zbelow.zabove) | copy-start | bytes 393220
  47.0 2.7 %copy-start.3 = (f32[14,32,128]{2,1,0:T(8,128)}, f32[14,32,128]{2,1,0:T(8,128)S(1)}, u32[]{:S(2)}) copy-start(f32[14,32,128]{2,1,0:T(8,128)S(1)} %collective-permute-done.xbelow) | copy-start | bytes 688132
  49.7 0.7 %copy-start.4 = (f32[14,32,128]{2,1,0:T(8,128)}, f32[14,32,128]{2,1,0:T(8,128)S(1)}, u32[]{:S(2)}) copy-start(f32[14,32,128]{2,1,0:T(8,128)S(1)} %collective-permute-done.1.xabove) | copy-start | bytes 688132
  56.5 0.7 %copy-start = (f32[8,32,384]{2,1,0:T(8,128)}, f32[8,32,384]{2,1,0:T(8,128)S(1)}, u32[]{:S(2)}) copy-start(f32[8,32,384]{2,1,0:T(8,128)S(1)} %all-to-all-done.1.planes) | copy-start | bytes 1179652

commit v3 on v2

--- a/solution.py
+++ b/solution.py
@@ -8,6 +8,7 @@
 from jax.experimental import pallas as pl
 from jax.experimental.pallas import tpu as pltpu
 from jax.sharding import PartitionSpec as P
+
 
 NEWTON = 4
 gamma_gas = 5.0 / 3.0
@@ -95,7 +96,7 @@
     row = lax.broadcasted_iota(jnp.int32, (ny, nz), 0)
     lane = lax.broadcasted_iota(jnp.int32, (ny, nz), 1)
 
-    for side, (at, face) in enumerate(((0, xbelow), (nx + 1, xabove))):
+    for at, face in ((0, xbelow), (nx + 1, xabove)):
         for f, value in enumerate(fields_of([face[c] for c in range(prim_n)])):
             ext[f, at] = value
     for side, face in enumerate((ybelow, yabove)):
@@ -223,7 +224,7 @@
 
 
 def along_y_kernel(size_g, block, parts, lines, table_y, tables, modes, sums, grid_rows):
-    groups, kz, _ = lines.shape
+    _, kz, _ = lines.shape
     nx, _, ny = modes.shape
     width = block
     per = LANES // width
@@ -366,7 +367,7 @@
         energy[x] = work
 
 
-def local(density, velocity, pressure, species, newton_count):
+def step(density, velocity, pressure, species, newton_count):
     size_x, size_y, size_g = (lax.axis_size(a) for a in ("hx", "hy", "ga"))
     nx, ny, nz = density.shape
     all_x, all_y, all_z = nx * size_x, ny * size_y, nz * size_g
@@ -410,8 +411,10 @@
         pack_kernel,
         [(nx, ny, nz)] + [(prim_n, ny, nz)] * 2 + [(prim_n, nx, nz)] * 2 + [(nx, ny, LANES)],
     )(density, velocity, pressure, species, newton_count)
-    xbelow, xabove = shifted(xhi, "hx", 1), shifted(xlo, "hx", -1)
-    ybelow, yabove = shifted(yhi, "hy", 1), shifted(ylo, "hy", -1)
+    xbelow = shifted(xhi, "hx", 1)
+    xabove = shifted(xlo, "hx", -1)
+    ybelow = shifted(yhi, "hy", 1)
+    yabove = shifted(ylo, "hy", -1)
     zbelow = shifted(zface, "ga", 1)
     zabove = zbelow if size_g == 2 else shifted(zface, "ga", -1)
 
@@ -452,7 +455,7 @@
     cells = P("hx", "hy", "ga")
     fields = P(None, "hx", "hy", "ga")
     return jax.shard_map(
-        local,
+        step,
         mesh=mesh,
         in_specs=(cells, fields, cells, fields, cells),
         out_specs=(cells, fields, cells, fields, cells),

time: 60.5 us -> 60.5 us (level)
  no operation moved by 1% of the time
where the time goes in v3:
time: 60.5 us; the launch traced here: 60 us
  starting transfers between devices  21.6 us (36%)
  Pallas kernels  20.4 us (34%)
  waiting for transfers between devices  14.5 us (24%)
  local copies, waits for them, and re-layouts  2.73 us (5%)
  between operations  0.68 us (1%)
    ppermute x8, starting transfers between devices, shifted(): lax.ppermute(value, axis, [(i, (i + step) % count) for i in range(count)])  13 us
    pallas_call x4, Pallas kernels, call(): vmem_call(kernel, out_shape, in_specs=specs, scratch_shapes=[pltpu.VMEM(s...  9.89 us
    ppermute x8, waiting for transfers between devices, shifted(): lax.ppermute(value, axis, [(i, (i + step) % count) for i in range(count)])  8.53 us
    pallas_call x1, Pallas kernels, step(): vmem_call(flux_kernel, [(nx, ny, nz), (3, nx, ny, nz), (nx, ny, nz), (spe...  6.06 us
    all_to_all x1, waiting for transfers between devices, step(): lax.all_to_all(spectral.reshape(groups, kz, main), ('hy', 'ga'), split_ax...  6 us
    all_to_all x1, starting transfers between devices, step(): lax.all_to_all(spectral.reshape(groups, kz, main), ('hy', 'ga'), split_ax...  5.2 us
    pallas_call x1, Pallas kernels, step(): vmem_call(pack_kernel, [(nx, ny, nz)] + [(prim_n, ny, nz)] * 2 + [(prim_n...  4.49 us
    all_to_all x1, starting transfers between devices, step(): lax.all_to_all(planes, ('hy', 'ga'), split_axis=0, concat_axis=0, tiled=T...  3.45 us
  transfers between devices with their start and end apart: 10, of which 8 were waited for; matrix products, arithmetic and copies ran while one was open for 0% of the time, Pallas kernels for 18%

profile of v3, /device:TPU:0, one launch (start us, length us, event | category | flops | bytes accessed | tf_op | source)
XLA Modules:
  0.0 60.0 jit_solution(8303599416731623208)
XLA Ops:
  0.6 2.1 %shard_map.139 = f32[256,256]{1,0:T(8,128)} custom-call(s32[1]{0:T(128)} %bitcast.part, f32[8,32,128]{2,1,0:T(8,128)} %den.7, f32[2,256,128]{2,1,0:T(8,128)} %constant.20.clone.table), custom_call_target="tpu_custom_call" | custom-call | tf_op jit(solution)/shard_map/pallas_call | solution.py:400
  2.7 5.2 %all-to-all-start = ((f32[8,32,256]{2,1,0:T(8,128)}), f32[8,32,256]{2,1,0:T(8,128)S(1)}, u32[]{:S(2)}, u32[]{:S(2)}) async-start(f32[8,32,256]{2,1,0:T(8,128)} %bitcast.3), calls=%async_computation | async-start | bytes 524288 | tf_op jit(solution)/shard_map/all_to_all | solution.py:406
  7.9 6.0 %all-to-all-done.lines = f32[8,32,256]{2,1,0:T(8,128)S(1)} async-done(((f32[8,32,256]{2,1,0:T(8,128)}), f32[8,32,256]{2,1,0:T(8,128)S(1)}, u32[]{:S(2)}, u32[]{:S(2)}) %all-to-all-start) | async-done | bytes 262176 | tf_op jit(solution)/shard_map/all_to_all | solution.py:406
  13.9 0.0 copy-start.1
  13.9 0.7 %copy-done.1 = f32[8,32,256]{2,1,0:T(8,128)} copy-done((f32[8,32,256]{2,1,0:T(8,128)}, f32[8,32,256]{2,1,0:T(8,128)S(1)}, u32[]{:S(2)}) %copy-start.1) | copy-done | bytes 262168
  14.6 2.1 %shard_map.140 = (f32[8,32,128]{2,1,0:T(8,128)}, f32[72,128]{1,0:T(8,128)}) custom-call(s32[1]{0:T(128)} %bitcast.1.parts, f32[8,32,256]{2,1,0:T(8,128)} %copy-done.1, f32[128,128]{1,0:T(8,128)} %constant.22.clone.table_y.rest_3_, f32[3,256,128]{2,1,0:T(8,128)} %constant.23.clone.tables.rest_4_), custom_call_target="tpu_custom_call" | custom-call | tf_op jit(solution)/shard_map/pallas_call | solution.py:400
  16.8 1.6 %collective-permute-start.5 = (f32[72,128]{1,0:T(8,128)}, f32[72,128]{1,0:T(8,128)S(1)}, u32[]{:S(2)}, u32[]{:S(2)}) collective-permute-start(f32[72,128]{1,0:T(8,128)} %get-tuple-element.28.own), channel_id=1, source_target_pairs={{0,8},{8,16},{16,24},{24,0},{1,9},{9,17},{17,25},{25,1},{2,10},{10... | collective-permute-start | bytes 110600 | tf_op jit(solution)/shard_map/ppermute | solution.py:179
  18.4 2.6 %collective-permute-start.6 = (f32[72,128]{1,0:T(8,128)}, f32[72,128]{1,0:T(8,128)S(1)}, u32[]{:S(2)}, u32[]{:S(2)}) collective-permute-start(f32[72,128]{1,0:T(8,128)} %get-tuple-element.28.own), channel_id=1, source_target_pairs={{0,16},{8,24},{16,0},{24,8},{1,17},{9,25},{17,1},{25,9},{2,18},{10... | collective-permute-start | bytes 110600 | tf_op jit(solution)/shard_map/ppermute | solution.py:179
  21.0 1.3 %collective-permute-start.7 = (f32[72,128]{1,0:T(8,128)}, f32[72,128]{1,0:T(8,128)S(1)}, u32[]{:S(2)}, u32[]{:S(2)}) collective-permute-start(f32[72,128]{1,0:T(8,128)} %get-tuple-element.28.own), channel_id=1, source_target_pairs={{0,24},{8,0},{16,8},{24,16},{1,25},{9,1},{17,9},{25,17},{2,26},{10... | collective-permute-start | bytes 110600 | tf_op jit(solution)/shard_map/ppermute | solution.py:179
  22.3 0.5 collective-permute-done.5.rest_0_
  22.8 0.0 copy-start.7
  22.8 1.3 %collective-permute-done.6.rest_1_ = f32[72,128]{1,0:T(8,128)S(1)} collective-permute-done((f32[72,128]{1,0:T(8,128)}, f32[72,128]{1,0:T(8,128)S(1)}, u32[]{:S(2)}, u32[]{:S(2)}) %collective-permute-start.6) | collective-permute-done | bytes 36896 | tf_op jit(solution)/shard_map/ppermute | solution.py:179
  24.1 0.0 copy-start.8
  24.1 1.0 %collective-permute-done.7.rest_2_ = f32[72,128]{1,0:T(8,128)S(1)} collective-permute-done((f32[72,128]{1,0:T(8,128)}, f32[72,128]{1,0:T(8,128)S(1)}, u32[]{:S(2)}, u32[]{:S(2)}) %collective-permute-start.7) | collective-permute-done | bytes 36896 | tf_op jit(solution)/shard_map/ppermute | solution.py:179
  25.1 0.0 copy-start.9
  25.1 0.0 copy-done.7
  25.1 0.0 copy-done.8
  25.1 0.6 copy-done.9
  25.7 2.8 %shard_map.141 = f32[8,32,384]{2,1,0:T(8,128)} custom-call(s32[1]{0:T(128)} %bitcast.1.parts, f32[8,32,128]{2,1,0:T(8,128)} %get-tuple-element.27.modes, f32[72,128]{1,0:T(8,128)} %get-tuple-element.28.own, f32[72,128]{1,0:T(8,128)} %copy-done.7, f32[72,128]{1,0:T(8,128)} %copy-done.8, f32[72,128]{1,0:T(8,128)} %copy-done.9, ...), custom_call_target="tpu_custom_call" | custom-call | tf_op jit(solution)/shard_map/pallas_call | solution.py:400
  28.5 3.5 %all-to-all-start.1 = ((f32[8,32,384]{2,1,0:T(8,128)}), f32[8,32,384]{2,1,0:T(8,128)S(1)}, u32[]{:S(2)}, u32[]{:S(2)}) async-start(f32[8,32,384]{2,1,0:T(8,128)} %shard_map.141), calls=%async_computation.1 | async-start | bytes 786432 | tf_op jit(solution)/shard_map/all_to_all | solution.py:434
  32.0 4.5 %shard_map.137 = (f32[8,32,128]{2,1,0:T(8,128)}, f32[14,32,128]{2,1,0:T(8,128)}, f32[14,32,128]{2,1,0:T(8,128)}, f32[14,8,128]{2,1,0:T(8,128)}, f32[14,8,128]{2,1,0:T(8,128)}, /*index=5*/f32[8,32,128]{2,1,0:T(8,128)}) custom-call(f32[8,32,128]{2,1,0:T(8,128)} %den.7, f32[3,8,32,128]{3,2,1,0:T(8,128)} %vel.5, f32[8,32,128]{2,1,0:T(8,128)} %pre.1, ...), custom_call_target="tpu_custom_call" | custom-call | tf_op jit(solution)/shard_map/pallas_call | solution.py:410
  36.5 0.5 collective-permute-start
  36.9 3.4 %collective-permute-start.1 = (f32[14,32,128]{2,1,0:T(8,128)}, f32[14,32,128]{2,1,0:T(8,128)S(1)}, u32[]{:S(2)}, u32[]{:S(2)}) collective-permute-start(f32[14,32,128]{2,1,0:T(8,128)} %get-tuple-element.22), channel_id=1, source_target_pairs={{0,24},{8,0},{16,8},{24,16},{1,25},{9,1},{17,9},{25,17},{2,26},{10... | collective-permute-start | bytes 688136 | tf_op jit(solution)/shard_map/ppermute | solution.py:179
  40.3 1.9 %collective-permute-start.4 = (f32[8,32,128]{2,1,0:T(8,128)}, f32[8,32,128]{2,1,0:T(8,128)S(1)}, u32[]{:S(2)}, u32[]{:S(2)}) collective-permute-start(f32[8,32,128]{2,1,0:T(8,128)} %get-tuple-element.25), channel_id=1, source_target_pairs={{0,1},{1,0},{2,3},{3,2},{4,5},{5,4},{6,7},{7,6},{8,9},{9,8},{10,11... | collective-permute-start | bytes 393224 | tf_op jit(solution)/shard_map/ppermute | solution.py:179
  42.2 0.0 collective-permute-start.2
  42.2 1.7 %collective-permute-start.3 = (f32[14,8,128]{2,1,0:T(8,128)}, f32[14,8,128]{2,1,0:T(8,128)S(1)}, u32[]{:S(2)}, u32[]{:S(2)}) collective-permute-start(f32[14,8,128]{2,1,0:T(8,128)} %get-tuple-element.24), channel_id=1, source_target_pairs={{0,6},{2,0},{4,2},{6,4},{1,7},{3,1},{5,3},{7,5},{8,14},{10,8},{12,... | collective-permute-start | bytes 172040 | tf_op jit(solution)/shard_map/ppermute | solution.py:179
  44.0 2.1 %collective-permute-done.2.ybelow = f32[14,8,128]{2,1,0:T(8,128)S(1)} collective-permute-done((f32[14,8,128]{2,1,0:T(8,128)}, f32[14,8,128]{2,1,0:T(8,128)S(1)}, u32[]{:S(2)}, u32[]{:S(2)}) %collective-permute-start.2) | collective-permute-done | bytes 57376 | tf_op jit(solution)/shard_map/ppermute | solution.py:179
  46.0 0.0 copy-start.5
  46.0 0.1 collective-permute-done.3.yabove
  46.1 0.0 copy-start.6
  46.1 0.0 collective-permute-done.4.zbelow.zabove
  46.1 0.0 copy-start.2
  46.1 0.9 %collective-permute-done.xbelow = f32[14,32,128]{2,1,0:T(8,128)S(1)} collective-permute-done((f32[14,32,128]{2,1,0:T(8,128)}, f32[14,32,128]{2,1,0:T(8,128)S(1)}, u32[]{:S(2)}, u32[]{:S(2)}) %collective-permute-start) | collective-permute-done | bytes 229408 | tf_op jit(solution)/shard_map/ppermute | solution.py:179
  47.0 0.0 copy-start.3
  47.0 2.7 %collective-permute-done.1.xabove = f32[14,32,128]{2,1,0:T(8,128)S(1)} collective-permute-done((f32[14,32,128]{2,1,0:T(8,128)}, f32[14,32,128]{2,1,0:T(8,128)S(1)}, u32[]{:S(2)}, u32[]{:S(2)}) %collective-permute-start.1) | collective-permute-done | bytes 229408 | tf_op jit(solution)/shard_map/ppermute | solution.py:179
  49.7 0.0 copy-start.4
  49.7 0.0 copy-done.5
  49.7 0.0 copy-done.6
  49.7 0.0 copy-done.2
  49.7 0.0 copy-done.3
  49.7 0.7 %copy-done.4 = f32[14,32,128]{2,1,0:T(8,128)} copy-done((f32[14,32,128]{2,1,0:T(8,128)}, f32[14,32,128]{2,1,0:T(8,128)S(1)}, u32[]{:S(2)}) %copy-start.4) | copy-done | bytes 229400
  50.4 6.1 %shard_map.138 = (f32[8,32,128]{2,1,0:T(8,128)}, f32[3,8,32,128]{3,2,1,0:T(8,128)}, f32[8,32,128]{2,1,0:T(8,128)}, f32[9,8,32,128]{3,2,1,0:T(8,128)}) custom-call(f32[8,32,128]{2,1,0:T(8,128)} %den.7, f32[3,8,32,128]{3,2,1,0:T(8,128)} %vel.5, f32[8,32,128]{2,1,0:T(8,128)} %get-tuple-element.20.cooled, f32[9,8,32,128]{3,2,1,0:T(8,128)} %spe.3, ...), custom_call_target="tpu_custom_call" | custom-call | tf_op jit(solution)/shard_map/pallas_call | solution.py:436
  56.4 0.0 all-to-all-done.1.planes
  56.5 0.0 copy-start
  56.5 0.7 %copy-done = f32[8,32,384]{2,1,0:T(8,128)} copy-done((f32[8,32,384]{2,1,0:T(8,128)}, f32[8,32,384]{2,1,0:T(8,128)S(1)}, u32[]{:S(2)}) %copy-start) | copy-done | bytes 393240
  57.2 2.9 %shard_map.142 = (f32[8,32,128]{2,1,0:T(8,128)}, f32[3,8,32,128]{3,2,1,0:T(8,128)}, f32[8,32,128]{2,1,0:T(8,128)}) custom-call(s32[1]{0:T(128)} %bitcast.part, f32[8,32,384]{2,1,0:T(8,128)} %copy-done, f32[2,256,256]{2,1,0:T(8,128)} %constant.21.clone.table, f32[8,32,128]{2,1,0:T(8,128)} %den.7, f32[3,8,32,128]{3,2,1,0:T(8,128)} %vel.5, ...), custom_call_target="tpu_custom_call" | custom-call | tf_op jit(solution)/shard_map/pallas_call | solution.py:400
Async XLA Ops:
  2.7 11.2 %all-to-all-start = ((f32[8,32,256]{2,1,0:T(8,128)}), f32[8,32,256]{2,1,0:T(8,128)S(1)}, u32[]{:S(2)}, u32[]{:S(2)}) async-start(f32[8,32,256]{2,1,0:T(8,128)} %bitcast.3), calls=%async_computation | async-start | bytes 524288 | tf_op jit(solution)/shard_map/all_to_all | solution.py:406
  13.9 0.7 %copy-start.1 = (f32[8,32,256]{2,1,0:T(8,128)}, f32[8,32,256]{2,1,0:T(8,128)S(1)}, u32[]{:S(2)}) copy-start(f32[8,32,256]{2,1,0:T(8,128)S(1)} %all-to-all-done.lines) | copy-start | bytes 786436
  16.8 6.0 %collective-permute-start.5 = (f32[72,128]{1,0:T(8,128)}, f32[72,128]{1,0:T(8,128)S(1)}, u32[]{:S(2)}, u32[]{:S(2)}) collective-permute-start(f32[72,128]{1,0:T(8,128)} %get-tuple-element.28.own), channel_id=1, source_target_pairs={{0,8},{8,16},{16,24},{24,0},{1,9},{9,17},{17,25},{25,1},{2,10},{10... | collective-permute-start | bytes 110600 | tf_op jit(solution)/shard_map/ppermute | solution.py:179
  18.4 5.7 %collective-permute-start.6 = (f32[72,128]{1,0:T(8,128)}, f32[72,128]{1,0:T(8,128)S(1)}, u32[]{:S(2)}, u32[]{:S(2)}) collective-permute-start(f32[72,128]{1,0:T(8,128)} %get-tuple-element.28.own), channel_id=1, source_target_pairs={{0,16},{8,24},{16,0},{24,8},{1,17},{9,25},{17,1},{25,9},{2,18},{10... | collective-permute-start | bytes 110600 | tf_op jit(solution)/shard_map/ppermute | solution.py:179
  21.0 4.2 %collective-permute-start.7 = (f32[72,128]{1,0:T(8,128)}, f32[72,128]{1,0:T(8,128)S(1)}, u32[]{:S(2)}, u32[]{:S(2)}) collective-permute-start(f32[72,128]{1,0:T(8,128)} %get-tuple-element.28.own), channel_id=1, source_target_pairs={{0,24},{8,0},{16,8},{24,16},{1,25},{9,1},{17,9},{25,17},{2,26},{10... | collective-permute-start | bytes 110600 | tf_op jit(solution)/shard_map/ppermute | solution.py:179
  22.8 2.4 %copy-start.7 = (f32[72,128]{1,0:T(8,128)}, f32[72,128]{1,0:T(8,128)S(1)}, u32[]{:S(2)}) copy-start(f32[72,128]{1,0:T(8,128)S(1)} %collective-permute-done.5.rest_0_) | copy-start | bytes 110596
  24.1 1.0 %copy-start.8 = (f32[72,128]{1,0:T(8,128)}, f32[72,128]{1,0:T(8,128)S(1)}, u32[]{:S(2)}) copy-start(f32[72,128]{1,0:T(8,128)S(1)} %collective-permute-done.6.rest_1_) | copy-start | bytes 110596
  25.1 0.6 %copy-start.9 = (f32[72,128]{1,0:T(8,128)}, f32[72,128]{1,0:T(8,128)S(1)}, u32[]{:S(2)}) copy-start(f32[72,128]{1,0:T(8,128)S(1)} %collective-permute-done.7.rest_2_) | copy-start | bytes 110596
  28.5 27.9 %all-to-all-start.1 = ((f32[8,32,384]{2,1,0:T(8,128)}), f32[8,32,384]{2,1,0:T(8,128)S(1)}, u32[]{:S(2)}, u32[]{:S(2)}) async-start(f32[8,32,384]{2,1,0:T(8,128)} %shard_map.141), calls=%async_computation.1 | async-start | bytes 786432 | tf_op jit(solution)/shard_map/all_to_all | solution.py:434
  36.5 10.5 %collective-permute-start = (f32[14,32,128]{2,1,0:T(8,128)}, f32[14,32,128]{2,1,0:T(8,128)S(1)}, u32[]{:S(2)}, u32[]{:S(2)}) collective-permute-start(f32[14,32,128]{2,1,0:T(8,128)} %get-tuple-element.21), channel_id=1, source_target_pairs={{0,8},{8,16},{16,24},{24,0},{1,9},{9,17},{17,25},{25,1},{2,10},{10... | collective-permute-start | bytes 688136 | tf_op jit(solution)/shard_map/ppermute | solution.py:179
  36.9 12.8 %collective-permute-start.1 = (f32[14,32,128]{2,1,0:T(8,128)}, f32[14,32,128]{2,1,0:T(8,128)S(1)}, u32[]{:S(2)}, u32[]{:S(2)}) collective-permute-start(f32[14,32,128]{2,1,0:T(8,128)} %get-tuple-element.22), channel_id=1, source_target_pairs={{0,24},{8,0},{16,8},{24,16},{1,25},{9,1},{17,9},{25,17},{2,26},{10... | collective-permute-start | bytes 688136 | tf_op jit(solution)/shard_map/ppermute | solution.py:179
  40.3 5.8 %collective-permute-start.4 = (f32[8,32,128]{2,1,0:T(8,128)}, f32[8,32,128]{2,1,0:T(8,128)S(1)}, u32[]{:S(2)}, u32[]{:S(2)}) collective-permute-start(f32[8,32,128]{2,1,0:T(8,128)} %get-tuple-element.25), channel_id=1, source_target_pairs={{0,1},{1,0},{2,3},{3,2},{4,5},{5,4},{6,7},{7,6},{8,9},{9,8},{10,11... | collective-permute-start | bytes 393224 | tf_op jit(solution)/shard_map/ppermute | solution.py:179
  42.2 3.8 %collective-permute-start.2 = (f32[14,8,128]{2,1,0:T(8,128)}, f32[14,8,128]{2,1,0:T(8,128)S(1)}, u32[]{:S(2)}, u32[]{:S(2)}) collective-permute-start(f32[14,8,128]{2,1,0:T(8,128)} %get-tuple-element.23), channel_id=1, source_target_pairs={{0,2},{2,4},{4,6},{6,0},{1,3},{3,5},{5,7},{7,1},{8,10},{10,12},{12... | collective-permute-start | bytes 172040 | tf_op jit(solution)/shard_map/ppermute | solution.py:179
  42.2 3.9 %collective-permute-start.3 = (f32[14,8,128]{2,1,0:T(8,128)}, f32[14,8,128]{2,1,0:T(8,128)S(1)}, u32[]{:S(2)}, u32[]{:S(2)}) collective-permute-start(f32[14,8,128]{2,1,0:T(8,128)} %get-tuple-element.24), channel_id=1, source_target_pairs={{0,6},{2,0},{4,2},{6,4},{1,7},{3,1},{5,3},{7,5},{8,14},{10,8},{12,... | collective-permute-start | bytes 172040 | tf_op jit(solution)/shard_map/ppermute | solution.py:179
  46.0 3.7 %copy-start.5 = (f32[14,8,128]{2,1,0:T(8,128)}, f32[14,8,128]{2,1,0:T(8,128)S(1)}, u32[]{:S(2)}) copy-start(f32[14,8,128]{2,1,0:T(8,128)S(1)} %collective-permute-done.2.ybelow) | copy-start | bytes 172036
  46.1 3.6 %copy-start.6 = (f32[14,8,128]{2,1,0:T(8,128)}, f32[14,8,128]{2,1,0:T(8,128)S(1)}, u32[]{:S(2)}) copy-start(f32[14,8,128]{2,1,0:T(8,128)S(1)} %collective-permute-done.3.yabove) | copy-start | bytes 172036
  46.1 3.6 %copy-start.2 = (f32[8,32,128]{2,1,0:T(8,128)}, f32[8,32,128]{2,1,0:T(8,128)S(1)}, u32[]{:S(2)}) copy-start(f32[8,32,128]{2,1,0:T(8,128)S(1)} %collective-permute-done.4.zbelow.zabove) | copy-start | bytes 393220
  47.0 2.7 %copy-start.3 = (f32[14,32,128]{2,1,0:T(8,128)}, f32[14,32,128]{2,1,0:T(8,128)S(1)}, u32[]{:S(2)}) copy-start(f32[14,32,128]{2,1,0:T(8,128)S(1)} %collective-permute-done.xbelow) | copy-start | bytes 688132
  49.7 0.7 %copy-start.4 = (f32[14,32,128]{2,1,0:T(8,128)}, f32[14,32,128]{2,1,0:T(8,128)S(1)}, u32[]{:S(2)}) copy-start(f32[14,32,128]{2,1,0:T(8,128)S(1)} %collective-permute-done.1.xabove) | copy-start | bytes 688132
  56.5 0.7 %copy-start = (f32[8,32,384]{2,1,0:T(8,128)}, f32[8,32,384]{2,1,0:T(8,128)S(1)}, u32[]{:S(2)}) copy-start(f32[8,32,384]{2,1,0:T(8,128)S(1)} %all-to-all-done.1.planes) | copy-start | bytes 1179652

commit v4 on v3

--- a/solution.py
+++ b/solution.py
@@ -19,6 +19,14 @@
 half_step = 0.5 * time_step
 highest = lax.Precision.HIGHEST
 LANES = 128
+GRANT = 16 * 2**20
+OUT_FIRST = "---"
+OUT_PACK = "vhhhvvvv"
+IN_Y = "-vv"
+OUT_Y = "v-"
+IN_OTHERS = "-"
+IN_FLUX = "vHHHHHH"
+IN_GRAVITY = "-vvvv"
 P_AT = prim_n
 C_AT = prim_n + 1
 V_AT = prim_n + 2
@@ -53,32 +61,89 @@
     return (gamma_gas - 1.0) * density * energy
 
 
-def pack_kernel(den, vel, pre, spe, cnt, cooled, xlo, xhi, ylo, yhi, zface):
+def copies_in(pairs, semaphores):
+    started = []
+    for n, (source, target) in enumerate(pairs):
+        copy = pltpu.make_async_copy(source, target, semaphores.at[n])
+        copy.start()
+        started.append(copy)
+    return started
+
+
+def primitive_plane(x, den, vel, pre, spe, cnt):
+    density = den[x]
+    species = [spe[s, x] for s in range(species_n)]
+    pressure = cooled_plane(density, pre[x], species, cnt[x])
+    return [density, vel[0, x], vel[1, x], vel[2, x], pressure] + [density * s for s in species]
+
+
+def first_kernel(part, den, vel, pre, spe, cnt, table, spectral, xlo, xhi,
+                 den_in, vel_in, pre_in, spe_in, cnt_in, table_in, semaphores):
     nx, ny, nz = den.shape
+    pairs = [(den, den_in), (table.at[part[0]], table_in)]
+    for n, x in enumerate((0, nx - 1)):
+        pairs += [(vel.at[:, x], vel_in.at[:, n]), (pre.at[x], pre_in.at[n])]
+        pairs += [(spe.at[:, x], spe_in.at[:, n]), (cnt.at[x], cnt_in.at[n])]
+    copies = copies_in(pairs, semaphores)
+    copies[0].wait()
+    copies[1].wait()
+    spectral[...] = lax.dot_general(
+        table_in[...], den_in[...].reshape(nx * ny, nz), (((1,), (1,)), ((), ())),
+        precision=highest, preferred_element_type=jnp.float32,
+    )
+    for copy in copies[2:]:
+        copy.wait()
+    for n, (x, face) in enumerate(((0, xlo), (nx - 1, xhi))):
+        species = [spe_in[s, n] for s in range(species_n)]
+        density = den_in[x]
+        pressure = cooled_plane(density, pre_in[n], species, cnt_in[n])
+        for c, value in enumerate(
+            [density, vel_in[0, n], vel_in[1, n], vel_in[2, n], pressure] + [density * s for s in species]
+        ):
+            face[c] = value
+
+
+def pack_kernel(parts, den, vel, pre, spe, cnt, table_y, tables, from_z, flat_table,
+                fields, ylo, yhi, zface, own_y, own_decay, own_z, own_flat,
+                den_in, vel_in, pre_in, spe_in, cnt_in, plane_semaphores, semaphores):
+    nx, ny, nz = den.shape
+    kz = own_decay.shape[1]
     lane = lax.broadcasted_iota(jnp.int32, (ny, LANES), 1)
+    arguments = ((den, den_in), (vel, vel_in), (pre, pre_in), (spe, spe_in), (cnt, cnt_in))
+
+    def plane_of(ref, x):
+        return ref.at[:, x] if len(ref.shape) == 4 else ref.at[x]
+
+    def plane_copies(x):
+        return [
+            pltpu.make_async_copy(plane_of(a, x), plane_of(b, x), plane_semaphores.at[n, x])
+            for n, (a, b) in enumerate(arguments)
+        ]
+
+    for x in range(nx):
+        for copy in plane_copies(x):
+            copy.start()
+    later = copies_in(
+        [
+            (table_y, own_y),
+            (tables.at[:, pl.ds(parts[1] * kz, kz), :], own_decay),
+            (from_z.at[parts[0]], own_z),
+            (flat_table, own_flat),
+        ],
+        semaphores,
+    )
 
     def plane(x, _):
-        density = den[x]
-        species = [spe[s, x] for s in range(species_n)]
-        pressure = cooled_plane(density, pre[x], species, cnt[x])
-        cooled[x] = pressure
-        primitive = [density, vel[0, x], vel[1, x], vel[2, x], pressure] + [density * s for s in species]
+        for copy in plane_copies(x):
+            copy.wait()
+        primitive = primitive_plane(x, den_in, vel_in, pre_in, spe_in, cnt_in)
         for c in range(prim_n):
             ylo[c, pl.ds(x, 1), :] = primitive[c][0:1, :]
             yhi[c, pl.ds(x, 1), :] = primitive[c][ny - 1 : ny, :]
-
-        @pl.when(x == 0)
-        def _():
-            for c in range(prim_n):
-                xlo[c] = primitive[c]
-
-        @pl.when(x == nx - 1)
-        def _():
-            for c in range(prim_n):
-                xhi[c] = primitive[c]
-
-        fields = fields_of(primitive)
-        carried = fields[: C_AT + 1] + [fields[V_AT + 2]]
+        derived = fields_of(primitive)
+        for f in range(field_n):
+            fields[f, x] = derived[f]
+        carried = derived[: C_AT + 1] + [derived[V_AT + 2]]
         packed = jnp.zeros((ny, LANES), jnp.float32)
         for c in range(face_n):
             first, last = carried[c][:, :LANES], carried[c][:, nz - LANES :]
@@ -88,39 +153,31 @@
         return 0
 
     lax.fori_loop(0, nx, plane, 0)
-
-
-def flux_kernel(den, vel, cooled, spe, xbelow, xabove, ybelow, yabove, zbelow, zabove,
-                new_density, momentum, energy, mass, ext, yedge):
-    nx, ny, nz = den.shape
+    for copy in later:
+        copy.wait()
+
+
+def flux_kernel(fields, xbelow, xabove, ybelow, yabove, zbelow, zabove,
+                new_density, momentum, energy, mass, xedge, yedge):
+    _, nx, ny, nz = fields.shape
     row = lax.broadcasted_iota(jnp.int32, (ny, nz), 0)
     lane = lax.broadcasted_iota(jnp.int32, (ny, nz), 1)
 
-    for at, face in ((0, xbelow), (nx + 1, xabove)):
+    for side, face in enumerate((xbelow, xabove)):
         for f, value in enumerate(fields_of([face[c] for c in range(prim_n)])):
-            ext[f, at] = value
+            xedge[side, f] = value
     for side, face in enumerate((ybelow, yabove)):
         for f, value in enumerate(fields_of([face[c] for c in range(prim_n)])):
             yedge[side, f] = value
 
-    def derive(x, _):
-        density = den[x]
-        primitive = [density, vel[0, x], vel[1, x], vel[2, x], cooled[x]]
-        primitive += [density * spe[s, x] for s in range(species_n)]
-        for f, value in enumerate(fields_of(primitive)):
-            ext[f, x + 1] = value
-        return 0
-
-    lax.fori_loop(0, nx, derive, 0)
-
-    def plane(x, _):
+    def plane(x, lower, upper):
         from_below = zbelow[x]
         from_above = zabove[x]
 
         def beside(f, direction, up):
             if direction == 0:
-                return ext[f, x + 2] if up else ext[f, x]
-            here = ext[f, x + 1]
+                return upper(f) if up else lower(f)
+            here = fields[f, x]
             if direction == 1:
                 edge = yedge[1 if up else 0, f, pl.ds(x, 1), :]
                 if up:
@@ -133,11 +190,11 @@
             edge = pltpu.roll(from_below, LANES - HIGH_FACE - slot, 1)
             return jnp.where(lane == 0, edge, pltpu.roll(here, 1, 1))
 
-        sound = ext[C_AT, x + 1]
+        sound = fields[C_AT, x]
         centre = 1.0
         above, below, push, work = [], [], [], 0.0
         for d in range(3):
-            speed = jnp.abs(ext[V_AT + d, x + 1]) + sound
+            speed = jnp.abs(fields[V_AT + d, x]) + sound
             v_up, v_lo = beside(V_AT + d, d, True), beside(V_AT + d, d, False)
             p_up, p_lo = beside(P_AT, d, True), beside(P_AT, d, False)
             s_up = jnp.maximum(speed, jnp.abs(v_up) + beside(C_AT, d, True))
@@ -149,7 +206,7 @@
             work = work + half_step * (p_lo * v_lo - p_up * v_up)
 
         def updated(f):
-            total = centre * ext[f, x + 1]
+            total = centre * fields[f, x]
             for d in range(3):
                 total = total + above[d] * beside(f, d, True)
                 total = total + below[d] * beside(f, d, False)
@@ -161,17 +218,41 @@
         energy[x] = updated(4) + work
         for s in range(species_n):
             mass[s, x] = updated(5 + s)
+
+    def inner(x, _):
+        plane(x, lambda f: fields[f, x - 1], lambda f: fields[f, x + 1])
         return 0
 
-    lax.fori_loop(0, nx, plane, 0)
-
-
-def vmem_call(kernel, out_shape, **more):
+    plane(0, lambda f: xedge[0, f], lambda f: fields[f, 1])
+    lax.fori_loop(1, nx - 1, inner, 0)
+    plane(nx - 1, lambda f: fields[f, nx - 2], lambda f: xedge[1, f])
+
+
+SPACES = {"h": pltpu.HBM, "v": pltpu.VMEM}
+
+
+def placed_call(kernel, inputs, in_spaces, outputs, out_spaces, scratch):
+    specs, operands = [], []
+    for value, space in zip(inputs, in_spaces, strict=True):
+        if space == "s":
+            specs.append(pl.BlockSpec(memory_space=pltpu.SMEM))
+        else:
+            specs.append(pl.BlockSpec(memory_space=pl.ANY if space == "h" else pltpu.VMEM))
+            if space != "-":
+                value = pltpu.with_memory_space_constraint(value, SPACES[space.lower()])
+        operands.append(value)
+    shapes = [
+        jax.ShapeDtypeStruct(shape, jnp.float32) if space == "-" else SPACES[space](shape, jnp.float32)
+        for shape, space in zip(outputs, out_spaces, strict=True)
+    ]
     return pl.pallas_call(
         kernel,
-        out_shape=[jax.ShapeDtypeStruct(s, jnp.float32) for s in out_shape],
-        **more,
-    )
+        out_shape=shapes,
+        in_specs=specs,
+        out_specs=[pl.BlockSpec(memory_space=pltpu.VMEM)] * len(shapes),
+        scratch_shapes=scratch,
+        compiler_params=pltpu.CompilerParams(vmem_limit_bytes=GRANT),
+    )(*operands)
 
 
 def shifted(value, axis, step):
@@ -206,14 +287,6 @@
     return (table / (ny * nz)).astype(np.float32)
 
 
-def along_z_kernel(part, den, table, out):
-    nx, ny, nz = den.shape
-    out[...] = lax.dot_general(
-        table[part[0]], den[...].reshape(nx * ny, nz), (((1,), (1,)), ((), ())),
-        precision=highest, preferred_element_type=jnp.float32,
-    )
-
-
 def segments(kz, width):
     return lax.broadcasted_iota(jnp.int32, (kz, LANES), 1) // width
 
@@ -223,7 +296,7 @@
     return pltpu.roll(value, lanes, 1) if lanes else value
 
 
-def along_y_kernel(size_g, block, parts, lines, table_y, tables, modes, sums, grid_rows):
+def along_y_kernel(size_g, block, lines, table_y, tables, modes, sums, grid_rows):
     _, kz, _ = lines.shape
     nx, _, ny = modes.shape
     width = block
@@ -248,7 +321,7 @@
         grid_rows[...], table_y[...], precision=highest, preferred_element_type=jnp.float32
     )
     modes[...] = spectrum.reshape(nx, kz, ny)
-    decay = tables[0, pl.ds(parts[0] * kz, kz), :]
+    decay = tables[0]
     forward, backward = modes[0], modes[nx - 1]
     for x in range(1, nx):
         forward = forward * decay + modes[x]
@@ -273,8 +346,7 @@
     )
     for tile in range(0, kz, 8):
         rows = slice(tile, tile + 8)
-        at = pl.ds(parts[0] * kz + tile, 8)
-        decay, closing, scale = tables[0, at, :], tables[1, at, :], tables[2, at, :]
+        decay, closing, scale = tables[0, rows], tables[1, rows], tables[2, rows]
         far = decay
         for _ in range(int(math.log2(nx))):
             far = far * far
@@ -296,7 +368,7 @@
         result[0] = from_left[0] + behind * decay
         if tile == 0:
             first = lax.broadcasted_iota(jnp.int32, (8, ny), 0) + lax.broadcasted_iota(jnp.int32, (8, ny), 1)
-            first = first + parts[0] == 0
+            first = first + parts[1] == 0
         for x in range(nx + 2):
             value = result[x] * scale
             if tile == 0:
@@ -332,12 +404,12 @@
                 out[target * size_g + g, :, p * LANES : (p + 1) * LANES] = piece
 
 
-def gravity_kernel(part, planes, table, den, vel, momentum_in, energy_in, potential, momentum, energy, solved, edges):
-    nx, ny, nz = den.shape
+def gravity_kernel(planes, table, fields, momentum_in, energy_in, potential, momentum, energy, solved, edges):
+    _, nx, ny, nz = fields.shape
     groups, kz, width = planes.shape
     main = nx * ny
     flat = planes[...].reshape(groups * kz, width)
-    here = table[part[0]]
+    here = table[...]
     contract = (((0,), (0,)), ((), ()))
     solved[...] = lax.dot_general(
         flat[:, :main], here, contract, precision=highest, preferred_element_type=jnp.float32
@@ -354,7 +426,7 @@
         at = 2 * ny + x
         right = jnp.where(row == ny - 1, edges[at + nx : at + nx + 1], pltpu.roll(value, ny - 1, 0))
         left = jnp.where(row == 0, edges[at : at + 1], pltpu.roll(value, 1, 0))
-        pull = time_step * den[x]
+        pull = time_step * fields[0, x]
         kicks = [
             pull * (-0.5 * (above - below)),
             pull * (-0.5 * (right - left)),
@@ -363,7 +435,7 @@
         work = energy_in[x]
         for d in range(3):
             momentum[d, x] = momentum_in[d, x] + kicks[d]
-            work = work + kicks[d] * vel[d, x]
+            work = work + kicks[d] * fields[V_AT + d, x]
         energy[x] = work
 
 
@@ -373,8 +445,9 @@
     all_x, all_y, all_z = nx * size_x, ny * size_y, nz * size_g
     groups = size_y * size_g
     kz = all_z // groups
-    in_g = lax.axis_index("ga").astype(jnp.int32).reshape(1)
-    in_plane = (lax.axis_index("hy") * size_g + lax.axis_index("ga")).astype(jnp.int32).reshape(1)
+    rank_g = lax.axis_index("ga").astype(jnp.int32)
+    rank = lax.axis_index("hy").astype(jnp.int32) * size_g + rank_g
+    parts = jnp.stack([rank_g, rank])
     main = nx * ny
     width = main + LANES
 
@@ -393,60 +466,84 @@
     tables = jnp.asarray(decay_tables(all_x, all_y, all_z))
     flat_table = jnp.asarray(flat_mode_table(nx, all_x, all_y, all_z))
 
-    scalar = pl.BlockSpec(memory_space=pltpu.SMEM)
-
-    def call(kernel, inputs, out_shape, scratch=(), **more):
-        specs = [scalar] + [pl.BlockSpec(memory_space=pltpu.VMEM)] * (len(inputs) - 1)
-        return vmem_call(
-            kernel, out_shape, in_specs=specs,
-            scratch_shapes=[pltpu.VMEM(s, jnp.float32) for s in scratch], **more,
-        )(*inputs)
-
-    (spectral,) = call(along_z_kernel, (in_g, density, into_z), [(all_z, main)])
+    floats = functools.partial(pltpu.VMEM, dtype=jnp.float32)
+    gas = (density, velocity, pressure, species, newton_count)
+
+    spectral, xlo, xhi = placed_call(
+        first_kernel,
+        (parts, *gas, into_z),
+        "shhhhhh",
+        [(all_z, main), (prim_n, ny, nz), (prim_n, ny, nz)],
+        OUT_FIRST,
+        [
+            floats((nx, ny, nz)),
+            floats((3, 2, ny, nz)),
+            floats((2, ny, nz)),
+            floats((species_n, 2, ny, nz)),
+            pltpu.VMEM((2, ny, nz), jnp.int32),
+            floats((all_z, nz)),
+            pltpu.SemaphoreType.DMA((10,)),
+        ],
+    )
+    xbelow = shifted(xhi, "hx", 1)
+    xabove = shifted(xlo, "hx", -1)
     spectral = lax.all_to_all(
         spectral.reshape(groups, kz, main), ("hy", "ga"), split_axis=0, concat_axis=0, tiled=True
     )
-
-    cooled, xlo, xhi, ylo, yhi, zface = vmem_call(
+    fields, ylo, yhi, zface, own_y, own_decay, own_z, own_flat = placed_call(
         pack_kernel,
-        [(nx, ny, nz)] + [(prim_n, ny, nz)] * 2 + [(prim_n, nx, nz)] * 2 + [(nx, ny, LANES)],
-    )(density, velocity, pressure, species, newton_count)
-    xbelow = shifted(xhi, "hx", 1)
-    xabove = shifted(xlo, "hx", -1)
+        (parts, *gas, table_y, tables, from_z, flat_table),
+        "shhhhhhhhh",
+        [(field_n, nx, ny, nz)] + [(prim_n, nx, nz)] * 2 + [(nx, ny, LANES)]
+        + [table_y.shape, (3, kz, all_y), from_z.shape[1:], flat_table.shape],
+        OUT_PACK,
+        [
+            floats((nx, ny, nz)),
+            floats((3, nx, ny, nz)),
+            floats((nx, ny, nz)),
+            floats((species_n, nx, ny, nz)),
+            pltpu.VMEM((nx, ny, nz), jnp.int32),
+            pltpu.SemaphoreType.DMA((5, nx)),
+            pltpu.SemaphoreType.DMA((4,)),
+        ],
+    )
+    modes, sums = placed_call(
+        functools.partial(along_y_kernel, size_g, ny),
+        (spectral, own_y, own_decay),
+        IN_Y,
+        [(nx, kz, all_y), (2 * kz + nx, all_y)],
+        OUT_Y,
+        [floats((nx * kz, all_y))],
+    )
+    others = [shifted(sums, "hx", s) for s in range(1, size_x)]
     ybelow = shifted(yhi, "hy", 1)
     yabove = shifted(ylo, "hy", -1)
     zbelow = shifted(zface, "ga", 1)
     zabove = zbelow if size_g == 2 else shifted(zface, "ga", -1)
-
-    modes, sums = call(
-        functools.partial(along_y_kernel, size_g, ny),
-        (in_plane, spectral, table_y, tables),
-        [(nx, kz, all_y), (2 * kz + nx, all_y)],
-        [(nx * kz, all_y)],
-    )
-    others = [shifted(sums, "hx", s) for s in range(1, size_x)]
-    (planes,) = call(
+    (planes,) = placed_call(
         functools.partial(along_x_kernel, size_x, size_g, ny),
-        (in_plane, modes, sums, *others, table_y, tables, flat_table),
+        (parts, modes, sums, *others, own_y, own_decay, own_flat),
+        "sv-" + IN_OTHERS * (size_x - 1) + "vvv",
         [(groups, kz, width)],
-        [(all_x, all_y), ((nx + 2) * kz, all_y), ((nx + 2) * kz, all_y)],
+        "-",
+        [floats((all_x, all_y)), floats(((nx + 2) * kz, all_y)), floats(((nx + 2) * kz, all_y))],
     )
     planes = lax.all_to_all(planes, ("hy", "ga"), split_axis=0, concat_axis=0, tiled=True)
-
-    new_density, momentum, total_energy, species_mass = vmem_call(
+    new_density, momentum, total_energy, species_mass = placed_call(
         flux_kernel,
+        (fields, xbelow, xabove, ybelow, yabove, zbelow, zabove),
+        IN_FLUX,
         [(nx, ny, nz), (3, nx, ny, nz), (nx, ny, nz), (species_n, nx, ny, nz)],
-        scratch_shapes=[
-            pltpu.VMEM((field_n, nx + 2, ny, nz), jnp.float32),
-            pltpu.VMEM((2, field_n, nx, nz), jnp.float32),
-        ],
-    )(density, velocity, cooled, species, xbelow, xabove, ybelow, yabove, zbelow, zabove)
-
-    potential, momentum, total_energy = call(
+        "-vv-",
+        [floats((2, field_n, ny, nz)), floats((2, field_n, nx, nz))],
+    )
+    potential, momentum, total_energy = placed_call(
         gravity_kernel,
-        (in_g, planes, from_z, density, velocity, momentum, total_energy),
+        (planes, own_z, fields, momentum, total_energy),
+        IN_GRAVITY,
         [(nx, ny, nz), (3, nx, ny, nz), (nx, ny, nz)],
-        [(main, 2 * nz), (LANES, nz)],
+        "---",
+        [floats((main, 2 * nz)), floats((LANES, nz))],
     )
     return (new_density, momentum, total_energy, species_mass, potential)
 

time: 60.5 us -> 51.7 us (0.85)
  waiting for transfers between devices: 14.5 us -> 9.62 us
  Pallas kernels: 20.4 us -> 16.3 us
    all_to_all x1, waiting for transfers between devices: 6 us -> 1.5 us  [step(): lax.all_to_all(spectral.reshape(groups, kz, main), ('hy', 'ga'), split_ax...]
    pallas_call x6, Pallas kernels: 20.4 us -> 16.3 us  [placed_call(): pl.pallas_call(kernel, out_shape=shapes, in_specs=specs, out_specs=[pl.Bl...]
    unnamed x20 -> x18, local copies, waits for them, and re-layouts: 2.73 us -> 2.92 us
  transfers between devices with their start and end apart: 10 -> 10, of which waited for: 8 -> 9; matrix products, arithmetic and copies ran while one was open for 0% -> 0% of each run, Pallas kernels for 18% -> 19%
where the time goes in v4:
time: 51.7 us; the launch traced here: 51.3 us
  starting transfers between devices  21.7 us (42%)
  Pallas kernels  16.3 us (32%)
  waiting for transfers between devices  9.62 us (19%)
  local copies, waits for them, and re-layouts  2.92 us (6%)
  between operations  0.71 us (1%)
    pallas_call x6, Pallas kernels, placed_call(): pl.pallas_call(kernel, out_shape=shapes, in_specs=specs, out_specs=[pl.Bl...  16.3 us
    ppermute x8, starting transfers between devices, shifted(): lax.ppermute(value, axis, [(i, (i + step) % count) for i in range(count)])  13.1 us
    ppermute x8, waiting for transfers between devices, shifted(): lax.ppermute(value, axis, [(i, (i + step) % count) for i in range(count)])  8.11 us
    all_to_all x1, starting transfers between devices, step(): lax.all_to_all(spectral.reshape(groups, kz, main), ('hy', 'ga'), split_ax...  5.2 us
    all_to_all x1, starting transfers between devices, step(): lax.all_to_all(planes, ('hy', 'ga'), split_axis=0, concat_axis=0, tiled=T...  3.45 us
    unnamed x18, local copies, waits for them, and re-layouts  2.92 us
    all_to_all x1, waiting for transfers between devices, step(): lax.all_to_all(spectral.reshape(groups, kz, main), ('hy', 'ga'), split_ax...  1.5 us
  transfers between devices with their start and end apart: 10, of which 9 were waited for; matrix products, arithmetic and copies ran while one was open for 0% of the time, Pallas kernels for 19%

profile of v4, /device:TPU:0, one launch (start us, length us, event | category | flops | bytes accessed | tf_op | source)
XLA Modules:
  0.0 51.3 jit_solution(3752039108228620967)
XLA Ops:
  0.6 0.1 pad_add_fusion.parts.part
  0.7 2.7 %shard_map.138 = (f32[256,256]{1,0:T(8,128)}, f32[14,32,128]{2,1,0:T(8,128)S(1)}, f32[14,32,128]{2,1,0:T(8,128)S(1)}) custom-call(s32[2]{0:T(128)S(1)} %pad_add_fusion.parts.part, f32[8,32,128]{2,1,0:T(8,128)} %den.3, f32[3,8,32,128]{3,2,1,0:T(8,128)} %vel.3, f32[8,32,128]{2,1,0:T(8,128)} %pre.3, f32[9,8,32,128]{3,2,1,0:T(8,128)} %spe.3, s32[8,32,128]{2,1,0:T(8,128)} %cnt.3, ...), custom_call_target="tpu_custom_call" | custom-call | tf_op jit(solution)/shard_map/pallas_call | solution.py:248
  3.4 0.0 copy-start.2
  3.4 0.7 %copy-done.2 = f32[14,32,128]{2,1,0:T(8,128)} copy-done((f32[14,32,128]{2,1,0:T(8,128)}, f32[14,32,128]{2,1,0:T(8,128)S(1)}, u32[]{:S(2)}) %copy-start.2) | copy-done | bytes 229400
  4.1 5.2 %all-to-all-start = ((f32[8,32,256]{2,1,0:T(8,128)}), f32[8,32,256]{2,1,0:T(8,128)S(1)}, u32[]{:S(2)}, u32[]{:S(2)}) async-start(f32[8,32,256]{2,1,0:T(8,128)} %bitcast.2), calls=%async_computation | async-start | bytes 524288 | tf_op jit(solution)/shard_map/all_to_all | solution.py:490
  9.3 4.5 %shard_map.137 = (f32[19,8,32,128]{3,2,1,0:T(8,128)S(1)}, f32[14,8,128]{2,1,0:T(8,128)}, f32[14,8,128]{2,1,0:T(8,128)}, f32[8,32,128]{2,1,0:T(8,128)}, f32[128,1...) custom-call(s32[2]{0:T(128)S(1)} %pad_add_fusion.parts.part, ...), custom_call_target="tpu_custom_call" | custom-call | tf_op jit(solution)/shard_map/pallas_call | solution.py:248
  13.8 0.0 copy-start.8
  13.8 1.5 %all-to-all-done.lines = f32[8,32,256]{2,1,0:T(8,128)S(1)} async-done(((f32[8,32,256]{2,1,0:T(8,128)}), f32[8,32,256]{2,1,0:T(8,128)S(1)}, u32[]{:S(2)}, u32[]{:S(2)}) %all-to-all-start) | async-done | bytes 262176 | tf_op jit(solution)/shard_map/all_to_all | solution.py:490
  15.3 0.4 shard_map.140
  15.7 1.6 %collective-permute-start.5 = (f32[72,128]{1,0:T(8,128)S(1)}, f32[72,128]{1,0:T(8,128)S(1)}, u32[]{:S(2)}, u32[]{:S(2)}) collective-permute-start(f32[72,128]{1,0:T(8,128)S(1)} %get-tuple-element.36.own), channel_id=1, source_target_pairs={{0,8},{8,16},{16,24},{24,0},{1,9},{9,17},{17,25},{25,1},{2,10},{10... | collective-permute-start | bytes 110600 | tf_op jit(solution)/shard_map/ppermute | solution.py:260
  17.3 2.6 %collective-permute-start.6 = (f32[72,128]{1,0:T(8,128)S(1)}, f32[72,128]{1,0:T(8,128)S(1)}, u32[]{:S(2)}, u32[]{:S(2)}) collective-permute-start(f32[72,128]{1,0:T(8,128)S(1)} %get-tuple-element.36.own), channel_id=1, source_target_pairs={{0,16},{8,24},{16,0},{24,8},{1,17},{9,25},{17,1},{25,9},{2,18},{10... | collective-permute-start | bytes 110600 | tf_op jit(solution)/shard_map/ppermute | solution.py:260
  19.9 1.3 %collective-permute-start.7 = (f32[72,128]{1,0:T(8,128)S(1)}, f32[72,128]{1,0:T(8,128)S(1)}, u32[]{:S(2)}, u32[]{:S(2)}) collective-permute-start(f32[72,128]{1,0:T(8,128)S(1)} %get-tuple-element.36.own), channel_id=1, source_target_pairs={{0,24},{8,0},{16,8},{24,16},{1,25},{9,1},{17,9},{25,17},{2,26},{10... | collective-permute-start | bytes 110600 | tf_op jit(solution)/shard_map/ppermute | solution.py:260
  21.3 0.2 collective-permute-done.5.rest_0_
  21.5 1.3 %collective-permute-done.6.rest_1_ = f32[72,128]{1,0:T(8,128)S(1)} collective-permute-done((f32[72,128]{1,0:T(8,128)S(1)}, f32[72,128]{1,0:T(8,128)S(1)}, u32[]{:S(2)}, u32[]{:S(2)}) %collective-permute-start.6) | collective-permute-done | bytes 36896 | tf_op jit(solution)/shard_map/ppermute | solution.py:260
  22.9 1.0 %collective-permute-done.7.rest_2_ = f32[72,128]{1,0:T(8,128)S(1)} collective-permute-done((f32[72,128]{1,0:T(8,128)S(1)}, f32[72,128]{1,0:T(8,128)S(1)}, u32[]{:S(2)}, u32[]{:S(2)}) %collective-permute-start.7) | collective-permute-done | bytes 36896 | tf_op jit(solution)/shard_map/ppermute | solution.py:260
  23.9 2.2 %shard_map.141 = f32[8,32,384]{2,1,0:T(8,128)} custom-call(s32[2]{0:T(128)S(1)} %pad_add_fusion.parts.part, f32[8,32,128]{2,1,0:T(8,128)S(1)} %get-tuple-element.35.modes, f32[72,128]{1,0:T(8,128)S(1)} %get-tuple-element.36.own, f32[72,128]{1,0:T(8,128)S(1)} %collective-permute-done.5.rest_0_, f32[72,128]{1,0:T(8,128)S(1)} %collective-permute-done.6.rest_1_, ...), custom_call_target="tpu_custom_call" | custom-call | tf_op jit(solution)/shard_map/pallas_call | solution.py:248
  26.0 3.5 %all-to-all-start.1 = ((f32[8,32,384]{2,1,0:T(8,128)}), f32[8,32,384]{2,1,0:T(8,128)S(1)}, u32[]{:S(2)}, u32[]{:S(2)}) async-start(f32[8,32,384]{2,1,0:T(8,128)} %shard_map.141), calls=%async_computation.1 | async-start | bytes 786432 | tf_op jit(solution)/shard_map/all_to_all | solution.py:531
  29.5 0.5 collective-permute-start
  30.0 3.4 %collective-permute-start.1 = (f32[14,32,128]{2,1,0:T(8,128)S(1)}, f32[14,32,128]{2,1,0:T(8,128)S(1)}, u32[]{:S(2)}, u32[]{:S(2)}) collective-permute-start(f32[14,32,128]{2,1,0:T(8,128)S(1)} %get-tuple-element.27), channel_id=1, source_target_pairs={{0,24},{8,0},{16,8},{24,16},{1,25},{9,1},{17,9},{25,17},{2,26},{10... | collective-permute-start | bytes 688136 | tf_op jit(solution)/shard_map/ppermute | solution.py:260
  33.4 0.0 copy-done.8
  33.4 1.9 %collective-permute-start.4 = (f32[8,32,128]{2,1,0:T(8,128)S(1)}, f32[8,32,128]{2,1,0:T(8,128)S(1)}, u32[]{:S(2)}, u32[]{:S(2)}) collective-permute-start(f32[8,32,128]{2,1,0:T(8,128)S(1)} %copy-done.8), channel_id=1, source_target_pairs={{0,1},{1,0},{2,3},{3,2},{4,5},{5,4},{6,7},{7,6},{8,9},{9,8},{10,11... | collective-permute-start | bytes 393224 | tf_op jit(solution)/shard_map/ppermute | solution.py:260
  35.3 0.0 collective-permute-start.2
  35.3 1.7 %collective-permute-start.3 = (f32[14,8,128]{2,1,0:T(8,128)}, f32[14,8,128]{2,1,0:T(8,128)S(1)}, u32[]{:S(2)}, u32[]{:S(2)}) collective-permute-start(f32[14,8,128]{2,1,0:T(8,128)} %get-tuple-element.29), channel_id=1, source_target_pairs={{0,6},{2,0},{4,2},{6,4},{1,7},{3,1},{5,3},{7,5},{8,14},{10,8},{12,... | collective-permute-start | bytes 172040 | tf_op jit(solution)/shard_map/ppermute | solution.py:260
  37.0 2.1 %collective-permute-done.2.ybelow = f32[14,8,128]{2,1,0:T(8,128)S(1)} collective-permute-done((f32[14,8,128]{2,1,0:T(8,128)}, f32[14,8,128]{2,1,0:T(8,128)S(1)}, u32[]{:S(2)}, u32[]{:S(2)}) %collective-permute-start.2) | collective-permute-done | bytes 57376 | tf_op jit(solution)/shard_map/ppermute | solution.py:260
  39.1 0.0 copy-start.6
  39.1 0.1 collective-permute-done.3.yabove
  39.1 0.0 copy-start.7
  39.1 0.5 collective-permute-done.4.zbelow.zabove
  39.6 0.0 copy-start.3
  39.6 0.5 collective-permute-done.xbelow
  40.1 0.0 copy-start.4
  40.1 2.4 %collective-permute-done.1.xabove = f32[14,32,128]{2,1,0:T(8,128)S(1)} collective-permute-done((f32[14,32,128]{2,1,0:T(8,128)S(1)}, f32[14,32,128]{2,1,0:T(8,128)S(1)}, u32[]{:S(2)}, u32[]{:S(2)}) %collective-permute-start.1) | collective-permute-done | bytes 229408 | tf_op jit(solution)/shard_map/ppermute | solution.py:260
  42.5 0.0 copy-start.5
  42.5 0.0 copy-done.6
  42.5 0.0 copy-done.7
  42.5 0.0 copy-done.3
  42.5 0.0 copy-done.4
  42.5 0.7 %copy-done.5 = f32[14,32,128]{2,1,0:T(8,128)} copy-done((f32[14,32,128]{2,1,0:T(8,128)}, f32[14,32,128]{2,1,0:T(8,128)S(1)}, u32[]{:S(2)}) %copy-start.5) | copy-done | bytes 229400
  43.2 5.2 %shard_map.139 = (f32[8,32,128]{2,1,0:T(8,128)}, f32[3,8,32,128]{3,2,1,0:T(8,128)S(1)}, f32[8,32,128]{2,1,0:T(8,128)S(1)}, f32[9,8,32,128]{3,2,1,0:T(8,128)}) custom-call(f32[19,8,32,128]{3,2,1,0:T(8,128)S(1)} %get-tuple-element.25.fields, f32[14,32,128]{2,1,0:T(8,128)} %copy-done.4, f32[14,32,128]{2,1,0:T(8,128)} %copy-done.5, f32[14,8,128]{2,1,0:T(8,128)} %copy-done.6, ...), custom_call_target="tpu_custom_call" | custom-call | tf_op jit(solution)/shard_map/pallas_call | solution.py:248
  48.4 0.0 copy-start
  48.4 0.7 %copy-done = f32[8,32,128]{2,1,0:T(8,128)} copy-done((f32[8,32,128]{2,1,0:T(8,128)}, f32[8,32,128]{2,1,0:T(8,128)S(1)}, u32[]{:S(2)}) %copy-start) | copy-done | bytes 131096
  49.0 0.0 all-to-all-done.1.planes
  49.0 0.0 copy-start.1
  49.0 0.9 %copy-done.1 = f32[8,32,128]{2,1,0:T(8,128)S(1)} copy-done((f32[8,32,128]{2,1,0:T(8,128)S(1)}, f32[8,32,128]{2,1,0:T(8,128)}, u32[]{:S(2)}) %copy-start.1) | copy-done | bytes 131096
  49.9 1.4 %shard_map.142 = (f32[8,32,128]{2,1,0:T(8,128)}, f32[3,8,32,128]{3,2,1,0:T(8,128)}, f32[8,32,128]{2,1,0:T(8,128)}) custom-call(f32[8,32,384]{2,1,0:T(8,128)S(1)} %all-to-all-done.1.planes, f32[256,256]{1,0:T(8,128)S(1)} %get-tuple-element.38.table, f32[19,8,32,128]{3,2,1,0:T(8,128)S(1)} %get-tuple-element.25.fields, ...), custom_call_target="tpu_custom_call" | custom-call | tf_op jit(solution)/shard_map/pallas_call | solution.py:248
Async XLA Ops:
  3.4 0.7 %copy-start.2 = (f32[14,32,128]{2,1,0:T(8,128)}, f32[14,32,128]{2,1,0:T(8,128)S(1)}, u32[]{:S(2)}) copy-start(f32[14,32,128]{2,1,0:T(8,128)S(1)} %get-tuple-element.26) | copy-start | bytes 688132
  4.1 11.2 %all-to-all-start = ((f32[8,32,256]{2,1,0:T(8,128)}), f32[8,32,256]{2,1,0:T(8,128)S(1)}, u32[]{:S(2)}, u32[]{:S(2)}) async-start(f32[8,32,256]{2,1,0:T(8,128)} %bitcast.2), calls=%async_computation | async-start | bytes 524288 | tf_op jit(solution)/shard_map/all_to_all | solution.py:490
  13.8 19.6 %copy-start.8 = (f32[8,32,128]{2,1,0:T(8,128)S(1)}, f32[8,32,128]{2,1,0:T(8,128)}, u32[]{:S(2)}) copy-start(f32[8,32,128]{2,1,0:T(8,128)} %get-tuple-element.30) | copy-start | bytes 393220
  15.7 5.8 %collective-permute-start.5 = (f32[72,128]{1,0:T(8,128)S(1)}, f32[72,128]{1,0:T(8,128)S(1)}, u32[]{:S(2)}, u32[]{:S(2)}) collective-permute-start(f32[72,128]{1,0:T(8,128)S(1)} %get-tuple-element.36.own), channel_id=1, source_target_pairs={{0,8},{8,16},{16,24},{24,0},{1,9},{9,17},{17,25},{25,1},{2,10},{10... | collective-permute-start | bytes 110600 | tf_op jit(solution)/shard_map/ppermute | solution.py:260
  17.3 5.5 %collective-permute-start.6 = (f32[72,128]{1,0:T(8,128)S(1)}, f32[72,128]{1,0:T(8,128)S(1)}, u32[]{:S(2)}, u32[]{:S(2)}) collective-permute-start(f32[72,128]{1,0:T(8,128)S(1)} %get-tuple-element.36.own), channel_id=1, source_target_pairs={{0,16},{8,24},{16,0},{24,8},{1,17},{9,25},{17,1},{25,9},{2,18},{10... | collective-permute-start | bytes 110600 | tf_op jit(solution)/shard_map/ppermute | solution.py:260
  19.9 4.0 %collective-permute-start.7 = (f32[72,128]{1,0:T(8,128)S(1)}, f32[72,128]{1,0:T(8,128)S(1)}, u32[]{:S(2)}, u32[]{:S(2)}) collective-permute-start(f32[72,128]{1,0:T(8,128)S(1)} %get-tuple-element.36.own), channel_id=1, source_target_pairs={{0,24},{8,0},{16,8},{24,16},{1,25},{9,1},{17,9},{25,17},{2,26},{10... | collective-permute-start | bytes 110600 | tf_op jit(solution)/shard_map/ppermute | solution.py:260
  26.0 23.0 %all-to-all-start.1 = ((f32[8,32,384]{2,1,0:T(8,128)}), f32[8,32,384]{2,1,0:T(8,128)S(1)}, u32[]{:S(2)}, u32[]{:S(2)}) async-start(f32[8,32,384]{2,1,0:T(8,128)} %shard_map.141), calls=%async_computation.1 | async-start | bytes 786432 | tf_op jit(solution)/shard_map/all_to_all | solution.py:531
  29.5 10.6 %collective-permute-start = (f32[14,32,128]{2,1,0:T(8,128)}, f32[14,32,128]{2,1,0:T(8,128)S(1)}, u32[]{:S(2)}, u32[]{:S(2)}) collective-permute-start(f32[14,32,128]{2,1,0:T(8,128)} %copy-done.2), channel_id=1, source_target_pairs={{0,8},{8,16},{16,24},{24,0},{1,9},{9,17},{17,25},{25,1},{2,10},{10... | collective-permute-start | bytes 688136 | tf_op jit(solution)/shard_map/ppermute | solution.py:260
  30.0 12.5 %collective-permute-start.1 = (f32[14,32,128]{2,1,0:T(8,128)S(1)}, f32[14,32,128]{2,1,0:T(8,128)S(1)}, u32[]{:S(2)}, u32[]{:S(2)}) collective-permute-start(f32[14,32,128]{2,1,0:T(8,128)S(1)} %get-tuple-element.27), channel_id=1, source_target_pairs={{0,24},{8,0},{16,8},{24,16},{1,25},{9,1},{17,9},{25,17},{2,26},{10... | collective-permute-start | bytes 688136 | tf_op jit(solution)/shard_map/ppermute | solution.py:260
  33.4 6.2 %collective-permute-start.4 = (f32[8,32,128]{2,1,0:T(8,128)S(1)}, f32[8,32,128]{2,1,0:T(8,128)S(1)}, u32[]{:S(2)}, u32[]{:S(2)}) collective-permute-start(f32[8,32,128]{2,1,0:T(8,128)S(1)} %copy-done.8), channel_id=1, source_target_pairs={{0,1},{1,0},{2,3},{3,2},{4,5},{5,4},{6,7},{7,6},{8,9},{9,8},{10,11... | collective-permute-start | bytes 393224 | tf_op jit(solution)/shard_map/ppermute | solution.py:260
  35.3 3.8 %collective-permute-start.2 = (f32[14,8,128]{2,1,0:T(8,128)}, f32[14,8,128]{2,1,0:T(8,128)S(1)}, u32[]{:S(2)}, u32[]{:S(2)}) collective-permute-start(f32[14,8,128]{2,1,0:T(8,128)} %get-tuple-element.28), channel_id=1, source_target_pairs={{0,2},{2,4},{4,6},{6,0},{1,3},{3,5},{5,7},{7,1},{8,10},{10,12},{12... | collective-permute-start | bytes 172040 | tf_op jit(solution)/shard_map/ppermute | solution.py:260
  35.3 3.9 %collective-permute-start.3 = (f32[14,8,128]{2,1,0:T(8,128)}, f32[14,8,128]{2,1,0:T(8,128)S(1)}, u32[]{:S(2)}, u32[]{:S(2)}) collective-permute-start(f32[14,8,128]{2,1,0:T(8,128)} %get-tuple-element.29), channel_id=1, source_target_pairs={{0,6},{2,0},{4,2},{6,4},{1,7},{3,1},{5,3},{7,5},{8,14},{10,8},{12,... | collective-permute-start | bytes 172040 | tf_op jit(solution)/shard_map/ppermute | solution.py:260
  39.1 3.5 %copy-start.6 = (f32[14,8,128]{2,1,0:T(8,128)}, f32[14,8,128]{2,1,0:T(8,128)S(1)}, u32[]{:S(2)}) copy-start(f32[14,8,128]{2,1,0:T(8,128)S(1)} %collective-permute-done.2.ybelow) | copy-start | bytes 172036
  39.1 3.4 %copy-start.7 = (f32[14,8,128]{2,1,0:T(8,128)}, f32[14,8,128]{2,1,0:T(8,128)S(1)}, u32[]{:S(2)}) copy-start(f32[14,8,128]{2,1,0:T(8,128)S(1)} %collective-permute-done.3.yabove) | copy-start | bytes 172036
  39.6 2.9 %copy-start.3 = (f32[8,32,128]{2,1,0:T(8,128)}, f32[8,32,128]{2,1,0:T(8,128)S(1)}, u32[]{:S(2)}) copy-start(f32[8,32,128]{2,1,0:T(8,128)S(1)} %collective-permute-done.4.zbelow.zabove) | copy-start | bytes 393220
  40.1 2.4 %copy-start.4 = (f32[14,32,128]{2,1,0:T(8,128)}, f32[14,32,128]{2,1,0:T(8,128)S(1)}, u32[]{:S(2)}) copy-start(f32[14,32,128]{2,1,0:T(8,128)S(1)} %collective-permute-done.xbelow) | copy-start | bytes 688132
  42.5 0.7 %copy-start.5 = (f32[14,32,128]{2,1,0:T(8,128)}, f32[14,32,128]{2,1,0:T(8,128)S(1)}, u32[]{:S(2)}) copy-start(f32[14,32,128]{2,1,0:T(8,128)S(1)} %collective-permute-done.1.xabove) | copy-start | bytes 688132
  48.4 0.7 %copy-start = (f32[8,32,128]{2,1,0:T(8,128)}, f32[8,32,128]{2,1,0:T(8,128)S(1)}, u32[]{:S(2)}) copy-start(f32[8,32,128]{2,1,0:T(8,128)S(1)} %get-tuple-element.40.energy_in) | copy-start | bytes 393220
  49.0 0.9 %copy-start.1 = (f32[8,32,128]{2,1,0:T(8,128)S(1)}, f32[8,32,128]{2,1,0:T(8,128)}, u32[]{:S(2)}) copy-start(f32[8,32,128]{2,1,0:T(8,128)} %copy-done) | copy-start | bytes 393220

commit v5 on v4

--- a/solution.py
+++ b/solution.py
@@ -20,30 +20,28 @@
 highest = lax.Precision.HIGHEST
 LANES = 128
 GRANT = 16 * 2**20
-OUT_FIRST = "---"
-OUT_PACK = "vhhhvvvv"
+OUT_FIRST = "vvvvvvvv"
+OUT_PACK = "vvvhhhvvv"
 IN_Y = "-vv"
 OUT_Y = "v-"
 IN_OTHERS = "-"
-IN_FLUX = "vHHHHHH"
+OUT_X = "h"
+IN_FLUX = "svvvvvhhvvvvh"
 IN_GRAVITY = "-vvvv"
-P_AT = prim_n
-C_AT = prim_n + 1
-V_AT = prim_n + 2
-field_n = prim_n + 5
+P_AT = 4
+C_AT = prim_n
 face_n = prim_n + 3
 HIGH_FACE = 64
 
 
-def fields_of(primitive):
-    density, v0, v1, v2, pressure = primitive[:5]
+def sound_speed(density, pressure):
+    return jnp.sqrt(gamma_gas * pressure / density)
+
+
+def conserved(kept):
+    density, v0, v1, v2, pressure = kept[:5]
     energy = pressure * (1.0 / (gamma_gas - 1.0)) + 0.5 * density * (v0 * v0 + v1 * v1 + v2 * v2)
-    sound = jnp.sqrt(gamma_gas * pressure / density)
-    return (
-        [density, density * v0, density * v1, density * v2, energy]
-        + list(primitive[5:])
-        + [pressure, sound, v0, v1, v2]
-    )
+    return [density, density * v0, density * v1, density * v2, energy] + list(kept[5:prim_n])
 
 
 def cooled_plane(density, pressure, species, count):
@@ -80,11 +78,10 @@
 def first_kernel(part, den, vel, pre, spe, cnt, table, spectral, xlo, xhi,
                  den_in, vel_in, pre_in, spe_in, cnt_in, table_in, semaphores):
     nx, ny, nz = den.shape
-    pairs = [(den, den_in), (table.at[part[0]], table_in)]
-    for n, x in enumerate((0, nx - 1)):
-        pairs += [(vel.at[:, x], vel_in.at[:, n]), (pre.at[x], pre_in.at[n])]
-        pairs += [(spe.at[:, x], spe_in.at[:, n]), (cnt.at[x], cnt_in.at[n])]
-    copies = copies_in(pairs, semaphores)
+    copies = copies_in(
+        [(den, den_in), (table.at[part[0]], table_in), (pre, pre_in), (cnt, cnt_in), (spe, spe_in), (vel, vel_in)],
+        semaphores,
+    )
     copies[0].wait()
     copies[1].wait()
     spectral[...] = lax.dot_general(
@@ -93,57 +90,36 @@
     )
     for copy in copies[2:]:
         copy.wait()
-    for n, (x, face) in enumerate(((0, xlo), (nx - 1, xhi))):
-        species = [spe_in[s, n] for s in range(species_n)]
-        density = den_in[x]
-        pressure = cooled_plane(density, pre_in[n], species, cnt_in[n])
-        for c, value in enumerate(
-            [density, vel_in[0, n], vel_in[1, n], vel_in[2, n], pressure] + [density * s for s in species]
-        ):
+    for x, face in ((0, xlo), (nx - 1, xhi)):
+        for c, value in enumerate(primitive_plane(x, den_in, vel_in, pre_in, spe_in, cnt_in)):
             face[c] = value
 
 
-def pack_kernel(parts, den, vel, pre, spe, cnt, table_y, tables, from_z, flat_table,
-                fields, ylo, yhi, zface, own_y, own_decay, own_z, own_flat,
-                den_in, vel_in, pre_in, spe_in, cnt_in, plane_semaphores, semaphores):
+def pack_kernel(parts, den, vel, pre, spe, cnt, table_y, tables, flat_table,
+                cooled, mass, sound, ylo, yhi, zface, own_y, own_decay, own_flat, semaphores):
     nx, ny, nz = den.shape
     kz = own_decay.shape[1]
     lane = lax.broadcasted_iota(jnp.int32, (ny, LANES), 1)
-    arguments = ((den, den_in), (vel, vel_in), (pre, pre_in), (spe, spe_in), (cnt, cnt_in))
-
-    def plane_of(ref, x):
-        return ref.at[:, x] if len(ref.shape) == 4 else ref.at[x]
-
-    def plane_copies(x):
-        return [
-            pltpu.make_async_copy(plane_of(a, x), plane_of(b, x), plane_semaphores.at[n, x])
-            for n, (a, b) in enumerate(arguments)
-        ]
-
-    for x in range(nx):
-        for copy in plane_copies(x):
-            copy.start()
     later = copies_in(
         [
             (table_y, own_y),
             (tables.at[:, pl.ds(parts[1] * kz, kz), :], own_decay),
-            (from_z.at[parts[0]], own_z),
             (flat_table, own_flat),
         ],
         semaphores,
     )
 
     def plane(x, _):
-        for copy in plane_copies(x):
-            copy.wait()
-        primitive = primitive_plane(x, den_in, vel_in, pre_in, spe_in, cnt_in)
+        primitive = primitive_plane(x, den, vel, pre, spe, cnt)
         for c in range(prim_n):
             ylo[c, pl.ds(x, 1), :] = primitive[c][0:1, :]
             yhi[c, pl.ds(x, 1), :] = primitive[c][ny - 1 : ny, :]
-        derived = fields_of(primitive)
-        for f in range(field_n):
-            fields[f, x] = derived[f]
-        carried = derived[: C_AT + 1] + [derived[V_AT + 2]]
+        kept = primitive + [sound_speed(primitive[0], primitive[P_AT])]
+        cooled[x] = kept[P_AT]
+        for s in range(species_n):
+            mass[s, x] = kept[P_AT + 1 + s]
+        sound[x] = kept[C_AT]
+        carried = conserved(kept) + [kept[P_AT], kept[C_AT], kept[3]]
         packed = jnp.zeros((ny, LANES), jnp.float32)
         for c in range(face_n):
             first, last = carried[c][:, :LANES], carried[c][:, nz - LANES :]
@@ -157,56 +133,68 @@
         copy.wait()
 
 
-def flux_kernel(fields, xbelow, xabove, ybelow, yabove, zbelow, zabove,
-                new_density, momentum, energy, mass, xedge, yedge):
-    _, nx, ny, nz = fields.shape
+def flux_kernel(parts, den, vel, cooled, dense, speed_of, xbelow, xabove, ybelow, yabove, zbelow, zabove, from_z,
+                new_density, carried, mass, own_z, xfaces, yedge, semaphores):
+    nx, ny, nz = den.shape
     row = lax.broadcasted_iota(jnp.int32, (ny, nz), 0)
     lane = lax.broadcasted_iota(jnp.int32, (ny, nz), 1)
-
-    for side, face in enumerate((xbelow, xabove)):
-        for f, value in enumerate(fields_of([face[c] for c in range(prim_n)])):
-            xedge[side, f] = value
+    copies = copies_in(
+        [(xbelow, xfaces.at[0]), (xabove, xfaces.at[1]), (from_z.at[parts[0]], own_z)], semaphores
+    )
+
+    def with_flow(kept):
+        return conserved(kept) + [kept[P_AT], kept[C_AT], kept[1], kept[2], kept[3]]
+
+    def stored(x):
+        kept = [den[x], vel[0, x], vel[1, x], vel[2, x], cooled[x]]
+        return with_flow(kept + [dense[s, x] for s in range(species_n)] + [speed_of[x]])
+
+    def faced(face):
+        kept = [face[c] for c in range(prim_n)]
+        return with_flow(kept + [sound_speed(kept[0], kept[P_AT])])
+
+    flow_p, flow_c, flow_v = prim_n, prim_n + 1, prim_n + 2
     for side, face in enumerate((ybelow, yabove)):
-        for f, value in enumerate(fields_of([face[c] for c in range(prim_n)])):
+        for f, value in enumerate(faced(face)):
             yedge[side, f] = value
 
     def plane(x, lower, upper):
         from_below = zbelow[x]
         from_above = zabove[x]
+        centre = stored(x)
 
         def beside(f, direction, up):
             if direction == 0:
-                return upper(f) if up else lower(f)
-            here = fields[f, x]
+                return upper[f] if up else lower[f]
+            here = centre[f]
             if direction == 1:
                 edge = yedge[1 if up else 0, f, pl.ds(x, 1), :]
                 if up:
                     return jnp.where(row == ny - 1, edge, pltpu.roll(here, ny - 1, 0))
                 return jnp.where(row == 0, edge, pltpu.roll(here, 1, 0))
-            slot = f if f < V_AT else prim_n + 2
+            slot = f if f < flow_v else flow_v
             if up:
                 edge = pltpu.roll(from_above, LANES - 1 - slot, 1)
                 return jnp.where(lane == nz - 1, edge, pltpu.roll(here, nz - 1, 1))
             edge = pltpu.roll(from_below, LANES - HIGH_FACE - slot, 1)
             return jnp.where(lane == 0, edge, pltpu.roll(here, 1, 1))
 
-        sound = fields[C_AT, x]
-        centre = 1.0
+        stay = 1.0
         above, below, push, work = [], [], [], 0.0
         for d in range(3):
-            speed = jnp.abs(fields[V_AT + d, x]) + sound
-            v_up, v_lo = beside(V_AT + d, d, True), beside(V_AT + d, d, False)
-            p_up, p_lo = beside(P_AT, d, True), beside(P_AT, d, False)
-            s_up = jnp.maximum(speed, jnp.abs(v_up) + beside(C_AT, d, True))
-            s_lo = jnp.maximum(speed, jnp.abs(v_lo) + beside(C_AT, d, False))
-            centre = centre - half_step * (s_up + s_lo)
+            speed = jnp.abs(centre[flow_v + d]) + centre[flow_c]
+            v_up, v_lo = beside(flow_v + d, d, True), beside(flow_v + d, d, False)
+            p_up, p_lo = beside(flow_p, d, True), beside(flow_p, d, False)
+            s_up = jnp.maximum(speed, jnp.abs(v_up) + beside(flow_c, d, True))
+            s_lo = jnp.maximum(speed, jnp.abs(v_lo) + beside(flow_c, d, False))
+            stay = stay - half_step * (s_up + s_lo)
             above.append(half_step * (s_up - v_up))
             below.append(half_step * (s_lo + v_lo))
             push.append(half_step * (p_lo - p_up))
             work = work + half_step * (p_lo * v_lo - p_up * v_up)
 
         def updated(f):
-            total = centre * fields[f, x]
+            total = stay * centre[f]
             for d in range(3):
                 total = total + above[d] * beside(f, d, True)
                 total = total + below[d] * beside(f, d, False)
@@ -214,24 +202,27 @@
 
         new_density[x] = updated(0)
         for d in range(3):
-            momentum[d, x] = updated(1 + d) + push[d]
-        energy[x] = updated(4) + work
+            carried[d, x] = updated(1 + d) + push[d]
+        carried[3, x] = updated(4) + work
         for s in range(species_n):
             mass[s, x] = updated(5 + s)
 
     def inner(x, _):
-        plane(x, lambda f: fields[f, x - 1], lambda f: fields[f, x + 1])
+        plane(x, stored(x - 1), stored(x + 1))
         return 0
 
-    plane(0, lambda f: xedge[0, f], lambda f: fields[f, 1])
     lax.fori_loop(1, nx - 1, inner, 0)
-    plane(nx - 1, lambda f: fields[f, nx - 2], lambda f: xedge[1, f])
+    copies[0].wait()
+    plane(0, faced(xfaces.at[0]), stored(1))
+    copies[1].wait()
+    plane(nx - 1, stored(nx - 2), faced(xfaces.at[1]))
+    copies[2].wait()
 
 
 SPACES = {"h": pltpu.HBM, "v": pltpu.VMEM}
 
 
-def placed_call(kernel, inputs, in_spaces, outputs, out_spaces, scratch):
+def placed_call(kernel, inputs, in_spaces, outputs, out_spaces, scratch, aliases={}):
     specs, operands = [], []
     for value, space in zip(inputs, in_spaces, strict=True):
         if space == "s":
@@ -241,16 +232,17 @@
             if space != "-":
                 value = pltpu.with_memory_space_constraint(value, SPACES[space.lower()])
         operands.append(value)
-    shapes = [
-        jax.ShapeDtypeStruct(shape, jnp.float32) if space == "-" else SPACES[space](shape, jnp.float32)
-        for shape, space in zip(outputs, out_spaces, strict=True)
-    ]
+    shapes = []
+    for shape, space in zip(outputs, out_spaces, strict=True):
+        shape, kind = (shape, jnp.float32) if isinstance(shape, tuple) else (shape.shape, shape.dtype)
+        shapes.append(jax.ShapeDtypeStruct(shape, kind) if space == "-" else SPACES[space](shape, kind))
     return pl.pallas_call(
         kernel,
         out_shape=shapes,
         in_specs=specs,
         out_specs=[pl.BlockSpec(memory_space=pltpu.VMEM)] * len(shapes),
         scratch_shapes=scratch,
+        input_output_aliases=aliases,
         compiler_params=pltpu.CompilerParams(vmem_limit_bytes=GRANT),
     )(*operands)
 
@@ -404,8 +396,8 @@
                 out[target * size_g + g, :, p * LANES : (p + 1) * LANES] = piece
 
 
-def gravity_kernel(planes, table, fields, momentum_in, energy_in, potential, momentum, energy, solved, edges):
-    _, nx, ny, nz = fields.shape
+def gravity_kernel(planes, table, den, vel, carried, potential, momentum, energy, solved, edges):
+    nx, ny, nz = den.shape
     groups, kz, width = planes.shape
     main = nx * ny
     flat = planes[...].reshape(groups * kz, width)
@@ -426,16 +418,16 @@
         at = 2 * ny + x
         right = jnp.where(row == ny - 1, edges[at + nx : at + nx + 1], pltpu.roll(value, ny - 1, 0))
         left = jnp.where(row == 0, edges[at : at + 1], pltpu.roll(value, 1, 0))
-        pull = time_step * fields[0, x]
+        pull = time_step * den[x]
         kicks = [
             pull * (-0.5 * (above - below)),
             pull * (-0.5 * (right - left)),
             pull * solved[x * ny : (x + 1) * ny, nz:],
         ]
-        work = energy_in[x]
+        work = carried[3, x]
         for d in range(3):
-            momentum[d, x] = momentum_in[d, x] + kicks[d]
-            work = work + kicks[d] * fields[V_AT + d, x]
+            momentum[d, x] = carried[d, x] + kicks[d]
+            work = work + kicks[d] * vel[d, x]
         energy[x] = work
 
 
@@ -467,45 +459,28 @@
     flat_table = jnp.asarray(flat_mode_table(nx, all_x, all_y, all_z))
 
     floats = functools.partial(pltpu.VMEM, dtype=jnp.float32)
-    gas = (density, velocity, pressure, species, newton_count)
-
-    spectral, xlo, xhi = placed_call(
+
+    spectral, xlo, xhi, den, vel, pre, spe, cnt = placed_call(
         first_kernel,
-        (parts, *gas, into_z),
+        (parts, density, velocity, pressure, species, newton_count, into_z),
         "shhhhhh",
-        [(all_z, main), (prim_n, ny, nz), (prim_n, ny, nz)],
+        [(all_z, main), (prim_n, ny, nz), (prim_n, ny, nz)]
+        + [density.shape, velocity.shape, pressure.shape, species.shape, newton_count],
         OUT_FIRST,
-        [
-            floats((nx, ny, nz)),
-            floats((3, 2, ny, nz)),
-            floats((2, ny, nz)),
-            floats((species_n, 2, ny, nz)),
-            pltpu.VMEM((2, ny, nz), jnp.int32),
-            floats((all_z, nz)),
-            pltpu.SemaphoreType.DMA((10,)),
-        ],
+        [floats((all_z, nz)), pltpu.SemaphoreType.DMA((6,))],
     )
     xbelow = shifted(xhi, "hx", 1)
     xabove = shifted(xlo, "hx", -1)
-    spectral = lax.all_to_all(
-        spectral.reshape(groups, kz, main), ("hy", "ga"), split_axis=0, concat_axis=0, tiled=True
-    )
-    fields, ylo, yhi, zface, own_y, own_decay, own_z, own_flat = placed_call(
+    spectral = lax.all_to_all(spectral.reshape(groups, kz, main), ("hy", "ga"), split_axis=0, concat_axis=0, tiled=True)
+    cooled, dense, sound, ylo, yhi, zface, own_y, own_decay, own_flat = placed_call(
         pack_kernel,
-        (parts, *gas, table_y, tables, from_z, flat_table),
-        "shhhhhhhhh",
-        [(field_n, nx, ny, nz)] + [(prim_n, nx, nz)] * 2 + [(nx, ny, LANES)]
-        + [table_y.shape, (3, kz, all_y), from_z.shape[1:], flat_table.shape],
+        (parts, den, vel, pre, spe, cnt, table_y, tables, flat_table),
+        "svvvvvhhh",
+        [pre.shape, spe.shape, pre.shape] + [(prim_n, nx, nz)] * 2 + [(nx, ny, LANES)]
+        + [table_y.shape, (3, kz, all_y), flat_table.shape],
         OUT_PACK,
-        [
-            floats((nx, ny, nz)),
-            floats((3, nx, ny, nz)),
-            floats((nx, ny, nz)),
-            floats((species_n, nx, ny, nz)),
-            pltpu.VMEM((nx, ny, nz), jnp.int32),
-            pltpu.SemaphoreType.DMA((5, nx)),
-            pltpu.SemaphoreType.DMA((4,)),
-        ],
+        [pltpu.SemaphoreType.DMA((3,))],
+        {3: 0, 4: 1},
     )
     modes, sums = placed_call(
         functools.partial(along_y_kernel, size_g, ny),
@@ -525,21 +500,25 @@
         (parts, modes, sums, *others, own_y, own_decay, own_flat),
         "sv-" + IN_OTHERS * (size_x - 1) + "vvv",
         [(groups, kz, width)],
-        "-",
-        [floats((all_x, all_y)), floats(((nx + 2) * kz, all_y)), floats(((nx + 2) * kz, all_y))],
+        OUT_X,
+        [
+            floats((all_x, all_y)),
+            floats(((nx + 2) * kz, all_y)),
+            floats(((nx + 2) * kz, all_y)),
+        ],
     )
     planes = lax.all_to_all(planes, ("hy", "ga"), split_axis=0, concat_axis=0, tiled=True)
-    new_density, momentum, total_energy, species_mass = placed_call(
+    new_density, carried, species_mass, own_z = placed_call(
         flux_kernel,
-        (fields, xbelow, xabove, ybelow, yabove, zbelow, zabove),
+        (parts, den, vel, cooled, dense, sound, xbelow, xabove, ybelow, yabove, zbelow, zabove, from_z),
         IN_FLUX,
-        [(nx, ny, nz), (3, nx, ny, nz), (nx, ny, nz), (species_n, nx, ny, nz)],
-        "-vv-",
-        [floats((2, field_n, ny, nz)), floats((2, field_n, nx, nz))],
+        [(nx, ny, nz), (4, nx, ny, nz), (species_n, nx, ny, nz), from_z.shape[1:]],
+        "-v-v",
+        [floats((2, prim_n, ny, nz)), floats((2, prim_n + 5, nx, nz)), pltpu.SemaphoreType.DMA((3,))],
     )
     potential, momentum, total_energy = placed_call(
         gravity_kernel,
-        (planes, own_z, fields, momentum, total_energy),
+        (planes, own_z, den, vel, carried),
         IN_GRAVITY,
         [(nx, ny, nz), (3, nx, ny, nz), (nx, ny, nz)],
         "---",

time: 51.7 us -> 49.3 us (0.954)
  local copies, waits for them, and re-layouts: 2.92 us -> 0.69 us
  Pallas kernels: 16.3 us -> 14.9 us
  waiting for transfers between devices: 9.62 us -> 10.9 us
    unnamed x18 -> x10, local copies, waits for them, and re-layouts: 2.92 us -> 0.69 us
    pallas_call x6, Pallas kernels: 16.3 us -> 14.9 us  [placed_call(): pl.pallas_call(kernel, out_shape=shapes, in_specs=specs, out_specs=[pl.Bl...]
    all_to_all x1, waiting for transfers between devices: 1.5 us -> 2.79 us  [step(): lax.all_to_all(spectral.reshape(groups, kz, main), ('hy', 'ga'), split_ax...]
  transfers between devices with their start and end apart: 10 -> 10, of which waited for: 9 -> 8; matrix products, arithmetic and copies ran while one was open for 0% -> 0% of each run, Pallas kernels for 19% -> 16%
where the time goes in v5:
time: 49.3 us; the launch traced here: 49 us
  starting transfers between devices  21.7 us (44%)
  Pallas kernels  14.9 us (30%)
  waiting for transfers between devices  10.9 us (22%)
  between operations  0.72 us (1%)
  local copies, waits for them, and re-layouts  0.69 us (1%)
    pallas_call x6, Pallas kernels, placed_call(): pl.pallas_call(kernel, out_shape=shapes, in_specs=specs, out_specs=[pl.Bl...  14.9 us
    ppermute x8, starting transfers between devices, shifted(): lax.ppermute(value, axis, [(i, (i + step) % count) for i in range(count)])  13.1 us
    ppermute x8, waiting for transfers between devices, shifted(): lax.ppermute(value, axis, [(i, (i + step) % count) for i in range(count)])  8.12 us
    all_to_all x1, starting transfers between devices, step(): lax.all_to_all(spectral.reshape(groups, kz, main), ('hy', 'ga'), split_ax...  5.21 us
    all_to_all x1, starting transfers between devices, step(): lax.all_to_all(planes, ('hy', 'ga'), split_axis=0, concat_axis=0, tiled=T...  3.45 us
    all_to_all x1, waiting for transfers between devices, step(): lax.all_to_all(spectral.reshape(groups, kz, main), ('hy', 'ga'), split_ax...  2.79 us
  transfers between devices with their start and end apart: 10, of which 8 were waited for; matrix products, arithmetic and copies ran while one was open for 0% of the time, Pallas kernels for 16%

profile of v5, /device:TPU:0, one launch (start us, length us, event | category | flops | bytes accessed | tf_op | source)
XLA Modules:
  0.0 49.0 jit_solution(10371765775279095085)
XLA Ops:
  0.6 0.1 pad_add_fusion.part.parts
  0.7 2.9 %shard_map.137 = (f32[256,256]{1,0:T(8,128)}, f32[14,32,128]{2,1,0:T(8,128)S(1)}, f32[14,32,128]{2,1,0:T(8,128)S(1)}, f32[8,32,128]{2,1,0:T(8,128)S(1)}, f32[3,8...) custom-call(s32[2]{0:T(128)S(1)} %pad_add_fusion.part.parts, ...), custom_call_target="tpu_custom_call" | custom-call | tf_op jit(solution)/shard_map/pallas_call | solution.py:239
  3.6 5.2 %all-to-all-start = ((f32[8,32,256]{2,1,0:T(8,128)}), f32[8,32,256]{2,1,0:T(8,128)S(1)}, u32[]{:S(2)}, u32[]{:S(2)}) async-start(f32[8,32,256]{2,1,0:T(8,128)} %bitcast.2), calls=%async_computation | async-start | bytes 524288 | tf_op jit(solution)/shard_map/all_to_all | solution.py:474
  8.9 3.2 %shard_map.138 = (f32[8,32,128]{2,1,0:T(8,128)S(1)}, f32[9,8,32,128]{3,2,1,0:T(8,128)S(1)}, f32[8,32,128]{2,1,0:T(8,128)S(1)}, f32[14,8,128]{2,1,0:T(8,128)}, f3...) custom-call(s32[2]{0:T(128)S(1)} %pad_add_fusion.part.parts, ...), custom_call_target="tpu_custom_call", output_to_operand_aliasing={{0}: (3, {}), {1}: (4, {})} | custom-call | tf_op jit(solution)/shard_map/pallas_call | solution.py:239
  12.0 0.0 copy-start.2
  12.0 0.0 copy-start.4
  12.1 0.0 copy-start.3
  12.1 2.8 %all-to-all-done.lines = f32[8,32,256]{2,1,0:T(8,128)S(1)} async-done(((f32[8,32,256]{2,1,0:T(8,128)}), f32[8,32,256]{2,1,0:T(8,128)S(1)}, u32[]{:S(2)}, u32[]{:S(2)}) %all-to-all-start) | async-done | bytes 262176 | tf_op jit(solution)/shard_map/all_to_all | solution.py:474
  14.9 0.4 shard_map.140
  15.3 1.6 %collective-permute-start.5 = (f32[72,128]{1,0:T(8,128)S(1)}, f32[72,128]{1,0:T(8,128)S(1)}, u32[]{:S(2)}, u32[]{:S(2)}) collective-permute-start(f32[72,128]{1,0:T(8,128)S(1)} %get-tuple-element.49.own), channel_id=1, source_target_pairs={{0,8},{8,16},{16,24},{24,0},{1,9},{9,17},{17,25},{25,1},{2,10},{10... | collective-permute-start | bytes 110600 | tf_op jit(solution)/shard_map/ppermute | solution.py:252
  16.9 2.6 %collective-permute-start.6 = (f32[72,128]{1,0:T(8,128)S(1)}, f32[72,128]{1,0:T(8,128)S(1)}, u32[]{:S(2)}, u32[]{:S(2)}) collective-permute-start(f32[72,128]{1,0:T(8,128)S(1)} %get-tuple-element.49.own), channel_id=1, source_target_pairs={{0,16},{8,24},{16,0},{24,8},{1,17},{9,25},{17,1},{25,9},{2,18},{10... | collective-permute-start | bytes 110600 | tf_op jit(solution)/shard_map/ppermute | solution.py:252
  19.5 1.3 %collective-permute-start.7 = (f32[72,128]{1,0:T(8,128)S(1)}, f32[72,128]{1,0:T(8,128)S(1)}, u32[]{:S(2)}, u32[]{:S(2)}) collective-permute-start(f32[72,128]{1,0:T(8,128)S(1)} %get-tuple-element.49.own), channel_id=1, source_target_pairs={{0,24},{8,0},{16,8},{24,16},{1,25},{9,1},{17,9},{25,17},{2,26},{10... | collective-permute-start | bytes 110600 | tf_op jit(solution)/shard_map/ppermute | solution.py:252
  20.8 0.2 collective-permute-done.5.rest_0_
  21.1 1.3 %collective-permute-done.6.rest_1_ = f32[72,128]{1,0:T(8,128)S(1)} collective-permute-done((f32[72,128]{1,0:T(8,128)S(1)}, f32[72,128]{1,0:T(8,128)S(1)}, u32[]{:S(2)}, u32[]{:S(2)}) %collective-permute-start.6) | collective-permute-done | bytes 36896 | tf_op jit(solution)/shard_map/ppermute | solution.py:252
  22.4 1.0 %collective-permute-done.7.rest_2_ = f32[72,128]{1,0:T(8,128)S(1)} collective-permute-done((f32[72,128]{1,0:T(8,128)S(1)}, f32[72,128]{1,0:T(8,128)S(1)}, u32[]{:S(2)}, u32[]{:S(2)}) %collective-permute-start.7) | collective-permute-done | bytes 36896 | tf_op jit(solution)/shard_map/ppermute | solution.py:252
  23.4 2.2 %shard_map.141 = f32[8,32,384]{2,1,0:T(8,128)} custom-call(s32[2]{0:T(128)S(1)} %pad_add_fusion.part.parts, f32[8,32,128]{2,1,0:T(8,128)S(1)} %get-tuple-element.48.modes, f32[72,128]{1,0:T(8,128)S(1)} %get-tuple-element.49.own, f32[72,128]{1,0:T(8,128)S(1)} %collective-permute-done.5.rest_0_, f32[72,128]{1,0:T(8,128)S(1)} %collective-permute-done.6.rest_1_, ...), custom_call_target="tpu_custom_call" | custom-call | tf_op jit(solution)/shard_map/pallas_call | solution.py:239
  25.6 3.5 %all-to-all-start.1 = ((f32[8,32,384]{2,1,0:T(8,128)}), f32[8,32,384]{2,1,0:T(8,128)S(1)}, u32[]{:S(2)}, u32[]{:S(2)}) async-start(f32[8,32,384]{2,1,0:T(8,128)} %shard_map.141), calls=%async_computation.1 | async-start | bytes 786432 | tf_op jit(solution)/shard_map/all_to_all | solution.py:510
  29.1 0.5 %collective-permute-start = (f32[14,32,128]{2,1,0:T(8,128)S(1)}, f32[14,32,128]{2,1,0:T(8,128)S(1)}, u32[]{:S(2)}, u32[]{:S(2)}) collective-permute-start(f32[14,32,128]{2,1,0:T(8,128)S(1)} %get-tuple-element.39), channel_id=1, source_target_pairs={{0,8},{8,16},{16,24},{24,0},{1,9},{9,17},{17,25},{25,1},{2,10},{10... | collective-permute-start | bytes 688136 | tf_op jit(solution)/shard_map/ppermute | solution.py:252
  29.6 3.4 %collective-permute-start.1 = (f32[14,32,128]{2,1,0:T(8,128)S(1)}, f32[14,32,128]{2,1,0:T(8,128)S(1)}, u32[]{:S(2)}, u32[]{:S(2)}) collective-permute-start(f32[14,32,128]{2,1,0:T(8,128)S(1)} %get-tuple-element.40), channel_id=1, source_target_pairs={{0,24},{8,0},{16,8},{24,16},{1,25},{9,1},{17,9},{25,17},{2,26},{10... | collective-permute-start | bytes 688136 | tf_op jit(solution)/shard_map/ppermute | solution.py:252
  32.9 0.0 copy-done.2
  32.9 1.9 %collective-permute-start.4 = (f32[8,32,128]{2,1,0:T(8,128)S(1)}, f32[8,32,128]{2,1,0:T(8,128)S(1)}, u32[]{:S(2)}, u32[]{:S(2)}) collective-permute-start(f32[8,32,128]{2,1,0:T(8,128)S(1)} %copy-done.2), channel_id=1, source_target_pairs={{0,1},{1,0},{2,3},{3,2},{4,5},{5,4},{6,7},{7,6},{8,9},{9,8},{10,11... | collective-permute-start | bytes 393224 | tf_op jit(solution)/shard_map/ppermute | solution.py:252
  34.8 0.0 copy-done.4
  34.8 0.0 collective-permute-start.2
  34.8 0.0 copy-done.3
  34.8 1.7 %collective-permute-start.3 = (f32[14,8,128]{2,1,0:T(8,128)S(1)}, f32[14,8,128]{2,1,0:T(8,128)S(1)}, u32[]{:S(2)}, u32[]{:S(2)}) collective-permute-start(f32[14,8,128]{2,1,0:T(8,128)S(1)} %copy-done.3), channel_id=1, source_target_pairs={{0,6},{2,0},{4,2},{6,4},{1,7},{3,1},{5,3},{7,5},{8,14},{10,8},{12,... | collective-permute-start | bytes 172040 | tf_op jit(solution)/shard_map/ppermute | solution.py:252
  36.6 1.9 %collective-permute-done.2.ybelow = f32[14,8,128]{2,1,0:T(8,128)S(1)} collective-permute-done((f32[14,8,128]{2,1,0:T(8,128)S(1)}, f32[14,8,128]{2,1,0:T(8,128)S(1)}, u32[]{:S(2)}, u32[]{:S(2)}) %collective-permute-start.2) | collective-permute-done | bytes 57376 | tf_op jit(solution)/shard_map/ppermute | solution.py:252
  38.4 0.0 collective-permute-done.3.yabove
  38.4 0.8 %collective-permute-done.4.zbelow.zabove = f32[8,32,128]{2,1,0:T(8,128)S(1)} collective-permute-done((f32[8,32,128]{2,1,0:T(8,128)S(1)}, f32[8,32,128]{2,1,0:T(8,128)S(1)}, u32[]{:S(2)}, u32[]{:S(2)}) %collective-permute-start.4) | collective-permute-done | bytes 131104 | tf_op jit(solution)/shard_map/ppermute | solution.py:252
  39.2 0.3 collective-permute-done.xbelow
  39.4 0.0 copy-start
  39.4 2.6 %collective-permute-done.1.xabove = f32[14,32,128]{2,1,0:T(8,128)S(1)} collective-permute-done((f32[14,32,128]{2,1,0:T(8,128)S(1)}, f32[14,32,128]{2,1,0:T(8,128)S(1)}, u32[]{:S(2)}, u32[]{:S(2)}) %collective-permute-start.1) | collective-permute-done | bytes 229408 | tf_op jit(solution)/shard_map/ppermute | solution.py:252
  42.1 0.0 copy-start.1
  42.1 0.0 copy-done
  42.1 0.7 %copy-done.1 = f32[14,32,128]{2,1,0:T(8,128)} copy-done((f32[14,32,128]{2,1,0:T(8,128)}, f32[14,32,128]{2,1,0:T(8,128)S(1)}, u32[]{:S(2)}) %copy-start.1) | copy-done | bytes 229400
  42.7 4.8 %shard_map.139 = (f32[8,32,128]{2,1,0:T(8,128)}, f32[4,8,32,128]{3,2,1,0:T(8,128)S(1)}, f32[9,8,32,128]{3,2,1,0:T(8,128)}, f32[256,256]{1,0:T(8,128)S(1)}) custom-call(s32[2]{0:T(128)S(1)} %pad_add_fusion.part.parts, f32[8,32,128]{2,1,0:T(8,128)S(1)} %get-tuple-element.31.den, f32[3,8,32,128]{3,2,1,0:T(8,128)S(1)} %get-tuple-element.32.vel, ...), custom_call_target="tpu_custom_call" | custom-call | tf_op jit(solution)/shard_map/pallas_call | solution.py:239
  47.6 0.0 all-to-all-done.1.planes
  47.6 1.4 %shard_map.142 = (f32[8,32,128]{2,1,0:T(8,128)}, f32[3,8,32,128]{3,2,1,0:T(8,128)}, f32[8,32,128]{2,1,0:T(8,128)}) custom-call(f32[8,32,384]{2,1,0:T(8,128)S(1)} %all-to-all-done.1.planes, f32[256,256]{1,0:T(8,128)S(1)} %get-tuple-element.51.table, f32[8,32,128]{2,1,0:T(8,128)S(1)} %get-tuple-element.31.den, f32[3,8,32,128]{3,2,1,0:T(8,128)S(1)} %get-tuple-element.32.vel, ...), custom_call_target="tpu_custom_call" | custom-call | tf_op jit(solution)/shard_map/pallas_call | solution.py:239
Async XLA Ops:
  3.6 11.2 %all-to-all-start = ((f32[8,32,256]{2,1,0:T(8,128)}), f32[8,32,256]{2,1,0:T(8,128)S(1)}, u32[]{:S(2)}, u32[]{:S(2)}) async-start(f32[8,32,256]{2,1,0:T(8,128)} %bitcast.2), calls=%async_computation | async-start | bytes 524288 | tf_op jit(solution)/shard_map/all_to_all | solution.py:474
  12.0 20.9 %copy-start.2 = (f32[8,32,128]{2,1,0:T(8,128)S(1)}, f32[8,32,128]{2,1,0:T(8,128)}, u32[]{:S(2)}) copy-start(f32[8,32,128]{2,1,0:T(8,128)} %get-tuple-element.43) | copy-start | bytes 393220
  12.0 22.8 %copy-start.4 = (f32[14,8,128]{2,1,0:T(8,128)S(1)}, f32[14,8,128]{2,1,0:T(8,128)}, u32[]{:S(2)}) copy-start(f32[14,8,128]{2,1,0:T(8,128)} %get-tuple-element.41) | copy-start | bytes 172036
  12.1 22.7 %copy-start.3 = (f32[14,8,128]{2,1,0:T(8,128)S(1)}, f32[14,8,128]{2,1,0:T(8,128)}, u32[]{:S(2)}) copy-start(f32[14,8,128]{2,1,0:T(8,128)} %get-tuple-element.42) | copy-start | bytes 172036
  15.3 5.8 %collective-permute-start.5 = (f32[72,128]{1,0:T(8,128)S(1)}, f32[72,128]{1,0:T(8,128)S(1)}, u32[]{:S(2)}, u32[]{:S(2)}) collective-permute-start(f32[72,128]{1,0:T(8,128)S(1)} %get-tuple-element.49.own), channel_id=1, source_target_pairs={{0,8},{8,16},{16,24},{24,0},{1,9},{9,17},{17,25},{25,1},{2,10},{10... | collective-permute-start | bytes 110600 | tf_op jit(solution)/shard_map/ppermute | solution.py:252
  16.9 5.5 %collective-permute-start.6 = (f32[72,128]{1,0:T(8,128)S(1)}, f32[72,128]{1,0:T(8,128)S(1)}, u32[]{:S(2)}, u32[]{:S(2)}) collective-permute-start(f32[72,128]{1,0:T(8,128)S(1)} %get-tuple-element.49.own), channel_id=1, source_target_pairs={{0,16},{8,24},{16,0},{24,8},{1,17},{9,25},{17,1},{25,9},{2,18},{10... | collective-permute-start | bytes 110600 | tf_op jit(solution)/shard_map/ppermute | solution.py:252
  19.5 4.0 %collective-permute-start.7 = (f32[72,128]{1,0:T(8,128)S(1)}, f32[72,128]{1,0:T(8,128)S(1)}, u32[]{:S(2)}, u32[]{:S(2)}) collective-permute-start(f32[72,128]{1,0:T(8,128)S(1)} %get-tuple-element.49.own), channel_id=1, source_target_pairs={{0,24},{8,0},{16,8},{24,16},{1,25},{9,1},{17,9},{25,17},{2,26},{10... | collective-permute-start | bytes 110600 | tf_op jit(solution)/shard_map/ppermute | solution.py:252
  25.6 22.0 %all-to-all-start.1 = ((f32[8,32,384]{2,1,0:T(8,128)}), f32[8,32,384]{2,1,0:T(8,128)S(1)}, u32[]{:S(2)}, u32[]{:S(2)}) async-start(f32[8,32,384]{2,1,0:T(8,128)} %shard_map.141), calls=%async_computation.1 | async-start | bytes 786432 | tf_op jit(solution)/shard_map/all_to_all | solution.py:510
  29.1 10.4 %collective-permute-start = (f32[14,32,128]{2,1,0:T(8,128)S(1)}, f32[14,32,128]{2,1,0:T(8,128)S(1)}, u32[]{:S(2)}, u32[]{:S(2)}) collective-permute-start(f32[14,32,128]{2,1,0:T(8,128)S(1)} %get-tuple-element.39), channel_id=1, source_target_pairs={{0,8},{8,16},{16,24},{24,0},{1,9},{9,17},{17,25},{25,1},{2,10},{10... | collective-permute-start | bytes 688136 | tf_op jit(solution)/shard_map/ppermute | solution.py:252
  29.6 12.5 %collective-permute-start.1 = (f32[14,32,128]{2,1,0:T(8,128)S(1)}, f32[14,32,128]{2,1,0:T(8,128)S(1)}, u32[]{:S(2)}, u32[]{:S(2)}) collective-permute-start(f32[14,32,128]{2,1,0:T(8,128)S(1)} %get-tuple-element.40), channel_id=1, source_target_pairs={{0,24},{8,0},{16,8},{24,16},{1,25},{9,1},{17,9},{25,17},{2,26},{10... | collective-permute-start | bytes 688136 | tf_op jit(solution)/shard_map/ppermute | solution.py:252
  32.9 6.2 %collective-permute-start.4 = (f32[8,32,128]{2,1,0:T(8,128)S(1)}, f32[8,32,128]{2,1,0:T(8,128)S(1)}, u32[]{:S(2)}, u32[]{:S(2)}) collective-permute-start(f32[8,32,128]{2,1,0:T(8,128)S(1)} %copy-done.2), channel_id=1, source_target_pairs={{0,1},{1,0},{2,3},{3,2},{4,5},{5,4},{6,7},{7,6},{8,9},{9,8},{10,11... | collective-permute-start | bytes 393224 | tf_op jit(solution)/shard_map/ppermute | solution.py:252
  34.8 3.6 %collective-permute-start.2 = (f32[14,8,128]{2,1,0:T(8,128)S(1)}, f32[14,8,128]{2,1,0:T(8,128)S(1)}, u32[]{:S(2)}, u32[]{:S(2)}) collective-permute-start(f32[14,8,128]{2,1,0:T(8,128)S(1)} %copy-done.4), channel_id=1, source_target_pairs={{0,2},{2,4},{4,6},{6,0},{1,3},{3,5},{5,7},{7,1},{8,10},{10,12},{12... | collective-permute-start | bytes 172040 | tf_op jit(solution)/shard_map/ppermute | solution.py:252
  34.8 3.6 %collective-permute-start.3 = (f32[14,8,128]{2,1,0:T(8,128)S(1)}, f32[14,8,128]{2,1,0:T(8,128)S(1)}, u32[]{:S(2)}, u32[]{:S(2)}) collective-permute-start(f32[14,8,128]{2,1,0:T(8,128)S(1)} %copy-done.3), channel_id=1, source_target_pairs={{0,6},{2,0},{4,2},{6,4},{1,7},{3,1},{5,3},{7,5},{8,14},{10,8},{12,... | collective-permute-start | bytes 172040 | tf_op jit(solution)/shard_map/ppermute | solution.py:252
  39.4 2.6 %copy-start = (f32[14,32,128]{2,1,0:T(8,128)}, f32[14,32,128]{2,1,0:T(8,128)S(1)}, u32[]{:S(2)}) copy-start(f32[14,32,128]{2,1,0:T(8,128)S(1)} %collective-permute-done.xbelow) | copy-start | bytes 688132
  42.1 0.7 %copy-start.1 = (f32[14,32,128]{2,1,0:T(8,128)}, f32[14,32,128]{2,1,0:T(8,128)S(1)}, u32[]{:S(2)}) copy-start(f32[14,32,128]{2,1,0:T(8,128)S(1)} %collective-permute-done.1.xabove) | copy-start | bytes 688132

commit v6 on v5

--- a/solution.py
+++ b/solution.py
@@ -20,18 +20,20 @@
 highest = lax.Precision.HIGHEST
 LANES = 128
 GRANT = 16 * 2**20
-OUT_FIRST = "vvvvvvvv"
-OUT_PACK = "vvvhhhvvv"
+OUT_FIRST = "vvvvvv"
+OUT_PACK = "vvvhhhhhvvv"
 IN_Y = "-vv"
 OUT_Y = "v-"
 IN_OTHERS = "-"
 OUT_X = "h"
-IN_FLUX = "svvvvvhhvvvvh"
-IN_GRAVITY = "-vvvv"
+IN_FLUX = "vvvvvvvvvh"
+OUT_FLUX = "xxvvv"
+IN_RIM = "vvvvvvhhhh"
+OUT_RIM = "xxv"
+IN_GRAVITY = "-vvvvv"
 P_AT = 4
 C_AT = prim_n
 face_n = prim_n + 3
-HIGH_FACE = 64
 
 
 def sound_speed(density, pressure):
@@ -75,45 +77,53 @@
     return [density, vel[0, x], vel[1, x], vel[2, x], pressure] + [density * s for s in species]
 
 
-def first_kernel(part, den, vel, pre, spe, cnt, table, spectral, xlo, xhi,
+def place_in_plane():
+    in_g = lax.axis_index("ga")
+    return in_g, lax.axis_index("hy") * lax.axis_size("ga") + in_g
+
+
+def first_kernel(den, vel, pre, spe, cnt, table, spectral,
                  den_in, vel_in, pre_in, spe_in, cnt_in, table_in, semaphores):
     nx, ny, nz = den.shape
-    copies = copies_in(
-        [(den, den_in), (table.at[part[0]], table_in), (pre, pre_in), (cnt, cnt_in), (spe, spe_in), (vel, vel_in)],
-        semaphores,
-    )
-    copies[0].wait()
-    copies[1].wait()
+    in_g, _ = place_in_plane()
+    needed = copies_in([(den, den_in), (table.at[in_g], table_in)], semaphores.at[0])
+    copies = copies_in([(pre, pre_in), (cnt, cnt_in), (spe, spe_in), (vel, vel_in)], semaphores.at[1])
+    for copy in needed:
+        copy.wait()
     spectral[...] = lax.dot_general(
         table_in[...], den_in[...].reshape(nx * ny, nz), (((1,), (1,)), ((), ())),
         precision=highest, preferred_element_type=jnp.float32,
     )
-    for copy in copies[2:]:
+    for copy in copies:
         copy.wait()
-    for x, face in ((0, xlo), (nx - 1, xhi)):
-        for c, value in enumerate(primitive_plane(x, den_in, vel_in, pre_in, spe_in, cnt_in)):
-            face[c] = value
-
-
-def pack_kernel(parts, den, vel, pre, spe, cnt, table_y, tables, flat_table,
-                cooled, mass, sound, ylo, yhi, zface, own_y, own_decay, own_flat, semaphores):
+
+
+def pack_kernel(den, vel, pre, spe, cnt, table_y, tables, flat_table,
+                cooled, mass, sound, xfirst, xlast, ylo, yhi, zface, own_y, own_decay, own_flat, semaphores):
     nx, ny, nz = den.shape
     kz = own_decay.shape[1]
+    _, place = place_in_plane()
     lane = lax.broadcasted_iota(jnp.int32, (ny, LANES), 1)
     later = copies_in(
         [
             (table_y, own_y),
-            (tables.at[:, pl.ds(parts[1] * kz, kz), :], own_decay),
+            (tables.at[:, pl.ds(place * kz, kz), :], own_decay),
             (flat_table, own_flat),
         ],
         semaphores,
     )
 
+    second, _ = face_roles("hx")
+
     def plane(x, _):
         primitive = primitive_plane(x, den, vel, pre, spe, cnt)
-        for c in range(prim_n):
-            ylo[c, pl.ds(x, 1), :] = primitive[c][0:1, :]
-            yhi[c, pl.ds(x, 1), :] = primitive[c][ny - 1 : ny, :]
+        for at, face in (((nx - 1) * (1 - second), xfirst), ((nx - 1) * second, xlast)):
+
+            @pl.when(x == at)
+            def _():
+                for c in range(prim_n):
+                    face[c] = primitive[c]
+
         kept = primitive + [sound_speed(primitive[0], primitive[P_AT])]
         cooled[x] = kept[P_AT]
         for s in range(species_n):
@@ -122,38 +132,45 @@
         carried = conserved(kept) + [kept[P_AT], kept[C_AT], kept[3]]
         packed = jnp.zeros((ny, LANES), jnp.float32)
         for c in range(face_n):
-            first, last = carried[c][:, :LANES], carried[c][:, nz - LANES :]
-            packed = jnp.where(lane == c, pltpu.roll(first, c, 1) if c else first, packed)
-            packed = jnp.where(lane == HIGH_FACE + c, pltpu.roll(last, HIGH_FACE + c + 1, 1), packed)
+            packed = jnp.where(lane // 2 == c, pltpu.roll(carried[c], 2 * c + 1, 1), packed)
         zface[x] = packed
         return 0
 
     lax.fori_loop(0, nx, plane, 0)
+    kept = [den] + [vel.at[d] for d in range(3)] + [cooled] + [mass.at[s] for s in range(species_n)]
+    for c in range(prim_n):
+        rows = kept[c].reshape(nx * ny, nz)
+        ylo[c] = rows[pl.ds(0, nx, stride=ny), :]
+        yhi[c] = rows[pl.ds(ny - 1, nx, stride=ny), :]
     for copy in later:
         copy.wait()
 
 
-def flux_kernel(parts, den, vel, cooled, dense, speed_of, xbelow, xabove, ybelow, yabove, zbelow, zabove, from_z,
-                new_density, carried, mass, own_z, xfaces, yedge, semaphores):
+flow_p, flow_c, flow_v = prim_n, prim_n + 1, prim_n + 2
+flow_n = prim_n + 5
+
+
+def with_flow(kept):
+    return conserved(kept) + [kept[P_AT], kept[C_AT], kept[1], kept[2], kept[3]]
+
+
+def faced(face):
+    kept = [face[c] for c in range(prim_n)]
+    return with_flow(kept + [sound_speed(kept[0], kept[P_AT])])
+
+
+def stored(x, den, vel, cooled, dense, speed_of):
+    kept = [den[x], vel[0, x], vel[1, x], vel[2, x], cooled[x]]
+    return with_flow(kept + [dense[s, x] for s in range(species_n)] + [speed_of[x]])
+
+
+def flux_kernel(den, vel, cooled, dense, speed_of, ybelow, yabove, zbelow, zabove, from_z,
+                new_density, mass, carried, rim, own_z, ready, yedge, out_semaphores, semaphores):
     nx, ny, nz = den.shape
     row = lax.broadcasted_iota(jnp.int32, (ny, nz), 0)
     lane = lax.broadcasted_iota(jnp.int32, (ny, nz), 1)
-    copies = copies_in(
-        [(xbelow, xfaces.at[0]), (xabove, xfaces.at[1]), (from_z.at[parts[0]], own_z)], semaphores
-    )
-
-    def with_flow(kept):
-        return conserved(kept) + [kept[P_AT], kept[C_AT], kept[1], kept[2], kept[3]]
-
-    def stored(x):
-        kept = [den[x], vel[0, x], vel[1, x], vel[2, x], cooled[x]]
-        return with_flow(kept + [dense[s, x] for s in range(species_n)] + [speed_of[x]])
-
-    def faced(face):
-        kept = [face[c] for c in range(prim_n)]
-        return with_flow(kept + [sound_speed(kept[0], kept[P_AT])])
-
-    flow_p, flow_c, flow_v = prim_n, prim_n + 1, prim_n + 2
+    copies = copies_in([(from_z.at[place_in_plane()[0]], own_z)], semaphores)
+    state = (den, vel, cooled, dense, speed_of)
     for side, face in enumerate((ybelow, yabove)):
         for f, value in enumerate(faced(face)):
             yedge[side, f] = value
@@ -161,7 +178,7 @@
     def plane(x, lower, upper):
         from_below = zbelow[x]
         from_above = zabove[x]
-        centre = stored(x)
+        centre = stored(x, *state)
 
         def beside(f, direction, up):
             if direction == 0:
@@ -174,63 +191,113 @@
                 return jnp.where(row == 0, edge, pltpu.roll(here, 1, 0))
             slot = f if f < flow_v else flow_v
             if up:
-                edge = pltpu.roll(from_above, LANES - 1 - slot, 1)
+                edge = pltpu.roll(from_above, (LANES - 2 - 2 * slot) % LANES, 1)
                 return jnp.where(lane == nz - 1, edge, pltpu.roll(here, nz - 1, 1))
-            edge = pltpu.roll(from_below, LANES - HIGH_FACE - slot, 1)
+            edge = pltpu.roll(from_below, (LANES - 2 * slot) % LANES, 1)
             return jnp.where(lane == 0, edge, pltpu.roll(here, 1, 1))
 
-        stay = 1.0
-        above, below, push, work = [], [], [], 0.0
+        stay, work = 1.0, 0.0
+        weights, push = [], []
         for d in range(3):
             speed = jnp.abs(centre[flow_v + d]) + centre[flow_c]
-            v_up, v_lo = beside(flow_v + d, d, True), beside(flow_v + d, d, False)
-            p_up, p_lo = beside(flow_p, d, True), beside(flow_p, d, False)
-            s_up = jnp.maximum(speed, jnp.abs(v_up) + beside(flow_c, d, True))
-            s_lo = jnp.maximum(speed, jnp.abs(v_lo) + beside(flow_c, d, False))
-            stay = stay - half_step * (s_up + s_lo)
-            above.append(half_step * (s_up - v_up))
-            below.append(half_step * (s_lo + v_lo))
-            push.append(half_step * (p_lo - p_up))
-            work = work + half_step * (p_lo * v_lo - p_up * v_up)
+            pushed = 0.0
+            for up in (False, True):
+                if d == 0 and (upper if up else lower) is None:
+                    continue
+                sign = -1.0 if up else 1.0
+                v, p = beside(flow_v + d, d, up), beside(flow_p, d, up)
+                signal = jnp.maximum(speed, jnp.abs(v) + beside(flow_c, d, up))
+                stay = stay - half_step * signal
+                weights.append((d, up, half_step * (signal + sign * v)))
+                pushed = pushed + sign * half_step * p
+                work = work + sign * half_step * (p * v)
+            push.append(pushed)
 
         def updated(f):
             total = stay * centre[f]
-            for d in range(3):
-                total = total + above[d] * beside(f, d, True)
-                total = total + below[d] * beside(f, d, False)
+            for d, up, weight in weights:
+                total = total + weight * beside(f, d, up)
             return total
 
-        new_density[x] = updated(0)
+        result = [updated(f) for f in range(prim_n)]
         for d in range(3):
-            carried[d, x] = updated(1 + d) + push[d]
-        carried[3, x] = updated(4) + work
+            result[1 + d] = result[1 + d] + push[d]
+        result[4] = result[4] + work
+        return result
+
+    def leave(x):
+        return [
+            pltpu.make_async_copy(ready.at[0, x - 1], new_density.at[x], out_semaphores.at[0, x - 1]),
+            pltpu.make_async_copy(
+                ready.at[pl.ds(1, species_n), x - 1], mass.at[:, x], out_semaphores.at[1, x - 1]
+            ),
+        ]
+
+    def inner(x, _):
+        result = plane(x, stored(x - 1, *state), stored(x + 1, *state))
+        ready[0, x - 1] = result[0]
+        for d in range(4):
+            carried[d, x] = result[1 + d]
         for s in range(species_n):
-            mass[s, x] = updated(5 + s)
-
-    def inner(x, _):
-        plane(x, stored(x - 1), stored(x + 1))
+            ready[1 + s, x - 1] = result[5 + s]
+        for copy in leave(x):
+            copy.start()
         return 0
 
+    def left(x, _):
+        for copy in leave(x):
+            copy.wait()
+        return 0
+
     lax.fori_loop(1, nx - 1, inner, 0)
-    copies[0].wait()
-    plane(0, faced(xfaces.at[0]), stored(1))
-    copies[1].wait()
-    plane(nx - 1, stored(nx - 2), faced(xfaces.at[1]))
-    copies[2].wait()
-
-
-SPACES = {"h": pltpu.HBM, "v": pltpu.VMEM}
+    for f, value in enumerate(plane(0, None, stored(1, *state))):
+        rim[f, 0] = value
+    for f, value in enumerate(plane(nx - 1, stored(nx - 2, *state), None)):
+        rim[f, 1] = value
+    for copy in copies:
+        copy.wait()
+    lax.fori_loop(1, nx - 1, left, 0)
+
+
+def rim_kernel(den, vel, cooled, dense, speed_of, rim, xfirst, xlast, density_in, mass_in,
+               new_density, mass, carried_rim, xfaces, ready, semaphores, out_semaphores):
+    nx, _, _ = den.shape
+    _, slot = face_roles("hx")
+    copies = copies_in([(xfirst, xfaces.at[slot]), (xlast, xfaces.at[1 - slot])], semaphores)
+    for copy in copies:
+        copy.wait()
+    leaving = []
+    for n, (x, sign) in enumerate(((0, 1.0), (nx - 1, -1.0))):
+        centre = stored(x, den, vel, cooled, dense, speed_of)
+        other = faced(xfaces.at[n])
+        v, p = other[flow_v], other[flow_p]
+        signal = jnp.maximum(jnp.abs(centre[flow_v]) + centre[flow_c], jnp.abs(v) + other[flow_c])
+        lost, weight = half_step * signal, half_step * (signal + sign * v)
+        result = [rim[f, n] - lost * centre[f] + weight * other[f] for f in range(prim_n)]
+        result[1] = result[1] + sign * half_step * p
+        result[4] = result[4] + sign * half_step * (p * v)
+        ready[0, n] = result[0]
+        for d in range(4):
+            carried_rim[d, n] = result[1 + d]
+        for s in range(species_n):
+            ready[1 + s, n] = result[5 + s]
+        leaving += copies_in(
+            [(ready.at[0, n], new_density.at[x]), (ready.at[pl.ds(1, species_n), n], mass.at[:, x])],
+            out_semaphores.at[n],
+        )
+    for copy in leaving:
+        copy.wait()
+
+
+SPACES = {"h": pltpu.HBM, "v": pltpu.VMEM, "x": pltpu.HBM}
 
 
 def placed_call(kernel, inputs, in_spaces, outputs, out_spaces, scratch, aliases={}):
     specs, operands = [], []
     for value, space in zip(inputs, in_spaces, strict=True):
-        if space == "s":
-            specs.append(pl.BlockSpec(memory_space=pltpu.SMEM))
-        else:
-            specs.append(pl.BlockSpec(memory_space=pl.ANY if space == "h" else pltpu.VMEM))
-            if space != "-":
-                value = pltpu.with_memory_space_constraint(value, SPACES[space.lower()])
+        specs.append(pl.BlockSpec(memory_space=pl.ANY if space == "h" else pltpu.VMEM))
+        if space != "-":
+            value = pltpu.with_memory_space_constraint(value, SPACES[space])
         operands.append(value)
     shapes = []
     for shape, space in zip(outputs, out_spaces, strict=True):
@@ -240,11 +307,40 @@
         kernel,
         out_shape=shapes,
         in_specs=specs,
-        out_specs=[pl.BlockSpec(memory_space=pltpu.VMEM)] * len(shapes),
+        out_specs=[pl.BlockSpec(memory_space=pl.ANY if space == "x" else pltpu.VMEM) for space in out_spaces],
         scratch_shapes=scratch,
         input_output_aliases=aliases,
         compiler_params=pltpu.CompilerParams(vmem_limit_bytes=GRANT),
     )(*operands)
+
+
+def exchanged(value, axis, step):
+    count = lax.axis_size(axis)
+    return lax.ppermute(value, axis, [(i, partner(i, step, count)) for i in range(count)])
+
+
+def partner(index, step, count):
+    return index ^ step if count & (count - 1) == 0 else (index + step) % count
+
+
+def source_of(index, step, count):
+    return index ^ step if count & (count - 1) == 0 else lax.rem(index + count - step, count)
+
+
+def face_roles(axis):
+    if lax.axis_size(axis) % 2:
+        return 0, 0
+    second = lax.rem(lax.axis_index(axis), 2)
+    return second, 1 - second
+
+
+def faced_pairs(value, axis, first_round):
+    count = lax.axis_size(axis)
+    if count % 2:
+        return shifted(value, axis, 1 if first_round else -1)
+    start = 0 if first_round else 1
+    pairs = [((start + i) % count, (start + i + 1) % count) for i in range(0, count, 2)]
+    return lax.ppermute(value, axis, pairs + [(b, a) for a, b in pairs])
 
 
 def shifted(value, axis, step):
@@ -324,15 +420,22 @@
         sums[2 * kz + x : 2 * kz + x + 1] = modes[x, 0:1, :]
 
 
-def along_x_kernel(count, size_g, block, parts, modes, own, *rest):
+def along_x_kernel(count, size_g, block, modes, own, *rest):
     others = rest[: count - 1]
-    table_y, tables, flat_table, out, gathered, potential, lines = rest[count - 1 :]
+    table_y, tables, flat_table, out, everyone, gathered, potential, lines = rest[count - 1 :]
+    me = lax.axis_index("hx")
+    everyone[me] = own[...]
+    for step in range(1, count):
+        everyone[source_of(me, step, count)] = others[step - 1][...]
+
+    def seen(distance):
+        return everyone.at[lax.rem(me + count - distance, count)]
+
     nx, kz, ny = modes.shape
     width = block
     per = LANES // width
     for s in range(count):
-        seen = own if s == 0 else others[s - 1]
-        gathered[s * nx : (s + 1) * nx] = seen[2 * kz : 2 * kz + nx]
+        gathered[s * nx : (s + 1) * nx] = seen(s)[2 * kz : 2 * kz + nx]
     flat = jnp.dot(
         flat_table[...], gathered[...], precision=highest, preferred_element_type=jnp.float32
     )
@@ -345,8 +448,8 @@
         left = own[tile : tile + 8]
         right = own[kz + tile : kz + tile + 8]
         for s in range(count - 1, 0, -1):
-            left = left * far + others[s - 1][tile : tile + 8]
-            right = right * far + others[count - s - 1][kz + tile : kz + tile + 8]
+            left = left * far + seen(s)[tile : tile + 8]
+            right = right * far + seen(count - s)[kz + tile : kz + tile + 8]
         left, right = left * closing, right * closing
         from_left = [left]
         for x in range(nx):
@@ -360,7 +463,7 @@
         result[0] = from_left[0] + behind * decay
         if tile == 0:
             first = lax.broadcasted_iota(jnp.int32, (8, ny), 0) + lax.broadcasted_iota(jnp.int32, (8, ny), 1)
-            first = first + parts[1] == 0
+            first = first + place_in_plane()[1] == 0
         for x in range(nx + 2):
             value = result[x] * scale
             if tile == 0:
@@ -396,7 +499,7 @@
                 out[target * size_g + g, :, p * LANES : (p + 1) * LANES] = piece
 
 
-def gravity_kernel(planes, table, den, vel, carried, potential, momentum, energy, solved, edges):
+def gravity_kernel(planes, table, den, vel, carried, carried_rim, potential, momentum, energy, solved, edges):
     nx, ny, nz = den.shape
     groups, kz, width = planes.shape
     main = nx * ny
@@ -424,9 +527,10 @@
             pull * (-0.5 * (right - left)),
             pull * solved[x * ny : (x + 1) * ny, nz:],
         ]
-        work = carried[3, x]
+        before = [carried_rim[d, x // (nx - 1)] if x in (0, nx - 1) else carried[d, x] for d in range(4)]
+        work = before[3]
         for d in range(3):
-            momentum[d, x] = carried[d, x] + kicks[d]
+            momentum[d, x] = before[d] + kicks[d]
             work = work + kicks[d] * vel[d, x]
         energy[x] = work
 
@@ -437,9 +541,6 @@
     all_x, all_y, all_z = nx * size_x, ny * size_y, nz * size_g
     groups = size_y * size_g
     kz = all_z // groups
-    rank_g = lax.axis_index("ga").astype(jnp.int32)
-    rank = lax.axis_index("hy").astype(jnp.int32) * size_g + rank_g
-    parts = jnp.stack([rank_g, rank])
     main = nx * ny
     width = main + LANES
 
@@ -460,27 +561,24 @@
 
     floats = functools.partial(pltpu.VMEM, dtype=jnp.float32)
 
-    spectral, xlo, xhi, den, vel, pre, spe, cnt = placed_call(
+    spectral, den, vel, pre, spe, cnt = placed_call(
         first_kernel,
-        (parts, density, velocity, pressure, species, newton_count, into_z),
-        "shhhhhh",
-        [(all_z, main), (prim_n, ny, nz), (prim_n, ny, nz)]
-        + [density.shape, velocity.shape, pressure.shape, species.shape, newton_count],
+        (density, velocity, pressure, species, newton_count, into_z),
+        "hhhhhh",
+        [(all_z, main), density.shape, velocity.shape, pressure.shape, species.shape, newton_count],
         OUT_FIRST,
-        [floats((all_z, nz)), pltpu.SemaphoreType.DMA((6,))],
-    )
-    xbelow = shifted(xhi, "hx", 1)
-    xabove = shifted(xlo, "hx", -1)
+        [floats((all_z, nz)), pltpu.SemaphoreType.DMA((2, 4))],
+    )
     spectral = lax.all_to_all(spectral.reshape(groups, kz, main), ("hy", "ga"), split_axis=0, concat_axis=0, tiled=True)
-    cooled, dense, sound, ylo, yhi, zface, own_y, own_decay, own_flat = placed_call(
+    cooled, dense, sound, xfirst, xlast, ylo, yhi, zface, own_y, own_decay, own_flat = placed_call(
         pack_kernel,
-        (parts, den, vel, pre, spe, cnt, table_y, tables, flat_table),
-        "svvvvvhhh",
-        [pre.shape, spe.shape, pre.shape] + [(prim_n, nx, nz)] * 2 + [(nx, ny, LANES)]
+        (den, vel, pre, spe, cnt, table_y, tables, flat_table),
+        "vvvvvhhh",
+        [pre.shape, spe.shape, pre.shape] + [(prim_n, ny, nz)] * 2 + [(prim_n, nx, nz)] * 2 + [(nx, ny, LANES)]
         + [table_y.shape, (3, kz, all_y), flat_table.shape],
         OUT_PACK,
         [pltpu.SemaphoreType.DMA((3,))],
-        {3: 0, 4: 1},
+        {2: 0, 3: 1},
     )
     modes, sums = placed_call(
         functools.partial(along_y_kernel, size_g, ny),
@@ -490,35 +588,63 @@
         OUT_Y,
         [floats((nx * kz, all_y))],
     )
-    others = [shifted(sums, "hx", s) for s in range(1, size_x)]
+    others = []
+    for step in range(1, size_x):
+        others.append(exchanged(sums, "hx", step))
     ybelow = shifted(yhi, "hy", 1)
     yabove = shifted(ylo, "hy", -1)
     zbelow = shifted(zface, "ga", 1)
     zabove = zbelow if size_g == 2 else shifted(zface, "ga", -1)
+    xfirst = faced_pairs(xfirst, "hx", True)
+    xlast = faced_pairs(xlast, "hx", False)
     (planes,) = placed_call(
         functools.partial(along_x_kernel, size_x, size_g, ny),
-        (parts, modes, sums, *others, own_y, own_decay, own_flat),
-        "sv-" + IN_OTHERS * (size_x - 1) + "vvv",
+        (modes, sums, *others, own_y, own_decay, own_flat),
+        "v-" + IN_OTHERS * (size_x - 1) + "vvv",
         [(groups, kz, width)],
         OUT_X,
         [
+            floats((size_x, 2 * kz + nx, all_y)),
             floats((all_x, all_y)),
             floats(((nx + 2) * kz, all_y)),
             floats(((nx + 2) * kz, all_y)),
         ],
     )
     planes = lax.all_to_all(planes, ("hy", "ga"), split_axis=0, concat_axis=0, tiled=True)
-    new_density, carried, species_mass, own_z = placed_call(
+    state = (den, vel, cooled, dense, sound)
+    new_density, species_mass, carried, rim, own_z = placed_call(
         flux_kernel,
-        (parts, den, vel, cooled, dense, sound, xbelow, xabove, ybelow, yabove, zbelow, zabove, from_z),
+        (*state, ybelow, yabove, zbelow, zabove, from_z),
         IN_FLUX,
-        [(nx, ny, nz), (4, nx, ny, nz), (species_n, nx, ny, nz), from_z.shape[1:]],
-        "-v-v",
-        [floats((2, prim_n, ny, nz)), floats((2, prim_n + 5, nx, nz)), pltpu.SemaphoreType.DMA((3,))],
+        [
+            (nx, ny, nz), (species_n, nx, ny, nz), (4, nx, ny, nz),
+            (prim_n, 2, ny, nz), from_z.shape[1:],
+        ],
+        OUT_FLUX,
+        [
+            floats((1 + species_n, nx - 2, ny, nz)),
+            floats((2, flow_n, nx, nz)),
+            pltpu.SemaphoreType.DMA((2, nx - 2)),
+            pltpu.SemaphoreType.DMA((1,)),
+        ],
+    )
+    new_density, species_mass, carried_rim = placed_call(
+        rim_kernel,
+        (*state, rim, xfirst, xlast, new_density, species_mass),
+        IN_RIM,
+        [(nx, ny, nz), (species_n, nx, ny, nz), (4, 2, ny, nz)],
+        OUT_RIM,
+        [
+            floats((2, prim_n, ny, nz)),
+            floats((1 + species_n, 2, ny, nz)),
+            pltpu.SemaphoreType.DMA((2,)),
+            pltpu.SemaphoreType.DMA((2, 2)),
+        ],
+        {8: 0, 9: 1},
     )
     potential, momentum, total_energy = placed_call(
         gravity_kernel,
-        (planes, own_z, den, vel, carried),
+        (planes, own_z, den, vel, carried, carried_rim),
         IN_GRAVITY,
         [(nx, ny, nz), (3, nx, ny, nz), (nx, ny, nz)],
         "---",

time: 49.3 us -> 47.4 us (0.961)
  starting transfers between devices: 21.7 us -> 18.3 us
  waiting for transfers between devices: 10.9 us -> 13.8 us
  Pallas kernels: 14.9 us -> 13.4 us
    ppermute x8 -> x3, starting transfers between devices: 13.1 us -> 3.6 us  [shifted(): lax.ppermute(value, axis, [(i, (i + step) % count) for i in range(count)])]
    ppermute x0 -> x5, starting transfers between devices: none -> 6.03 us  [the longest x3 4.45 us: exchanged(): lax.ppermute(value, axis, [(i, partner(i, step, count)) for i in range(co...]
    ppermute x0 -> x5, waiting for transfers between devices: none -> 5.54 us  [the longest x3 5.53 us: exchanged(): lax.ppermute(value, axis, [(i, partner(i, step, count)) for i in range(co...]
    ppermute x8 -> x3, waiting for transfers between devices: 8.12 us -> 4.92 us  [shifted(): lax.ppermute(value, axis, [(i, (i + step) % count) for i in range(count)])]
    pallas_call x6 -> x7, Pallas kernels: 14.9 us -> 13.4 us  [placed_call(): pl.pallas_call(kernel, out_shape=shapes, in_specs=specs, out_specs=[pl.Bl...]
    all_to_all x1, waiting for transfers between devices: 2.79 us -> 3.29 us  [step(): lax.all_to_all(spectral.reshape(groups, kz, main), ('hy', 'ga'), split_ax...]
  transfers between devices with their start and end apart: 10 -> 10, of which waited for: 8 -> 5; matrix products, arithmetic and copies ran while one was open for 0% -> 0% of each run, Pallas kernels for 16% -> 16%
where the time goes in v6:
time: 47.4 us; the launch traced here: 47 us
  starting transfers between devices  18.3 us (39%)
  waiting for transfers between devices  13.8 us (29%)
  Pallas kernels  13.4 us (28%)
  between operations  0.78 us (2%)
  local copies, waits for them, and re-layouts  0.77 us (2%)
    pallas_call x7, Pallas kernels, placed_call(): pl.pallas_call(kernel, out_shape=shapes, in_specs=specs, out_specs=[pl.Bl...  13.4 us
    ppermute x3, waiting for transfers between devices, exchanged(): lax.ppermute(value, axis, [(i, partner(i, step, count)) for i in range(co...  5.53 us
    all_to_all x1, starting transfers between devices, step(): lax.all_to_all(spectral.reshape(groups, kz, main), ('hy', 'ga'), split_ax...  5.21 us
    ppermute x3, waiting for transfers between devices, shifted(): lax.ppermute(value, axis, [(i, (i + step) % count) for i in range(count)])  4.92 us
    ppermute x3, starting transfers between devices, exchanged(): lax.ppermute(value, axis, [(i, partner(i, step, count)) for i in range(co...  4.45 us
    ppermute x3, starting transfers between devices, shifted(): lax.ppermute(value, axis, [(i, (i + step) % count) for i in range(count)])  3.6 us
    all_to_all x1, starting transfers between devices, step(): lax.all_to_all(planes, ('hy', 'ga'), split_axis=0, concat_axis=0, tiled=T...  3.45 us
    all_to_all x1, waiting for transfers between devices, step(): lax.all_to_all(spectral.reshape(groups, kz, main), ('hy', 'ga'), split_ax...  3.29 us
  transfers between devices with their start and end apart: 10, of which 5 were waited for; matrix products, arithmetic and copies ran while one was open for 0% of the time, Pallas kernels for 16%

profile of v6, /device:TPU:0, one launch (start us, length us, event | category | flops | bytes accessed | tf_op | source)
XLA Modules:
  0.0 47.0 jit_solution(622809646550779890)
XLA Ops:
  0.6 2.4 %shard_map.137 = (f32[256,256]{1,0:T(8,128)}, f32[8,32,128]{2,1,0:T(8,128)S(1)}, f32[3,8,32,128]{3,2,1,0:T(8,128)S(1)}, f32[8,32,128]{2,1,0:T(8,128)S(1)}, f32[9...) custom-call(f32[8,32,128]{2,1,0:T(8,128)} %den.1, f32[3,8,32,128]{3,2,1,0:T(8,128)} %vel.1, f32[8,32,128]{2,1,0:T(8,128)} %pre.1, ...), custom_call_target="tpu_custom_call" | custom-call | tf_op jit(solution)/shard_map/pallas_call | solution.py:306
  3.0 5.2 %all-to-all-start = ((f32[8,32,256]{2,1,0:T(8,128)}), f32[8,32,256]{2,1,0:T(8,128)S(1)}, u32[]{:S(2)}, u32[]{:S(2)}) async-start(f32[8,32,256]{2,1,0:T(8,128)} %bitcast), calls=%async_computation | async-start | bytes 524288 | tf_op jit(solution)/shard_map/all_to_all | solution.py:572
  8.2 2.7 %shard_map.138 = (f32[8,32,128]{2,1,0:T(8,128)S(1)}, f32[9,8,32,128]{3,2,1,0:T(8,128)S(1)}, f32[8,32,128]{2,1,0:T(8,128)S(1)}, f32[14,32,128]{2,1,0:T(8,128)}, f...) custom-call(f32[8,32,128]{2,1,0:T(8,128)S(1)} %get-tuple-element.35., ...), custom_call_target="tpu_custom_call", output_to_operand_aliasing={{0}: (2, {}), {1}: (3, {})} | custom-call | tf_op jit(solution)/shard_map/pallas_call | solution.py:306
  10.9 0.0 copy-start.2
  10.9 0.0 copy-start.3
  10.9 0.0 copy-start.5
  10.9 0.0 copy-start.4
  11.0 3.3 %all-to-all-done.lines = f32[8,32,256]{2,1,0:T(8,128)S(1)} async-done(((f32[8,32,256]{2,1,0:T(8,128)}), f32[8,32,256]{2,1,0:T(8,128)S(1)}, u32[]{:S(2)}, u32[]{:S(2)}) %all-to-all-start) | async-done | bytes 262176 | tf_op jit(solution)/shard_map/all_to_all | solution.py:572
  14.2 0.4 shard_map.141
  14.6 1.6 %collective-permute-start.5 = (f32[72,128]{1,0:T(8,128)S(1)}, f32[72,128]{1,0:T(8,128)S(1)}, u32[]{:S(2)}, u32[]{:S(2)}) collective-permute-start(f32[72,128]{1,0:T(8,128)S(1)} %get-tuple-element.56.own), channel_id=1, source_target_pairs={{0,8},{8,0},{16,24},{24,16},{1,9},{9,1},{17,25},{25,17},{2,10},{10... | collective-permute-start | bytes 110600 | tf_op jit(solution)/shard_map/ppermute | solution.py:319
  16.3 2.6 %collective-permute-start.6 = (f32[72,128]{1,0:T(8,128)S(1)}, f32[72,128]{1,0:T(8,128)S(1)}, u32[]{:S(2)}, u32[]{:S(2)}) collective-permute-start(f32[72,128]{1,0:T(8,128)S(1)} %get-tuple-element.56.own), channel_id=1, source_target_pairs={{0,16},{8,24},{16,0},{24,8},{1,17},{9,25},{17,1},{25,9},{2,18},{10... | collective-permute-start | bytes 110600 | tf_op jit(solution)/shard_map/ppermute | solution.py:319
  18.9 0.2 collective-permute-start.7
  19.1 0.0 collective-permute-done.5.rest_0_
  19.1 2.7 %collective-permute-done.6.rest_1_ = f32[72,128]{1,0:T(8,128)S(1)} collective-permute-done((f32[72,128]{1,0:T(8,128)S(1)}, f32[72,128]{1,0:T(8,128)S(1)}, u32[]{:S(2)}, u32[]{:S(2)}) %collective-permute-start.6) | collective-permute-done | bytes 36896 | tf_op jit(solution)/shard_map/ppermute | solution.py:319
  21.8 2.8 %collective-permute-done.7.rest_2_ = f32[72,128]{1,0:T(8,128)S(1)} collective-permute-done((f32[72,128]{1,0:T(8,128)S(1)}, f32[72,128]{1,0:T(8,128)S(1)}, u32[]{:S(2)}, u32[]{:S(2)}) %collective-permute-start.7) | collective-permute-done | bytes 36896 | tf_op jit(solution)/shard_map/ppermute | solution.py:319
  24.6 1.6 %shard_map.142 = f32[8,32,384]{2,1,0:T(8,128)} custom-call(f32[8,32,128]{2,1,0:T(8,128)S(1)} %get-tuple-element.55.modes, f32[72,128]{1,0:T(8,128)S(1)} %get-tuple-element.56.own, f32[72,128]{1,0:T(8,128)S(1)} %collective-permute-done.5.rest_0_, f32[72,128]{1,0:T(8,128)S(1)} %collective-permute-done.6.rest_1_, f32[72,128]{1,0:T(8,128)S(1)} %collective-permute-done.7.rest_2_, ...), custom_call_target="tpu_custom_call" | custom-call | tf_op jit(solution)/shard_map/pallas_call | solution.py:306
  26.3 3.5 %all-to-all-start.1 = ((f32[8,32,384]{2,1,0:T(8,128)}), f32[8,32,384]{2,1,0:T(8,128)S(1)}, u32[]{:S(2)}, u32[]{:S(2)}) async-start(f32[8,32,384]{2,1,0:T(8,128)} %shard_map.142), calls=%async_computation.1 | async-start | bytes 786432 | tf_op jit(solution)/shard_map/all_to_all | solution.py:613
  29.7 0.1 collective-permute-start.3
  29.8 0.0 copy-done.2
  29.8 1.5 %collective-permute-start.4 = (f32[14,32,128]{2,1,0:T(8,128)S(1)}, f32[14,32,128]{2,1,0:T(8,128)S(1)}, u32[]{:S(2)}, u32[]{:S(2)}) collective-permute-start(f32[14,32,128]{2,1,0:T(8,128)S(1)} %copy-done.2), channel_id=1, source_target_pairs={{8,16},{24,0},{16,8},{0,24},{9,17},{25,1},{17,9},{1,25},{10,18},{2... | collective-permute-start | bytes 688136 | tf_op jit(solution)/shard_map/ppermute | solution.py:343
  31.3 0.0 copy-done.3
  31.3 1.9 %collective-permute-start.2 = (f32[8,32,128]{2,1,0:T(8,128)S(1)}, f32[8,32,128]{2,1,0:T(8,128)S(1)}, u32[]{:S(2)}, u32[]{:S(2)}) collective-permute-start(f32[8,32,128]{2,1,0:T(8,128)S(1)} %copy-done.3), channel_id=1, source_target_pairs={{0,1},{1,0},{2,3},{3,2},{4,5},{5,4},{6,7},{7,6},{8,9},{9,8},{10,11... | collective-permute-start | bytes 393224 | tf_op jit(solution)/shard_map/ppermute | solution.py:348
  33.2 0.0 copy-done.5
  33.2 0.0 collective-permute-start
  33.2 0.0 copy-done.4
  33.2 1.7 %collective-permute-start.1 = (f32[14,8,128]{2,1,0:T(8,128)S(1)}, f32[14,8,128]{2,1,0:T(8,128)S(1)}, u32[]{:S(2)}, u32[]{:S(2)}) collective-permute-start(f32[14,8,128]{2,1,0:T(8,128)S(1)} %copy-done.4), channel_id=1, source_target_pairs={{0,6},{2,0},{4,2},{6,4},{1,7},{3,1},{5,3},{7,5},{8,14},{10,8},{12,... | collective-permute-start | bytes 172040 | tf_op jit(solution)/shard_map/ppermute | solution.py:348
  34.9 2.7 %collective-permute-done.ybelow = f32[14,8,128]{2,1,0:T(8,128)S(1)} collective-permute-done((f32[14,8,128]{2,1,0:T(8,128)S(1)}, f32[14,8,128]{2,1,0:T(8,128)S(1)}, u32[]{:S(2)}, u32[]{:S(2)}) %collective-permute-start) | collective-permute-done | bytes 57376 | tf_op jit(solution)/shard_map/ppermute | solution.py:348
  37.7 0.0 collective-permute-done.1.yabove
  37.7 2.2 %collective-permute-done.2.zbelow.zabove = f32[8,32,128]{2,1,0:T(8,128)S(1)} collective-permute-done((f32[8,32,128]{2,1,0:T(8,128)S(1)}, f32[8,32,128]{2,1,0:T(8,128)S(1)}, u32[]{:S(2)}, u32[]{:S(2)}) %collective-permute-start.2) | collective-permute-done | bytes 131104 | tf_op jit(solution)/shard_map/ppermute | solution.py:348
  39.9 3.1 %shard_map.139 = (f32[8,32,128]{2,1,0:T(8,128)}, f32[9,8,32,128]{3,2,1,0:T(8,128)}, f32[4,8,32,128]{3,2,1,0:T(8,128)S(1)}, f32[14,2,32,128]{3,2,1,0:T(8,128)S(1)}, f32[256,256]{1,0:T(8,128)S(1)}) custom-call(f32[8,32,128]{2,1,0:T(8,128)S(1)} %get-tuple-element.35.den, f32[3,8,32,128]{3,2,1,0:T(8,128)S(1)} %get-tuple-element.36.vel, ...), custom_call_target="tpu_custom_call" | custom-call | tf_op jit(solution)/shard_map/pallas_call | solution.py:306
  43.0 0.0 collective-permute-done.3.xfirst
  43.0 0.0 copy-start
  43.0 0.0 collective-permute-done.4.xlast
  43.0 0.0 copy-start.1
  43.0 0.7 %copy-done = f32[14,32,128]{2,1,0:T(8,128)} copy-done((f32[14,32,128]{2,1,0:T(8,128)}, f32[14,32,128]{2,1,0:T(8,128)S(1)}, u32[]{:S(2)}) %copy-start) | copy-done | bytes 229400
  43.7 0.1 copy-done.1
  43.7 1.9 %shard_map.140 = (f32[8,32,128]{2,1,0:T(8,128)}, f32[9,8,32,128]{3,2,1,0:T(8,128)}, f32[4,2,32,128]{3,2,1,0:T(8,128)S(1)}) custom-call(f32[8,32,128]{2,1,0:T(8,128)S(1)} %get-tuple-element.35.den, f32[3,8,32,128]{3,2,1,0:T(8,128)S(1)} %get-tuple-element.36.vel, ...), custom_call_target="tpu_custom_call", output_to_operand_aliasing={{0}: (8, {}), {1}: (9, {})} | custom-call | tf_op jit(solution)/shard_map/pallas_call | solution.py:306
  45.6 0.0 all-to-all-done.1.planes
  45.6 1.4 %shard_map.143 = (f32[8,32,128]{2,1,0:T(8,128)}, f32[3,8,32,128]{3,2,1,0:T(8,128)}, f32[8,32,128]{2,1,0:T(8,128)}) custom-call(f32[8,32,384]{2,1,0:T(8,128)S(1)} %all-to-all-done.1.planes, f32[256,256]{1,0:T(8,128)S(1)} %get-tuple-element.58.table, f32[8,32,128]{2,1,0:T(8,128)S(1)} %get-tuple-element.35.den, f32[3,8,32,128]{3,2,1,0:T(8,128)S(1)} %get-tuple-element.36.vel, ...), custom_call_target="tpu_custom_call" | custom-call | tf_op jit(solution)/shard_map/pallas_call | solution.py:306
Async XLA Ops:
  3.0 11.2 %all-to-all-start = ((f32[8,32,256]{2,1,0:T(8,128)}), f32[8,32,256]{2,1,0:T(8,128)S(1)}, u32[]{:S(2)}, u32[]{:S(2)}) async-start(f32[8,32,256]{2,1,0:T(8,128)} %bitcast), calls=%async_computation | async-start | bytes 524288 | tf_op jit(solution)/shard_map/all_to_all | solution.py:572
  10.9 18.9 %copy-start.2 = (f32[14,32,128]{2,1,0:T(8,128)S(1)}, f32[14,32,128]{2,1,0:T(8,128)}, u32[]{:S(2)}) copy-start(f32[14,32,128]{2,1,0:T(8,128)} %get-tuple-element.48) | copy-start | bytes 688132
  10.9 20.4 %copy-start.3 = (f32[8,32,128]{2,1,0:T(8,128)S(1)}, f32[8,32,128]{2,1,0:T(8,128)}, u32[]{:S(2)}) copy-start(f32[8,32,128]{2,1,0:T(8,128)} %get-tuple-element.45) | copy-start | bytes 393220
  10.9 22.3 %copy-start.5 = (f32[14,8,128]{2,1,0:T(8,128)S(1)}, f32[14,8,128]{2,1,0:T(8,128)}, u32[]{:S(2)}) copy-start(f32[14,8,128]{2,1,0:T(8,128)} %get-tuple-element.43) | copy-start | bytes 172036
  10.9 22.2 %copy-start.4 = (f32[14,8,128]{2,1,0:T(8,128)S(1)}, f32[14,8,128]{2,1,0:T(8,128)}, u32[]{:S(2)}) copy-start(f32[14,8,128]{2,1,0:T(8,128)} %get-tuple-element.44) | copy-start | bytes 172036
  14.6 4.5 %collective-permute-start.5 = (f32[72,128]{1,0:T(8,128)S(1)}, f32[72,128]{1,0:T(8,128)S(1)}, u32[]{:S(2)}, u32[]{:S(2)}) collective-permute-start(f32[72,128]{1,0:T(8,128)S(1)} %get-tuple-element.56.own), channel_id=1, source_target_pairs={{0,8},{8,0},{16,24},{24,16},{1,9},{9,1},{17,25},{25,17},{2,10},{10... | collective-permute-start | bytes 110600 | tf_op jit(solution)/shard_map/ppermute | solution.py:319
  16.3 5.5 %collective-permute-start.6 = (f32[72,128]{1,0:T(8,128)S(1)}, f32[72,128]{1,0:T(8,128)S(1)}, u32[]{:S(2)}, u32[]{:S(2)}) collective-permute-start(f32[72,128]{1,0:T(8,128)S(1)} %get-tuple-element.56.own), channel_id=1, source_target_pairs={{0,16},{8,24},{16,0},{24,8},{1,17},{9,25},{17,1},{25,9},{2,18},{10... | collective-permute-start | bytes 110600 | tf_op jit(solution)/shard_map/ppermute | solution.py:319
  18.9 5.8 %collective-permute-start.7 = (f32[72,128]{1,0:T(8,128)S(1)}, f32[72,128]{1,0:T(8,128)S(1)}, u32[]{:S(2)}, u32[]{:S(2)}) collective-permute-start(f32[72,128]{1,0:T(8,128)S(1)} %get-tuple-element.56.own), channel_id=1, source_target_pairs={{0,24},{8,16},{16,8},{24,0},{1,25},{9,17},{17,9},{25,1},{2,26},{10... | collective-permute-start | bytes 110600 | tf_op jit(solution)/shard_map/ppermute | solution.py:319
  26.3 19.4 %all-to-all-start.1 = ((f32[8,32,384]{2,1,0:T(8,128)}), f32[8,32,384]{2,1,0:T(8,128)S(1)}, u32[]{:S(2)}, u32[]{:S(2)}) async-start(f32[8,32,384]{2,1,0:T(8,128)} %shard_map.142), calls=%async_computation.1 | async-start | bytes 786432 | tf_op jit(solution)/shard_map/all_to_all | solution.py:613
  29.7 13.2 %collective-permute-start.3 = (f32[14,32,128]{2,1,0:T(8,128)}, f32[14,32,128]{2,1,0:T(8,128)S(1)}, u32[]{:S(2)}, u32[]{:S(2)}) collective-permute-start(f32[14,32,128]{2,1,0:T(8,128)} %get-tuple-element.47), channel_id=1, source_target_pairs={{0,8},{16,24},{8,0},{24,16},{1,9},{17,25},{9,1},{25,17},{2,10},{18... | collective-permute-start | bytes 688136 | tf_op jit(solution)/shard_map/ppermute | solution.py:343
  29.8 13.2 %collective-permute-start.4 = (f32[14,32,128]{2,1,0:T(8,128)S(1)}, f32[14,32,128]{2,1,0:T(8,128)S(1)}, u32[]{:S(2)}, u32[]{:S(2)}) collective-permute-start(f32[14,32,128]{2,1,0:T(8,128)S(1)} %copy-done.2), channel_id=1, source_target_pairs={{8,16},{24,0},{16,8},{0,24},{9,17},{25,1},{17,9},{1,25},{10,18},{2... | collective-permute-start | bytes 688136 | tf_op jit(solution)/shard_map/ppermute | solution.py:343
  31.3 8.5 %collective-permute-start.2 = (f32[8,32,128]{2,1,0:T(8,128)S(1)}, f32[8,32,128]{2,1,0:T(8,128)S(1)}, u32[]{:S(2)}, u32[]{:S(2)}) collective-permute-start(f32[8,32,128]{2,1,0:T(8,128)S(1)} %copy-done.3), channel_id=1, source_target_pairs={{0,1},{1,0},{2,3},{3,2},{4,5},{5,4},{6,7},{7,6},{8,9},{9,8},{10,11... | collective-permute-start | bytes 393224 | tf_op jit(solution)/shard_map/ppermute | solution.py:348
  33.2 4.5 %collective-permute-start = (f32[14,8,128]{2,1,0:T(8,128)S(1)}, f32[14,8,128]{2,1,0:T(8,128)S(1)}, u32[]{:S(2)}, u32[]{:S(2)}) collective-permute-start(f32[14,8,128]{2,1,0:T(8,128)S(1)} %copy-done.5), channel_id=1, source_target_pairs={{0,2},{2,4},{4,6},{6,0},{1,3},{3,5},{5,7},{7,1},{8,10},{10,12},{12... | collective-permute-start | bytes 172040 | tf_op jit(solution)/shard_map/ppermute | solution.py:348
  33.2 4.5 %collective-permute-start.1 = (f32[14,8,128]{2,1,0:T(8,128)S(1)}, f32[14,8,128]{2,1,0:T(8,128)S(1)}, u32[]{:S(2)}, u32[]{:S(2)}) collective-permute-start(f32[14,8,128]{2,1,0:T(8,128)S(1)} %copy-done.4), channel_id=1, source_target_pairs={{0,6},{2,0},{4,2},{6,4},{1,7},{3,1},{5,3},{7,5},{8,14},{10,8},{12,... | collective-permute-start | bytes 172040 | tf_op jit(solution)/shard_map/ppermute | solution.py:348
  43.0 0.7 %copy-start = (f32[14,32,128]{2,1,0:T(8,128)}, f32[14,32,128]{2,1,0:T(8,128)S(1)}, u32[]{:S(2)}) copy-start(f32[14,32,128]{2,1,0:T(8,128)S(1)} %collective-permute-done.3.xfirst) | copy-start | bytes 688132
  43.0 0.8 %copy-start.1 = (f32[14,32,128]{2,1,0:T(8,128)}, f32[14,32,128]{2,1,0:T(8,128)S(1)}, u32[]{:S(2)}) copy-start(f32[14,32,128]{2,1,0:T(8,128)S(1)} %collective-permute-done.4.xlast) | copy-start | bytes 688132

commit v7 on v6

--- a/solution.py
+++ b/solution.py
@@ -20,9 +20,8 @@
 highest = lax.Precision.HIGHEST
 LANES = 128
 GRANT = 16 * 2**20
-OUT_FIRST = "vvvvvv"
-OUT_PACK = "vvvhhhhhvvv"
-IN_Y = "-vv"
+GROUP = 2
+OUT_PACK = "vvvvvvhhhhhvvv"
 OUT_Y = "v-"
 IN_OTHERS = "-"
 OUT_X = "h"
@@ -79,33 +78,53 @@
 
 def place_in_plane():
     in_g = lax.axis_index("ga")
-    return in_g, lax.axis_index("hy") * lax.axis_size("ga") + in_g
-
-
-def first_kernel(den, vel, pre, spe, cnt, table, spectral,
-                 den_in, vel_in, pre_in, spe_in, cnt_in, table_in, semaphores):
+    return in_g, in_g * lax.axis_size("hy") + lax.axis_index("hy")
+
+
+def along_z_kernel(count_g, count_y, den, *rest):
+    others, (table, *outs, spectrum) = rest[: count_g - 1], rest[count_g - 1 :]
     nx, ny, nz = den.shape
-    in_g, _ = place_in_plane()
-    needed = copies_in([(den, den_in), (table.at[in_g], table_in)], semaphores.at[0])
-    copies = copies_in([(pre, pre_in), (cnt, cnt_in), (spe, spe_in), (vel, vel_in)], semaphores.at[1])
-    for copy in needed:
-        copy.wait()
-    spectral[...] = lax.dot_general(
-        table_in[...], den_in[...].reshape(nx * ny, nz), (((1,), (1,)), ((), ())),
-        precision=highest, preferred_element_type=jnp.float32,
-    )
-    for copy in copies:
-        copy.wait()
-
-
-def pack_kernel(den, vel, pre, spe, cnt, table_y, tables, flat_table,
-                cooled, mass, sound, xfirst, xlast, ylo, yhi, zface, own_y, own_decay, own_flat, semaphores):
+    me = lax.axis_index("ga")
+    total = None
+    for step in range(count_g):
+        cells = den if step == 0 else others[step - 1]
+        part = lax.dot_general(
+            table[source_of(me, step, count_g)], cells[...].reshape(nx * ny, nz),
+            (((1,), (1,)), ((), ())), precision=highest, preferred_element_type=jnp.float32,
+        )
+        total = part if step == 0 else total + part
+    spectrum[...] = total
+    kz = outs[0].shape[0]
+    row = lax.axis_index("hy")
+    for step, out in enumerate(outs):
+        out[...] = spectrum[pl.ds(target_of(row, step, count_y) * kz, kz), :]
+
+
+def pack_kernel(den_at, vel_at, pre_at, spe_at, cnt_at, into_z, table_y, tables, flat_table, into,
+                den, vel, cooled, mass, sound, xfirst, xlast, ylo, yhi, zface, own_y, own_decay, own_flat,
+                cnt, gas_semaphores, semaphores):
     nx, ny, nz = den.shape
     kz = own_decay.shape[1]
-    _, place = place_in_plane()
+    in_g, place = place_in_plane()
+    parts = []
+    for n in range(2):
+        half = pl.ds(n * (nx // 2), nx // 2)
+        parts.append(
+            copies_in(
+                [
+                    (den_at.at[half], den.at[half]),
+                    (pre_at.at[half], cooled.at[half]),
+                    (cnt_at.at[half], cnt.at[half]),
+                    (spe_at.at[:, half], mass.at[:, half]),
+                    (vel_at.at[:, half], vel.at[:, half]),
+                ],
+                gas_semaphores.at[n],
+            )
+        )
     lane = lax.broadcasted_iota(jnp.int32, (ny, LANES), 1)
     later = copies_in(
         [
+            (into_z.at[in_g], into),
             (table_y, own_y),
             (tables.at[:, pl.ds(place * kz, kz), :], own_decay),
             (flat_table, own_flat),
@@ -115,15 +134,8 @@
 
     second, _ = face_roles("hx")
 
-    def plane(x, _):
-        primitive = primitive_plane(x, den, vel, pre, spe, cnt)
-        for at, face in (((nx - 1) * (1 - second), xfirst), ((nx - 1) * second, xlast)):
-
-            @pl.when(x == at)
-            def _():
-                for c in range(prim_n):
-                    face[c] = primitive[c]
-
+    def plane(x):
+        primitive = primitive_plane(x, den, vel, cooled, mass, cnt)
         kept = primitive + [sound_speed(primitive[0], primitive[P_AT])]
         cooled[x] = kept[P_AT]
         for s in range(species_n):
@@ -134,14 +146,24 @@
         for c in range(face_n):
             packed = jnp.where(lane // 2 == c, pltpu.roll(carried[c], 2 * c + 1, 1), packed)
         zface[x] = packed
+
+    def planes(i, _):
+        for n in range(GROUP):
+            plane(i * GROUP + n)
         return 0
 
-    lax.fori_loop(0, nx, plane, 0)
+    turns = nx // 2 // GROUP
+    for n, copies in enumerate(parts):
+        for copy in copies:
+            copy.wait()
+        lax.fori_loop(n * turns, (n + 1) * turns, planes, 0)
     kept = [den] + [vel.at[d] for d in range(3)] + [cooled] + [mass.at[s] for s in range(species_n)]
     for c in range(prim_n):
         rows = kept[c].reshape(nx * ny, nz)
         ylo[c] = rows[pl.ds(0, nx, stride=ny), :]
         yhi[c] = rows[pl.ds(ny - 1, nx, stride=ny), :]
+        xfirst[c] = kept[c][(nx - 1) * (1 - second)]
+        xlast[c] = kept[c][(nx - 1) * second]
     for copy in later:
         copy.wait()
 
@@ -323,6 +345,10 @@
     return index ^ step if count & (count - 1) == 0 else (index + step) % count
 
 
+def target_of(index, step, count):
+    return index ^ step if count & (count - 1) == 0 else lax.rem(index + step, count)
+
+
 def source_of(index, step, count):
     return index ^ step if count & (count - 1) == 0 else lax.rem(index + count - step, count)
 
@@ -384,8 +410,11 @@
     return pltpu.roll(value, lanes, 1) if lanes else value
 
 
-def along_y_kernel(size_g, block, lines, table_y, tables, modes, sums, grid_rows):
-    _, kz, _ = lines.shape
+def along_y_kernel(count, block, *rest):
+    received, (table_y, tables, modes, sums, grid_rows, lines) = rest[:count], rest[count:]
+    for step in range(count):
+        lines[source_of(lax.axis_index("hy"), step, count)] = received[step][...]
+    kz = lines.shape[1]
     nx, _, ny = modes.shape
     width = block
     per = LANES // width
@@ -394,11 +423,7 @@
         for high in range(nx // per):
             source = []
             for s in range(per):
-                first = (column * per + s) * size_g
-                total = lines[first, :, high * LANES : (high + 1) * LANES]
-                for g in range(1, size_g):
-                    total = total + lines[first + g, :, high * LANES : (high + 1) * LANES]
-                source.append(total)
+                source.append(lines[column * per + s, :, high * LANES : (high + 1) * LANES])
             for low in range(per):
                 line = turned(source[0], -low * width)
                 for s in range(1, per):
@@ -548,12 +573,14 @@
     table_z = hartley(keys_z, keys_z, all_z)
     ahead = hartley(keys_z, keys_z + 1, all_z)
     behind = hartley(keys_z, keys_z - 1, all_z)
-    into_z = jnp.asarray(table_z.reshape(all_z, size_g, nz).transpose(1, 0, 2), jnp.float32)
+    into_z = table_z.reshape(size_g, all_z // size_g, size_g, nz).transpose(0, 2, 1, 3)
+    into_z = jnp.asarray(into_z, jnp.float32)
     pull_z = -0.5 * (ahead - behind)
     from_z = np.concatenate(
         [t.reshape(all_z, size_g, nz).transpose(1, 0, 2) for t in (table_z, pull_z)], axis=2
     )
-    from_z = jnp.asarray(from_z, jnp.float32)
+    from_z = from_z.reshape(size_g, size_g, size_y, kz, 2 * nz).transpose(0, 2, 1, 3, 4)
+    from_z = jnp.asarray(from_z.reshape(size_g, all_z, 2 * nz), jnp.float32)
     keys_y = np.arange(all_y)
     table_y = jnp.asarray(hartley(keys_y, keys_y, all_y), jnp.float32)
     tables = jnp.asarray(decay_tables(all_x, all_y, all_z))
@@ -561,40 +588,47 @@
 
     floats = functools.partial(pltpu.VMEM, dtype=jnp.float32)
 
-    spectral, den, vel, pre, spe, cnt = placed_call(
-        first_kernel,
-        (density, velocity, pressure, species, newton_count, into_z),
-        "hhhhhh",
-        [(all_z, main), density.shape, velocity.shape, pressure.shape, species.shape, newton_count],
-        OUT_FIRST,
-        [floats((all_z, nz)), pltpu.SemaphoreType.DMA((2, 4))],
-    )
-    spectral = lax.all_to_all(spectral.reshape(groups, kz, main), ("hy", "ga"), split_axis=0, concat_axis=0, tiled=True)
-    cooled, dense, sound, xfirst, xlast, ylo, yhi, zface, own_y, own_decay, own_flat = placed_call(
+    near_density = [exchanged(density, "ga", step) for step in range(1, size_g)]
+    into, den, vel, cooled, dense, sound, xfirst, xlast, ylo, yhi, zface, own_y, own_decay, own_flat = placed_call(
         pack_kernel,
-        (den, vel, pre, spe, cnt, table_y, tables, flat_table),
-        "vvvvvhhh",
-        [pre.shape, spe.shape, pre.shape] + [(prim_n, ny, nz)] * 2 + [(prim_n, nx, nz)] * 2 + [(nx, ny, LANES)]
+        (density, velocity, pressure, species, newton_count, into_z, table_y, tables, flat_table),
+        "hhhhhhhhh",
+        [into_z.shape[1:], density.shape, velocity.shape, pressure.shape, species.shape, density.shape]
+        + [(prim_n, ny, nz)] * 2 + [(prim_n, nx, nz)] * 2 + [(nx, ny, LANES)]
         + [table_y.shape, (3, kz, all_y), flat_table.shape],
         OUT_PACK,
-        [pltpu.SemaphoreType.DMA((3,))],
-        {2: 0, 3: 1},
-    )
+        [
+            pltpu.VMEM((nx, ny, nz), jnp.int32),
+            pltpu.SemaphoreType.DMA((2, 5)),
+            pltpu.SemaphoreType.DMA((4,)),
+        ],
+    )
+    spectral = placed_call(
+        functools.partial(along_z_kernel, size_g, size_y),
+        (den, *near_density, into),
+        "v" + "-" * (size_g - 1) + "v",
+        [(kz, main)] * size_y,
+        "-" * size_y,
+        [floats((all_z // size_g, main))],
+    )
+    spectral = list(spectral)
+    for step in range(1, size_y):
+        spectral[step] = exchanged(spectral[step], "hy", step)
     modes, sums = placed_call(
-        functools.partial(along_y_kernel, size_g, ny),
-        (spectral, own_y, own_decay),
-        IN_Y,
+        functools.partial(along_y_kernel, size_y, ny),
+        (*spectral, own_y, own_decay),
+        "-" * size_y + "vv",
         [(nx, kz, all_y), (2 * kz + nx, all_y)],
         OUT_Y,
-        [floats((nx * kz, all_y))],
-    )
-    others = []
-    for step in range(1, size_x):
-        others.append(exchanged(sums, "hx", step))
+        [floats((nx * kz, all_y)), floats((size_y, kz, main))],
+    )
     ybelow = shifted(yhi, "hy", 1)
     yabove = shifted(ylo, "hy", -1)
     zbelow = shifted(zface, "ga", 1)
     zabove = zbelow if size_g == 2 else shifted(zface, "ga", -1)
+    others = []
+    for step in range(1, size_x):
+        others.append(exchanged(sums, "hx", step))
     xfirst = faced_pairs(xfirst, "hx", True)
     xlast = faced_pairs(xlast, "hx", False)
     (planes,) = placed_call(

time: 47.4 us -> 46.1 us (0.973)
  Pallas kernels: 13.4 us -> 12.2 us
    all_to_all x1 -> x0, starting transfers between devices: 5.21 us -> none  [step(): lax.all_to_all(spectral.reshape(groups, kz, main), ('hy', 'ga'), split_ax...]
    ppermute x3 -> x7, starting transfers between devices: 4.45 us -> 9.43 us  [exchanged(): lax.ppermute(value, axis, [(i, partner(i, step, count)) for i in range(co...]
    ppermute x3 -> x7, waiting for transfers between devices: 5.53 us -> 9.09 us  [exchanged(): lax.ppermute(value, axis, [(i, partner(i, step, count)) for i in range(co...]
    all_to_all x1 -> x0, waiting for transfers between devices: 3.29 us -> none  [step(): lax.all_to_all(spectral.reshape(groups, kz, main), ('hy', 'ga'), split_ax...]
    pallas_call x7, Pallas kernels: 13.4 us -> 12.2 us  [placed_call(): pl.pallas_call(kernel, out_shape=shapes, in_specs=specs, out_specs=[pl.Bl...]
  transfers between devices with their start and end apart: 10 -> 13, of which waited for: 5 -> 7; matrix products, arithmetic and copies ran while one was open for 0% -> 0% of each run, Pallas kernels for 16% -> 18%
where the time goes in v7:
time: 46.1 us; the launch traced here: 45.8 us
  starting transfers between devices  18 us (39%)
  waiting for transfers between devices  14.1 us (31%)
  Pallas kernels  12.2 us (26%)
  between operations  0.79 us (2%)
  local copies, waits for them, and re-layouts  0.77 us (2%)
    pallas_call x7, Pallas kernels, placed_call(): pl.pallas_call(kernel, out_shape=shapes, in_specs=specs, out_specs=[pl.Bl...  12.2 us
    ppermute x7, starting transfers between devices, exchanged(): lax.ppermute(value, axis, [(i, partner(i, step, count)) for i in range(co...  9.43 us
    ppermute x7, waiting for transfers between devices, exchanged(): lax.ppermute(value, axis, [(i, partner(i, step, count)) for i in range(co...  9.09 us
    ppermute x3, waiting for transfers between devices, shifted(): lax.ppermute(value, axis, [(i, (i + step) % count) for i in range(count)])  5 us
    ppermute x3, starting transfers between devices, shifted(): lax.ppermute(value, axis, [(i, (i + step) % count) for i in range(count)])  3.6 us
    all_to_all x1, starting transfers between devices, step(): lax.all_to_all(planes, ('hy', 'ga'), split_axis=0, concat_axis=0, tiled=T...  3.45 us
    ppermute x2, starting transfers between devices, faced_pairs(): return lax.ppermute(value, axis, pairs + [(b, a) for a, b in pairs])  1.49 us
  transfers between devices with their start and end apart: 13, of which 7 were waited for; matrix products, arithmetic and copies ran while one was open for 0% of the time, Pallas kernels for 18%

profile of v7, /device:TPU:0, one launch (start us, length us, event | category | flops | bytes accessed | tf_op | source)
XLA Modules:
  0.0 45.8 jit_solution(18263792294434981751)
XLA Ops:
  0.6 3.1 %collective-permute-start.5 = (f32[8,32,128]{2,1,0:T(8,128)}, f32[8,32,128]{2,1,0:T(8,128)S(1)}, u32[]{:S(2)}, u32[]{:S(2)}) collective-permute-start(f32[8,32,128]{2,1,0:T(8,128)} %den_at.1), channel_id=1, source_target_pairs={{0,1},{1,0},{2,3},{3,2},{4,5},{5,4},{6,7},{7,6},{8,9},{9,8},{10,11... | collective-permute-start | bytes 393224 | tf_op jit(solution)/shard_map/ppermute | solution.py:341
  3.7 3.4 %shard_map.137 = (f32[2,128,128]{2,1,0:T(8,128)S(1)}, f32[8,32,128]{2,1,0:T(8,128)S(1)}, f32[3,8,32,128]{3,2,1,0:T(8,128)S(1)}, f32[8,32,128]{2,1,0:T(8,128)S(1)...) custom-call(f32[8,32,128]{2,1,0:T(8,128)} %den_at.1, ...), custom_call_target="tpu_custom_call" | custom-call | tf_op jit(solution)/shard_map/pallas_call | solution.py:328
  7.1 0.0 copy-start.2
  7.1 0.0 copy-start.3
  7.1 0.0 copy-start.5
  7.1 0.0 copy-start.4
  7.1 0.3 collective-permute-done.5.rest_0_
  7.4 0.4 shard_map.140
  7.8 0.1 collective-permute-start.6
  7.9 1.8 %collective-permute-start.7 = (f32[32,256]{1,0:T(8,128)S(1)}, f32[32,256]{1,0:T(8,128)S(1)}, u32[]{:S(2)}, u32[]{:S(2)}) collective-permute-start(f32[32,256]{1,0:T(8,128)S(1)} %get-tuple-element.53), channel_id=1, source_target_pairs={{0,4},{2,6},{4,0},{6,2},{1,5},{3,7},{5,1},{7,3},{8,12},{10,14},{12... | collective-permute-start | bytes 98312 | tf_op jit(solution)/shard_map/ppermute | solution.py:341
  9.6 0.1 collective-permute-start.8
  9.7 0.0 collective-permute-done.6.rest_1_
  9.7 2.1 %collective-permute-done.7.rest_2_ = f32[32,256]{1,0:T(8,128)S(1)} collective-permute-done((f32[32,256]{1,0:T(8,128)S(1)}, f32[32,256]{1,0:T(8,128)S(1)}, u32[]{:S(2)}, u32[]{:S(2)}) %collective-permute-start.7) | collective-permute-done | bytes 32800 | tf_op jit(solution)/shard_map/ppermute | solution.py:341
  11.8 1.2 %collective-permute-done.8.rest_3_ = f32[32,256]{1,0:T(8,128)S(1)} collective-permute-done((f32[32,256]{1,0:T(8,128)S(1)}, f32[32,256]{1,0:T(8,128)S(1)}, u32[]{:S(2)}, u32[]{:S(2)}) %collective-permute-start.8) | collective-permute-done | bytes 32800 | tf_op jit(solution)/shard_map/ppermute | solution.py:341
  13.0 0.4 shard_map.141
  13.4 1.6 %collective-permute-start.9 = (f32[72,128]{1,0:T(8,128)S(1)}, f32[72,128]{1,0:T(8,128)S(1)}, u32[]{:S(2)}, u32[]{:S(2)}) collective-permute-start(f32[72,128]{1,0:T(8,128)S(1)} %get-tuple-element.58.own), channel_id=1, source_target_pairs={{0,8},{8,0},{16,24},{24,16},{1,9},{9,1},{17,25},{25,17},{2,10},{10... | collective-permute-start | bytes 110600 | tf_op jit(solution)/shard_map/ppermute | solution.py:341
  15.1 2.6 %collective-permute-start.10 = (f32[72,128]{1,0:T(8,128)S(1)}, f32[72,128]{1,0:T(8,128)S(1)}, u32[]{:S(2)}, u32[]{:S(2)}) collective-permute-start(f32[72,128]{1,0:T(8,128)S(1)} %get-tuple-element.58.own), channel_id=1, source_target_pairs={{0,16},{8,24},{16,0},{24,8},{1,17},{9,25},{17,1},{25,9},{2,18},{10... | collective-permute-start | bytes 110600 | tf_op jit(solution)/shard_map/ppermute | solution.py:341
  17.7 0.2 collective-permute-start.11
  17.9 0.0 collective-permute-done.9.rest_0_
  17.9 2.8 %collective-permute-done.10.rest_1_ = f32[72,128]{1,0:T(8,128)S(1)} collective-permute-done((f32[72,128]{1,0:T(8,128)S(1)}, f32[72,128]{1,0:T(8,128)S(1)}, u32[]{:S(2)}, u32[]{:S(2)}) %collective-permute-start.10) | collective-permute-done | bytes 36896 | tf_op jit(solution)/shard_map/ppermute | solution.py:341
  20.6 2.8 %collective-permute-done.11.rest_2_ = f32[72,128]{1,0:T(8,128)S(1)} collective-permute-done((f32[72,128]{1,0:T(8,128)S(1)}, f32[72,128]{1,0:T(8,128)S(1)}, u32[]{:S(2)}, u32[]{:S(2)}) %collective-permute-start.11) | collective-permute-done | bytes 36896 | tf_op jit(solution)/shard_map/ppermute | solution.py:341
  23.4 1.6 %shard_map.142 = f32[8,32,384]{2,1,0:T(8,128)} custom-call(f32[8,32,128]{2,1,0:T(8,128)S(1)} %get-tuple-element.57.modes, f32[72,128]{1,0:T(8,128)S(1)} %get-tuple-element.58.own, f32[72,128]{1,0:T(8,128)S(1)} %collective-permute-done.9.rest_0_, f32[72,128]{1,0:T(8,128)S(1)} %collective-permute-done.10.rest_1_, ...), custom_call_target="tpu_custom_call" | custom-call | tf_op jit(solution)/shard_map/pallas_call | solution.py:328
  25.0 3.5 %all-to-all-start = ((f32[8,32,384]{2,1,0:T(8,128)}), f32[8,32,384]{2,1,0:T(8,128)S(1)}, u32[]{:S(2)}, u32[]{:S(2)}) async-start(f32[8,32,384]{2,1,0:T(8,128)} %shard_map.142), calls=%async_computation | async-start | bytes 786432 | tf_op jit(solution)/shard_map/all_to_all | solution.py:647
  28.5 0.1 collective-permute-start.3
  28.6 0.0 copy-done.2
  28.6 1.4 %collective-permute-start.4 = (f32[14,32,128]{2,1,0:T(8,128)S(1)}, f32[14,32,128]{2,1,0:T(8,128)S(1)}, u32[]{:S(2)}, u32[]{:S(2)}) collective-permute-start(f32[14,32,128]{2,1,0:T(8,128)S(1)} %copy-done.2), channel_id=1, source_target_pairs={{8,16},{24,0},{16,8},{0,24},{9,17},{25,1},{17,9},{1,25},{10,18},{2... | collective-permute-start | bytes 688136 | tf_op jit(solution)/shard_map/ppermute | solution.py:369
  30.0 0.0 copy-done.3
  30.0 1.9 %collective-permute-start.2 = (f32[8,32,128]{2,1,0:T(8,128)S(1)}, f32[8,32,128]{2,1,0:T(8,128)S(1)}, u32[]{:S(2)}, u32[]{:S(2)}) collective-permute-start(f32[8,32,128]{2,1,0:T(8,128)S(1)} %copy-done.3), channel_id=1, source_target_pairs={{0,1},{1,0},{2,3},{3,2},{4,5},{5,4},{6,7},{7,6},{8,9},{9,8},{10,11... | collective-permute-start | bytes 393224 | tf_op jit(solution)/shard_map/ppermute | solution.py:374
  31.9 0.0 copy-done.5
  31.9 0.0 collective-permute-start
  31.9 0.0 copy-done.4
  31.9 1.7 %collective-permute-start.1 = (f32[14,8,128]{2,1,0:T(8,128)S(1)}, f32[14,8,128]{2,1,0:T(8,128)S(1)}, u32[]{:S(2)}, u32[]{:S(2)}) collective-permute-start(f32[14,8,128]{2,1,0:T(8,128)S(1)} %copy-done.4), channel_id=1, source_target_pairs={{0,6},{2,0},{4,2},{6,4},{1,7},{3,1},{5,3},{7,5},{8,14},{10,8},{12,... | collective-permute-start | bytes 172040 | tf_op jit(solution)/shard_map/ppermute | solution.py:374
  33.6 2.8 %collective-permute-done.ybelow = f32[14,8,128]{2,1,0:T(8,128)S(1)} collective-permute-done((f32[14,8,128]{2,1,0:T(8,128)S(1)}, f32[14,8,128]{2,1,0:T(8,128)S(1)}, u32[]{:S(2)}, u32[]{:S(2)}) %collective-permute-start) | collective-permute-done | bytes 57376 | tf_op jit(solution)/shard_map/ppermute | solution.py:374
  36.5 0.0 collective-permute-done.1.yabove
  36.5 2.2 %collective-permute-done.2.zbelow.zabove = f32[8,32,128]{2,1,0:T(8,128)S(1)} collective-permute-done((f32[8,32,128]{2,1,0:T(8,128)S(1)}, f32[8,32,128]{2,1,0:T(8,128)S(1)}, u32[]{:S(2)}, u32[]{:S(2)}) %collective-permute-start.2) | collective-permute-done | bytes 131104 | tf_op jit(solution)/shard_map/ppermute | solution.py:374
  38.6 3.1 %shard_map.138 = (f32[8,32,128]{2,1,0:T(8,128)}, f32[9,8,32,128]{3,2,1,0:T(8,128)}, f32[4,8,32,128]{3,2,1,0:T(8,128)S(1)}, f32[14,2,32,128]{3,2,1,0:T(8,128)S(1)}, f32[256,256]{1,0:T(8,128)S(1)}) custom-call(f32[8,32,128]{2,1,0:T(8,128)S(1)} %get-tuple-element.36.den, f32[3,8,32,128]{3,2,1,0:T(8,128)S(1)} %get-tuple-element.37.vel, ...), custom_call_target="tpu_custom_call" | custom-call | tf_op jit(solution)/shard_map/pallas_call | solution.py:328
  41.7 0.0 collective-permute-done.3.xfirst
  41.8 0.0 copy-start
  41.8 0.0 collective-permute-done.4.xlast
  41.8 0.0 copy-start.1
  41.8 0.7 %copy-done = f32[14,32,128]{2,1,0:T(8,128)} copy-done((f32[14,32,128]{2,1,0:T(8,128)}, f32[14,32,128]{2,1,0:T(8,128)S(1)}, u32[]{:S(2)}) %copy-start) | copy-done | bytes 229400
  42.4 0.1 copy-done.1
  42.5 1.9 %shard_map.139 = (f32[8,32,128]{2,1,0:T(8,128)}, f32[9,8,32,128]{3,2,1,0:T(8,128)}, f32[4,2,32,128]{3,2,1,0:T(8,128)S(1)}) custom-call(f32[8,32,128]{2,1,0:T(8,128)S(1)} %get-tuple-element.36.den, f32[3,8,32,128]{3,2,1,0:T(8,128)S(1)} %get-tuple-element.37.vel, ...), custom_call_target="tpu_custom_call", output_to_operand_aliasing={{0}: (8, {}), {1}: (9, {})} | custom-call | tf_op jit(solution)/shard_map/pallas_call | solution.py:328
  44.4 0.0 all-to-all-done.planes
  44.4 1.4 %shard_map.143 = (f32[8,32,128]{2,1,0:T(8,128)}, f32[3,8,32,128]{3,2,1,0:T(8,128)}, f32[8,32,128]{2,1,0:T(8,128)}) custom-call(f32[8,32,384]{2,1,0:T(8,128)S(1)} %all-to-all-done.planes, f32[256,256]{1,0:T(8,128)S(1)} %get-tuple-element.60.table, f32[8,32,128]{2,1,0:T(8,128)S(1)} %get-tuple-element.36.den, f32[3,8,32,128]{3,2,1,0:T(8,128)S(1)} %get-tuple-element.37.vel, ...), custom_call_target="tpu_custom_call" | custom-call | tf_op jit(solution)/shard_map/pallas_call | solution.py:328
Async XLA Ops:
  0.6 6.8 %collective-permute-start.5 = (f32[8,32,128]{2,1,0:T(8,128)}, f32[8,32,128]{2,1,0:T(8,128)S(1)}, u32[]{:S(2)}, u32[]{:S(2)}) collective-permute-start(f32[8,32,128]{2,1,0:T(8,128)} %den_at.1), channel_id=1, source_target_pairs={{0,1},{1,0},{2,3},{3,2},{4,5},{5,4},{6,7},{7,6},{8,9},{9,8},{10,11... | collective-permute-start | bytes 393224 | tf_op jit(solution)/shard_map/ppermute | solution.py:341
  7.1 21.5 %copy-start.2 = (f32[14,32,128]{2,1,0:T(8,128)S(1)}, f32[14,32,128]{2,1,0:T(8,128)}, u32[]{:S(2)}) copy-start(f32[14,32,128]{2,1,0:T(8,128)} %get-tuple-element.46) | copy-start | bytes 688132
  7.1 22.9 %copy-start.3 = (f32[8,32,128]{2,1,0:T(8,128)S(1)}, f32[8,32,128]{2,1,0:T(8,128)}, u32[]{:S(2)}) copy-start(f32[8,32,128]{2,1,0:T(8,128)} %get-tuple-element.43) | copy-start | bytes 393220
  7.1 24.8 %copy-start.5 = (f32[14,8,128]{2,1,0:T(8,128)S(1)}, f32[14,8,128]{2,1,0:T(8,128)}, u32[]{:S(2)}) copy-start(f32[14,8,128]{2,1,0:T(8,128)} %get-tuple-element.41) | copy-start | bytes 172036
  7.1 24.8 %copy-start.4 = (f32[14,8,128]{2,1,0:T(8,128)S(1)}, f32[14,8,128]{2,1,0:T(8,128)}, u32[]{:S(2)}) copy-start(f32[14,8,128]{2,1,0:T(8,128)} %get-tuple-element.42) | copy-start | bytes 172036
  7.8 1.9 %collective-permute-start.6 = (f32[32,256]{1,0:T(8,128)S(1)}, f32[32,256]{1,0:T(8,128)S(1)}, u32[]{:S(2)}, u32[]{:S(2)}) collective-permute-start(f32[32,256]{1,0:T(8,128)S(1)} %get-tuple-element.52), channel_id=1, source_target_pairs={{0,2},{2,0},{4,6},{6,4},{1,3},{3,1},{5,7},{7,5},{8,10},{10,8},{12,... | collective-permute-start | bytes 98312 | tf_op jit(solution)/shard_map/ppermute | solution.py:341
  7.9 4.0 %collective-permute-start.7 = (f32[32,256]{1,0:T(8,128)S(1)}, f32[32,256]{1,0:T(8,128)S(1)}, u32[]{:S(2)}, u32[]{:S(2)}) collective-permute-start(f32[32,256]{1,0:T(8,128)S(1)} %get-tuple-element.53), channel_id=1, source_target_pairs={{0,4},{2,6},{4,0},{6,2},{1,5},{3,7},{5,1},{7,3},{8,12},{10,14},{12... | collective-permute-start | bytes 98312 | tf_op jit(solution)/shard_map/ppermute | solution.py:341
  9.6 3.4 %collective-permute-start.8 = (f32[32,256]{1,0:T(8,128)S(1)}, f32[32,256]{1,0:T(8,128)S(1)}, u32[]{:S(2)}, u32[]{:S(2)}) collective-permute-start(f32[32,256]{1,0:T(8,128)S(1)} %get-tuple-element.54), channel_id=1, source_target_pairs={{0,6},{2,4},{4,2},{6,0},{1,7},{3,5},{5,3},{7,1},{8,14},{10,12},{12... | collective-permute-start | bytes 98312 | tf_op jit(solution)/shard_map/ppermute | solution.py:341
  13.4 4.5 %collective-permute-start.9 = (f32[72,128]{1,0:T(8,128)S(1)}, f32[72,128]{1,0:T(8,128)S(1)}, u32[]{:S(2)}, u32[]{:S(2)}) collective-permute-start(f32[72,128]{1,0:T(8,128)S(1)} %get-tuple-element.58.own), channel_id=1, source_target_pairs={{0,8},{8,0},{16,24},{24,16},{1,9},{9,1},{17,25},{25,17},{2,10},{10... | collective-permute-start | bytes 110600 | tf_op jit(solution)/shard_map/ppermute | solution.py:341
  15.1 5.6 %collective-permute-start.10 = (f32[72,128]{1,0:T(8,128)S(1)}, f32[72,128]{1,0:T(8,128)S(1)}, u32[]{:S(2)}, u32[]{:S(2)}) collective-permute-start(f32[72,128]{1,0:T(8,128)S(1)} %get-tuple-element.58.own), channel_id=1, source_target_pairs={{0,16},{8,24},{16,0},{24,8},{1,17},{9,25},{17,1},{25,9},{2,18},{10... | collective-permute-start | bytes 110600 | tf_op jit(solution)/shard_map/ppermute | solution.py:341
  17.7 5.8 %collective-permute-start.11 = (f32[72,128]{1,0:T(8,128)S(1)}, f32[72,128]{1,0:T(8,128)S(1)}, u32[]{:S(2)}, u32[]{:S(2)}) collective-permute-start(f32[72,128]{1,0:T(8,128)S(1)} %get-tuple-element.58.own), channel_id=1, source_target_pairs={{0,24},{8,16},{16,8},{24,0},{1,25},{9,17},{17,9},{25,1},{2,26},{10... | collective-permute-start | bytes 110600 | tf_op jit(solution)/shard_map/ppermute | solution.py:341
  25.0 19.4 %all-to-all-start = ((f32[8,32,384]{2,1,0:T(8,128)}), f32[8,32,384]{2,1,0:T(8,128)S(1)}, u32[]{:S(2)}, u32[]{:S(2)}) async-start(f32[8,32,384]{2,1,0:T(8,128)} %shard_map.142), calls=%async_computation | async-start | bytes 786432 | tf_op jit(solution)/shard_map/all_to_all | solution.py:647
  28.5 13.2 %collective-permute-start.3 = (f32[14,32,128]{2,1,0:T(8,128)}, f32[14,32,128]{2,1,0:T(8,128)S(1)}, u32[]{:S(2)}, u32[]{:S(2)}) collective-permute-start(f32[14,32,128]{2,1,0:T(8,128)} %get-tuple-element.45), channel_id=1, source_target_pairs={{0,8},{16,24},{8,0},{24,16},{1,9},{17,25},{9,1},{25,17},{2,10},{18... | collective-permute-start | bytes 688136 | tf_op jit(solution)/shard_map/ppermute | solution.py:369
  28.6 13.2 %collective-permute-start.4 = (f32[14,32,128]{2,1,0:T(8,128)S(1)}, f32[14,32,128]{2,1,0:T(8,128)S(1)}, u32[]{:S(2)}, u32[]{:S(2)}) collective-permute-start(f32[14,32,128]{2,1,0:T(8,128)S(1)} %copy-done.2), channel_id=1, source_target_pairs={{8,16},{24,0},{16,8},{0,24},{9,17},{25,1},{17,9},{1,25},{10,18},{2... | collective-permute-start | bytes 688136 | tf_op jit(solution)/shard_map/ppermute | solution.py:369
  30.0 8.6 %collective-permute-start.2 = (f32[8,32,128]{2,1,0:T(8,128)S(1)}, f32[8,32,128]{2,1,0:T(8,128)S(1)}, u32[]{:S(2)}, u32[]{:S(2)}) collective-permute-start(f32[8,32,128]{2,1,0:T(8,128)S(1)} %copy-done.3), channel_id=1, source_target_pairs={{0,1},{1,0},{2,3},{3,2},{4,5},{5,4},{6,7},{7,6},{8,9},{9,8},{10,11... | collective-permute-start | bytes 393224 | tf_op jit(solution)/shard_map/ppermute | solution.py:374
  31.9 4.6 %collective-permute-start = (f32[14,8,128]{2,1,0:T(8,128)S(1)}, f32[14,8,128]{2,1,0:T(8,128)S(1)}, u32[]{:S(2)}, u32[]{:S(2)}) collective-permute-start(f32[14,8,128]{2,1,0:T(8,128)S(1)} %copy-done.5), channel_id=1, source_target_pairs={{0,2},{2,4},{4,6},{6,0},{1,3},{3,5},{5,7},{7,1},{8,10},{10,12},{12... | collective-permute-start | bytes 172040 | tf_op jit(solution)/shard_map/ppermute | solution.py:374
  31.9 4.6 %collective-permute-start.1 = (f32[14,8,128]{2,1,0:T(8,128)S(1)}, f32[14,8,128]{2,1,0:T(8,128)S(1)}, u32[]{:S(2)}, u32[]{:S(2)}) collective-permute-start(f32[14,8,128]{2,1,0:T(8,128)S(1)} %copy-done.4), channel_id=1, source_target_pairs={{0,6},{2,0},{4,2},{6,4},{1,7},{3,1},{5,3},{7,5},{8,14},{10,8},{12,... | collective-permute-start | bytes 172040 | tf_op jit(solution)/shard_map/ppermute | solution.py:374
  41.8 0.7 %copy-start = (f32[14,32,128]{2,1,0:T(8,128)}, f32[14,32,128]{2,1,0:T(8,128)S(1)}, u32[]{:S(2)}) copy-start(f32[14,32,128]{2,1,0:T(8,128)S(1)} %collective-permute-done.3.xfirst) | copy-start | bytes 688132
  41.8 0.8 %copy-start.1 = (f32[14,32,128]{2,1,0:T(8,128)}, f32[14,32,128]{2,1,0:T(8,128)S(1)}, u32[]{:S(2)}) copy-start(f32[14,32,128]{2,1,0:T(8,128)S(1)} %collective-permute-done.4.xlast) | copy-start | bytes 688132

commit v8 on v7

--- a/solution.py
+++ b/solution.py
@@ -24,7 +24,7 @@
 OUT_PACK = "vvvvvvhhhhhvvv"
 OUT_Y = "v-"
 IN_OTHERS = "-"
-OUT_X = "h"
+OUT_X = "x"
 IN_FLUX = "vvvvvvvvvh"
 OUT_FLUX = "xxvvv"
 IN_RIM = "vvvvvvhhhh"
@@ -447,7 +447,8 @@
 
 def along_x_kernel(count, size_g, block, modes, own, *rest):
     others = rest[: count - 1]
-    table_y, tables, flat_table, out, everyone, gathered, potential, lines = rest[count - 1 :]
+    table_y, tables, flat_table, out, everyone, gathered, potential, lines, ready, semaphores = rest[count - 1 :]
+    leaving = []
     me = lax.axis_index("hx")
     everyone[me] = own[...]
     for step in range(1, count):
@@ -519,12 +520,16 @@
                 slot = 2 * width + side * nx + x
                 edge = jnp.where(lane == slot, turned(line(x, y // LANES), slot - y % LANES), edge)
         pieces.append(edge)
-        for g in range(size_g):
-            for p, piece in enumerate(pieces):
-                out[target * size_g + g, :, p * LANES : (p + 1) * LANES] = piece
-
-
-def gravity_kernel(planes, table, den, vel, carried, carried_rim, potential, momentum, energy, solved, edges):
+        for p, piece in enumerate(pieces):
+            ready[target, :, p * LANES : (p + 1) * LANES] = piece
+        leaving += copies_in(
+            [(ready.at[target], out.at[target * size_g + g]) for g in range(size_g)], semaphores.at[target]
+        )
+    for copy in leaving:
+        copy.wait()
+
+
+def gravity_kernel(planes, table, den, vel, carried, carried_rim, potential, momentum, energy, solved, edges, ready, semaphores):
     nx, ny, nz = den.shape
     groups, kz, width = planes.shape
     main = nx * ny
@@ -537,10 +542,11 @@
     edges[...] = lax.dot_general(
         flat[:, main:], here[:, :nz], contract, precision=highest, preferred_element_type=jnp.float32
     )
+    leaving = []
     row = lax.broadcasted_iota(jnp.int32, (ny, nz), 0)
     for x in range(nx):
         value = solved[x * ny : (x + 1) * ny, :nz]
-        potential[x] = value
+        ready[4, x] = value
         above = solved[(x + 1) * ny : (x + 2) * ny, :nz] if x < nx - 1 else edges[ny : 2 * ny]
         below = solved[(x - 1) * ny : x * ny, :nz] if x > 0 else edges[:ny]
         at = 2 * ny + x
@@ -555,9 +561,21 @@
         before = [carried_rim[d, x // (nx - 1)] if x in (0, nx - 1) else carried[d, x] for d in range(4)]
         work = before[3]
         for d in range(3):
-            momentum[d, x] = before[d] + kicks[d]
+            ready[d, x] = before[d] + kicks[d]
             work = work + kicks[d] * vel[d, x]
-        energy[x] = work
+        ready[3, x] = work
+        if x % 2:
+            pair = pl.ds(x - 1, 2)
+            leaving += copies_in(
+                [
+                    (ready.at[pl.ds(0, 3), pair], momentum.at[:, pair]),
+                    (ready.at[3, pair], energy.at[pair]),
+                    (ready.at[4, pair], potential.at[pair]),
+                ],
+                semaphores.at[x // 2],
+            )
+    for copy in leaving:
+        copy.wait()
 
 
 def step(density, velocity, pressure, species, newton_count):
@@ -642,6 +660,8 @@
             floats((all_x, all_y)),
             floats(((nx + 2) * kz, all_y)),
             floats(((nx + 2) * kz, all_y)),
+            floats((size_y, kz, width)),
+            pltpu.SemaphoreType.DMA((size_y, size_g)),
         ],
     )
     planes = lax.all_to_all(planes, ("hy", "ga"), split_axis=0, concat_axis=0, tiled=True)
@@ -681,8 +701,8 @@
         (planes, own_z, den, vel, carried, carried_rim),
         IN_GRAVITY,
         [(nx, ny, nz), (3, nx, ny, nz), (nx, ny, nz)],
-        "---",
-        [floats((main, 2 * nz)), floats((LANES, nz))],
+        "xxx",
+        [floats((main, 2 * nz)), floats((LANES, nz)), floats((5, nx, ny, nz)), pltpu.SemaphoreType.DMA((nx // 2, 3))],
     )
     return (new_density, momentum, total_energy, species_mass, potential)
 

time: 46.1 us -> 46.2 us (level)
  no operation moved by 1% of the time
where the time goes in v8:
time: 46.2 us; the launch traced here: 46 us
  starting transfers between devices  18 us (39%)
  waiting for transfers between devices  14.1 us (31%)
  Pallas kernels  12.3 us (27%)
  between operations  0.8 us (2%)
  local copies, waits for them, and re-layouts  0.77 us (2%)
    pallas_call x7, Pallas kernels, placed_call(): pl.pallas_call(kernel, out_shape=shapes, in_specs=specs, out_specs=[pl.Bl...  12.3 us
    ppermute x7, starting transfers between devices, exchanged(): lax.ppermute(value, axis, [(i, partner(i, step, count)) for i in range(co...  9.43 us
    ppermute x7, waiting for transfers between devices, exchanged(): lax.ppermute(value, axis, [(i, partner(i, step, count)) for i in range(co...  9.09 us
    ppermute x3, waiting for transfers between devices, shifted(): lax.ppermute(value, axis, [(i, (i + step) % count) for i in range(count)])  5 us
    ppermute x3, starting transfers between devices, shifted(): lax.ppermute(value, axis, [(i, (i + step) % count) for i in range(count)])  3.6 us
    all_to_all x1, starting transfers between devices, step(): lax.all_to_all(planes, ('hy', 'ga'), split_axis=0, concat_axis=0, tiled=T...  3.47 us
    ppermute x2, starting transfers between devices, faced_pairs(): return lax.ppermute(value, axis, pairs + [(b, a) for a, b in pairs])  1.49 us
  transfers between devices with their start and end apart: 13, of which 7 were waited for; matrix products, arithmetic and copies ran while one was open for 0% of the time, Pallas kernels for 18%

profile of v8, /device:TPU:0, one launch (start us, length us, event | category | flops | bytes accessed | tf_op | source)
XLA Modules:
  0.0 46.0 jit_solution(12041242023730819544)
XLA Ops:
  0.6 3.1 %collective-permute-start.5 = (f32[8,32,128]{2,1,0:T(8,128)}, f32[8,32,128]{2,1,0:T(8,128)S(1)}, u32[]{:S(2)}, u32[]{:S(2)}) collective-permute-start(f32[8,32,128]{2,1,0:T(8,128)} %den_at.1), channel_id=1, source_target_pairs={{0,1},{1,0},{2,3},{3,2},{4,5},{5,4},{6,7},{7,6},{8,9},{9,8},{10,11... | collective-permute-start | bytes 393224 | tf_op jit(solution)/shard_map/ppermute | solution.py:341
  3.7 3.4 %shard_map.137 = (f32[2,128,128]{2,1,0:T(8,128)S(1)}, f32[8,32,128]{2,1,0:T(8,128)S(1)}, f32[3,8,32,128]{3,2,1,0:T(8,128)S(1)}, f32[8,32,128]{2,1,0:T(8,128)S(1)...) custom-call(f32[8,32,128]{2,1,0:T(8,128)} %den_at.1, ...), custom_call_target="tpu_custom_call" | custom-call | tf_op jit(solution)/shard_map/pallas_call | solution.py:328
  7.1 0.0 copy-start.2
  7.1 0.0 copy-start.3
  7.1 0.0 copy-start.5
  7.1 0.0 copy-start.4
  7.1 0.3 collective-permute-done.5.rest_0_
  7.4 0.4 shard_map.140
  7.8 0.1 collective-permute-start.6
  7.9 1.8 %collective-permute-start.7 = (f32[32,256]{1,0:T(8,128)S(1)}, f32[32,256]{1,0:T(8,128)S(1)}, u32[]{:S(2)}, u32[]{:S(2)}) collective-permute-start(f32[32,256]{1,0:T(8,128)S(1)} %get-tuple-element.53), channel_id=1, source_target_pairs={{0,4},{2,6},{4,0},{6,2},{1,5},{3,7},{5,1},{7,3},{8,12},{10,14},{12... | collective-permute-start | bytes 98312 | tf_op jit(solution)/shard_map/ppermute | solution.py:341
  9.6 0.1 collective-permute-start.8
  9.7 0.0 collective-permute-done.6.rest_1_
  9.7 2.1 %collective-permute-done.7.rest_2_ = f32[32,256]{1,0:T(8,128)S(1)} collective-permute-done((f32[32,256]{1,0:T(8,128)S(1)}, f32[32,256]{1,0:T(8,128)S(1)}, u32[]{:S(2)}, u32[]{:S(2)}) %collective-permute-start.7) | collective-permute-done | bytes 32800 | tf_op jit(solution)/shard_map/ppermute | solution.py:341
  11.8 1.2 %collective-permute-done.8.rest_3_ = f32[32,256]{1,0:T(8,128)S(1)} collective-permute-done((f32[32,256]{1,0:T(8,128)S(1)}, f32[32,256]{1,0:T(8,128)S(1)}, u32[]{:S(2)}, u32[]{:S(2)}) %collective-permute-start.8) | collective-permute-done | bytes 32800 | tf_op jit(solution)/shard_map/ppermute | solution.py:341
  13.0 0.4 shard_map.141
  13.4 1.6 %collective-permute-start.9 = (f32[72,128]{1,0:T(8,128)S(1)}, f32[72,128]{1,0:T(8,128)S(1)}, u32[]{:S(2)}, u32[]{:S(2)}) collective-permute-start(f32[72,128]{1,0:T(8,128)S(1)} %get-tuple-element.58.own), channel_id=1, source_target_pairs={{0,8},{8,0},{16,24},{24,16},{1,9},{9,1},{17,25},{25,17},{2,10},{10... | collective-permute-start | bytes 110600 | tf_op jit(solution)/shard_map/ppermute | solution.py:341
  15.1 2.6 %collective-permute-start.10 = (f32[72,128]{1,0:T(8,128)S(1)}, f32[72,128]{1,0:T(8,128)S(1)}, u32[]{:S(2)}, u32[]{:S(2)}) collective-permute-start(f32[72,128]{1,0:T(8,128)S(1)} %get-tuple-element.58.own), channel_id=1, source_target_pairs={{0,16},{8,24},{16,0},{24,8},{1,17},{9,25},{17,1},{25,9},{2,18},{10... | collective-permute-start | bytes 110600 | tf_op jit(solution)/shard_map/ppermute | solution.py:341
  17.7 0.2 collective-permute-start.11
  17.9 0.0 collective-permute-done.9.rest_0_
  17.9 2.8 %collective-permute-done.10.rest_1_ = f32[72,128]{1,0:T(8,128)S(1)} collective-permute-done((f32[72,128]{1,0:T(8,128)S(1)}, f32[72,128]{1,0:T(8,128)S(1)}, u32[]{:S(2)}, u32[]{:S(2)}) %collective-permute-start.10) | collective-permute-done | bytes 36896 | tf_op jit(solution)/shard_map/ppermute | solution.py:341
  20.6 2.8 %collective-permute-done.11.rest_2_ = f32[72,128]{1,0:T(8,128)S(1)} collective-permute-done((f32[72,128]{1,0:T(8,128)S(1)}, f32[72,128]{1,0:T(8,128)S(1)}, u32[]{:S(2)}, u32[]{:S(2)}) %collective-permute-start.11) | collective-permute-done | bytes 36896 | tf_op jit(solution)/shard_map/ppermute | solution.py:341
  23.4 1.7 %shard_map.142 = f32[8,32,384]{2,1,0:T(8,128)} custom-call(f32[8,32,128]{2,1,0:T(8,128)S(1)} %get-tuple-element.57.modes, f32[72,128]{1,0:T(8,128)S(1)} %get-tuple-element.58.own, f32[72,128]{1,0:T(8,128)S(1)} %collective-permute-done.9.rest_0_, f32[72,128]{1,0:T(8,128)S(1)} %collective-permute-done.10.rest_1_, ...), custom_call_target="tpu_custom_call" | custom-call | tf_op jit(solution)/shard_map/pallas_call | solution.py:328
  25.1 3.5 %all-to-all-start = ((f32[8,32,384]{2,1,0:T(8,128)}), f32[8,32,384]{2,1,0:T(8,128)S(1)}, u32[]{:S(2)}, u32[]{:S(2)}) async-start(f32[8,32,384]{2,1,0:T(8,128)} %shard_map.142), calls=%async_computation | async-start | bytes 786432 | tf_op jit(solution)/shard_map/all_to_all | solution.py:667
  28.6 0.1 collective-permute-start.3
  28.6 0.0 copy-done.2
  28.7 1.4 %collective-permute-start.4 = (f32[14,32,128]{2,1,0:T(8,128)S(1)}, f32[14,32,128]{2,1,0:T(8,128)S(1)}, u32[]{:S(2)}, u32[]{:S(2)}) collective-permute-start(f32[14,32,128]{2,1,0:T(8,128)S(1)} %copy-done.2), channel_id=1, source_target_pairs={{8,16},{24,0},{16,8},{0,24},{9,17},{25,1},{17,9},{1,25},{10,18},{2... | collective-permute-start | bytes 688136 | tf_op jit(solution)/shard_map/ppermute | solution.py:369
  30.1 0.0 copy-done.3
  30.1 1.9 %collective-permute-start.2 = (f32[8,32,128]{2,1,0:T(8,128)S(1)}, f32[8,32,128]{2,1,0:T(8,128)S(1)}, u32[]{:S(2)}, u32[]{:S(2)}) collective-permute-start(f32[8,32,128]{2,1,0:T(8,128)S(1)} %copy-done.3), channel_id=1, source_target_pairs={{0,1},{1,0},{2,3},{3,2},{4,5},{5,4},{6,7},{7,6},{8,9},{9,8},{10,11... | collective-permute-start | bytes 393224 | tf_op jit(solution)/shard_map/ppermute | solution.py:374
  31.9 0.0 copy-done.5
  31.9 0.0 collective-permute-start
  31.9 0.0 copy-done.4
  31.9 1.7 %collective-permute-start.1 = (f32[14,8,128]{2,1,0:T(8,128)S(1)}, f32[14,8,128]{2,1,0:T(8,128)S(1)}, u32[]{:S(2)}, u32[]{:S(2)}) collective-permute-start(f32[14,8,128]{2,1,0:T(8,128)S(1)} %copy-done.4), channel_id=1, source_target_pairs={{0,6},{2,0},{4,2},{6,4},{1,7},{3,1},{5,3},{7,5},{8,14},{10,8},{12,... | collective-permute-start | bytes 172040 | tf_op jit(solution)/shard_map/ppermute | solution.py:374
  33.7 2.8 %collective-permute-done.ybelow = f32[14,8,128]{2,1,0:T(8,128)S(1)} collective-permute-done((f32[14,8,128]{2,1,0:T(8,128)S(1)}, f32[14,8,128]{2,1,0:T(8,128)S(1)}, u32[]{:S(2)}, u32[]{:S(2)}) %collective-permute-start) | collective-permute-done | bytes 57376 | tf_op jit(solution)/shard_map/ppermute | solution.py:374
  36.5 0.0 collective-permute-done.1.yabove
  36.5 2.2 %collective-permute-done.2.zbelow.zabove = f32[8,32,128]{2,1,0:T(8,128)S(1)} collective-permute-done((f32[8,32,128]{2,1,0:T(8,128)S(1)}, f32[8,32,128]{2,1,0:T(8,128)S(1)}, u32[]{:S(2)}, u32[]{:S(2)}) %collective-permute-start.2) | collective-permute-done | bytes 131104 | tf_op jit(solution)/shard_map/ppermute | solution.py:374
  38.7 3.1 %shard_map.138 = (f32[8,32,128]{2,1,0:T(8,128)}, f32[9,8,32,128]{3,2,1,0:T(8,128)}, f32[4,8,32,128]{3,2,1,0:T(8,128)S(1)}, f32[14,2,32,128]{3,2,1,0:T(8,128)S(1)}, f32[256,256]{1,0:T(8,128)S(1)}) custom-call(f32[8,32,128]{2,1,0:T(8,128)S(1)} %get-tuple-element.36.den, f32[3,8,32,128]{3,2,1,0:T(8,128)S(1)} %get-tuple-element.37.vel, ...), custom_call_target="tpu_custom_call" | custom-call | tf_op jit(solution)/shard_map/pallas_call | solution.py:328
  41.8 0.0 collective-permute-done.3.xfirst
  41.8 0.0 copy-start
  41.8 0.0 collective-permute-done.4.xlast
  41.8 0.0 copy-start.1
  41.8 0.7 %copy-done = f32[14,32,128]{2,1,0:T(8,128)} copy-done((f32[14,32,128]{2,1,0:T(8,128)}, f32[14,32,128]{2,1,0:T(8,128)S(1)}, u32[]{:S(2)}) %copy-start) | copy-done | bytes 229400
  42.5 0.1 copy-done.1
  42.6 1.9 %shard_map.139 = (f32[8,32,128]{2,1,0:T(8,128)}, f32[9,8,32,128]{3,2,1,0:T(8,128)}, f32[4,2,32,128]{3,2,1,0:T(8,128)S(1)}) custom-call(f32[8,32,128]{2,1,0:T(8,128)S(1)} %get-tuple-element.36.den, f32[3,8,32,128]{3,2,1,0:T(8,128)S(1)} %get-tuple-element.37.vel, ...), custom_call_target="tpu_custom_call", output_to_operand_aliasing={{0}: (8, {}), {1}: (9, {})} | custom-call | tf_op jit(solution)/shard_map/pallas_call | solution.py:328
  44.5 0.0 all-to-all-done.planes
  44.5 1.5 %shard_map.143 = (f32[8,32,128]{2,1,0:T(8,128)}, f32[3,8,32,128]{3,2,1,0:T(8,128)}, f32[8,32,128]{2,1,0:T(8,128)}) custom-call(f32[8,32,384]{2,1,0:T(8,128)S(1)} %all-to-all-done.planes, f32[256,256]{1,0:T(8,128)S(1)} %get-tuple-element.60.table, f32[8,32,128]{2,1,0:T(8,128)S(1)} %get-tuple-element.36.den, f32[3,8,32,128]{3,2,1,0:T(8,128)S(1)} %get-tuple-element.37.vel, ...), custom_call_target="tpu_custom_call" | custom-call | tf_op jit(solution)/shard_map/pallas_call | solution.py:328
Async XLA Ops:
  0.6 6.8 %collective-permute-start.5 = (f32[8,32,128]{2,1,0:T(8,128)}, f32[8,32,128]{2,1,0:T(8,128)S(1)}, u32[]{:S(2)}, u32[]{:S(2)}) collective-permute-start(f32[8,32,128]{2,1,0:T(8,128)} %den_at.1), channel_id=1, source_target_pairs={{0,1},{1,0},{2,3},{3,2},{4,5},{5,4},{6,7},{7,6},{8,9},{9,8},{10,11... | collective-permute-start | bytes 393224 | tf_op jit(solution)/shard_map/ppermute | solution.py:341
  7.1 21.6 %copy-start.2 = (f32[14,32,128]{2,1,0:T(8,128)S(1)}, f32[14,32,128]{2,1,0:T(8,128)}, u32[]{:S(2)}) copy-start(f32[14,32,128]{2,1,0:T(8,128)} %get-tuple-element.46) | copy-start | bytes 688132
  7.1 23.0 %copy-start.3 = (f32[8,32,128]{2,1,0:T(8,128)S(1)}, f32[8,32,128]{2,1,0:T(8,128)}, u32[]{:S(2)}) copy-start(f32[8,32,128]{2,1,0:T(8,128)} %get-tuple-element.43) | copy-start | bytes 393220
  7.1 24.8 %copy-start.5 = (f32[14,8,128]{2,1,0:T(8,128)S(1)}, f32[14,8,128]{2,1,0:T(8,128)}, u32[]{:S(2)}) copy-start(f32[14,8,128]{2,1,0:T(8,128)} %get-tuple-element.41) | copy-start | bytes 172036
  7.1 24.8 %copy-start.4 = (f32[14,8,128]{2,1,0:T(8,128)S(1)}, f32[14,8,128]{2,1,0:T(8,128)}, u32[]{:S(2)}) copy-start(f32[14,8,128]{2,1,0:T(8,128)} %get-tuple-element.42) | copy-start | bytes 172036
  7.8 1.9 %collective-permute-start.6 = (f32[32,256]{1,0:T(8,128)S(1)}, f32[32,256]{1,0:T(8,128)S(1)}, u32[]{:S(2)}, u32[]{:S(2)}) collective-permute-start(f32[32,256]{1,0:T(8,128)S(1)} %get-tuple-element.52), channel_id=1, source_target_pairs={{0,2},{2,0},{4,6},{6,4},{1,3},{3,1},{5,7},{7,5},{8,10},{10,8},{12,... | collective-permute-start | bytes 98312 | tf_op jit(solution)/shard_map/ppermute | solution.py:341
  7.9 4.0 %collective-permute-start.7 = (f32[32,256]{1,0:T(8,128)S(1)}, f32[32,256]{1,0:T(8,128)S(1)}, u32[]{:S(2)}, u32[]{:S(2)}) collective-permute-start(f32[32,256]{1,0:T(8,128)S(1)} %get-tuple-element.53), channel_id=1, source_target_pairs={{0,4},{2,6},{4,0},{6,2},{1,5},{3,7},{5,1},{7,3},{8,12},{10,14},{12... | collective-permute-start | bytes 98312 | tf_op jit(solution)/shard_map/ppermute | solution.py:341
  9.6 3.4 %collective-permute-start.8 = (f32[32,256]{1,0:T(8,128)S(1)}, f32[32,256]{1,0:T(8,128)S(1)}, u32[]{:S(2)}, u32[]{:S(2)}) collective-permute-start(f32[32,256]{1,0:T(8,128)S(1)} %get-tuple-element.54), channel_id=1, source_target_pairs={{0,6},{2,4},{4,2},{6,0},{1,7},{3,5},{5,3},{7,1},{8,14},{10,12},{12... | collective-permute-start | bytes 98312 | tf_op jit(solution)/shard_map/ppermute | solution.py:341
  13.4 4.5 %collective-permute-start.9 = (f32[72,128]{1,0:T(8,128)S(1)}, f32[72,128]{1,0:T(8,128)S(1)}, u32[]{:S(2)}, u32[]{:S(2)}) collective-permute-start(f32[72,128]{1,0:T(8,128)S(1)} %get-tuple-element.58.own), channel_id=1, source_target_pairs={{0,8},{8,0},{16,24},{24,16},{1,9},{9,1},{17,25},{25,17},{2,10},{10... | collective-permute-start | bytes 110600 | tf_op jit(solution)/shard_map/ppermute | solution.py:341
  15.1 5.6 %collective-permute-start.10 = (f32[72,128]{1,0:T(8,128)S(1)}, f32[72,128]{1,0:T(8,128)S(1)}, u32[]{:S(2)}, u32[]{:S(2)}) collective-permute-start(f32[72,128]{1,0:T(8,128)S(1)} %get-tuple-element.58.own), channel_id=1, source_target_pairs={{0,16},{8,24},{16,0},{24,8},{1,17},{9,25},{17,1},{25,9},{2,18},{10... | collective-permute-start | bytes 110600 | tf_op jit(solution)/shard_map/ppermute | solution.py:341
  17.7 5.8 %collective-permute-start.11 = (f32[72,128]{1,0:T(8,128)S(1)}, f32[72,128]{1,0:T(8,128)S(1)}, u32[]{:S(2)}, u32[]{:S(2)}) collective-permute-start(f32[72,128]{1,0:T(8,128)S(1)} %get-tuple-element.58.own), channel_id=1, source_target_pairs={{0,24},{8,16},{16,8},{24,0},{1,25},{9,17},{17,9},{25,1},{2,26},{10... | collective-permute-start | bytes 110600 | tf_op jit(solution)/shard_map/ppermute | solution.py:341
  25.1 19.4 %all-to-all-start = ((f32[8,32,384]{2,1,0:T(8,128)}), f32[8,32,384]{2,1,0:T(8,128)S(1)}, u32[]{:S(2)}, u32[]{:S(2)}) async-start(f32[8,32,384]{2,1,0:T(8,128)} %shard_map.142), calls=%async_computation | async-start | bytes 786432 | tf_op jit(solution)/shard_map/all_to_all | solution.py:667
  28.6 13.2 %collective-permute-start.3 = (f32[14,32,128]{2,1,0:T(8,128)}, f32[14,32,128]{2,1,0:T(8,128)S(1)}, u32[]{:S(2)}, u32[]{:S(2)}) collective-permute-start(f32[14,32,128]{2,1,0:T(8,128)} %get-tuple-element.45), channel_id=1, source_target_pairs={{0,8},{16,24},{8,0},{24,16},{1,9},{17,25},{9,1},{25,17},{2,10},{18... | collective-permute-start | bytes 688136 | tf_op jit(solution)/shard_map/ppermute | solution.py:369
  28.7 13.2 %collective-permute-start.4 = (f32[14,32,128]{2,1,0:T(8,128)S(1)}, f32[14,32,128]{2,1,0:T(8,128)S(1)}, u32[]{:S(2)}, u32[]{:S(2)}) collective-permute-start(f32[14,32,128]{2,1,0:T(8,128)S(1)} %copy-done.2), channel_id=1, source_target_pairs={{8,16},{24,0},{16,8},{0,24},{9,17},{25,1},{17,9},{1,25},{10,18},{2... | collective-permute-start | bytes 688136 | tf_op jit(solution)/shard_map/ppermute | solution.py:369
  30.1 8.6 %collective-permute-start.2 = (f32[8,32,128]{2,1,0:T(8,128)S(1)}, f32[8,32,128]{2,1,0:T(8,128)S(1)}, u32[]{:S(2)}, u32[]{:S(2)}) collective-permute-start(f32[8,32,128]{2,1,0:T(8,128)S(1)} %copy-done.3), channel_id=1, source_target_pairs={{0,1},{1,0},{2,3},{3,2},{4,5},{5,4},{6,7},{7,6},{8,9},{9,8},{10,11... | collective-permute-start | bytes 393224 | tf_op jit(solution)/shard_map/ppermute | solution.py:374
  31.9 4.6 %collective-permute-start = (f32[14,8,128]{2,1,0:T(8,128)S(1)}, f32[14,8,128]{2,1,0:T(8,128)S(1)}, u32[]{:S(2)}, u32[]{:S(2)}) collective-permute-start(f32[14,8,128]{2,1,0:T(8,128)S(1)} %copy-done.5), channel_id=1, source_target_pairs={{0,2},{2,4},{4,6},{6,0},{1,3},{3,5},{5,7},{7,1},{8,10},{10,12},{12... | collective-permute-start | bytes 172040 | tf_op jit(solution)/shard_map/ppermute | solution.py:374
  31.9 4.6 %collective-permute-start.1 = (f32[14,8,128]{2,1,0:T(8,128)S(1)}, f32[14,8,128]{2,1,0:T(8,128)S(1)}, u32[]{:S(2)}, u32[]{:S(2)}) collective-permute-start(f32[14,8,128]{2,1,0:T(8,128)S(1)} %copy-done.4), channel_id=1, source_target_pairs={{0,6},{2,0},{4,2},{6,4},{1,7},{3,1},{5,3},{7,5},{8,14},{10,8},{12,... | collective-permute-start | bytes 172040 | tf_op jit(solution)/shard_map/ppermute | solution.py:374
  41.8 0.7 %copy-start = (f32[14,32,128]{2,1,0:T(8,128)}, f32[14,32,128]{2,1,0:T(8,128)S(1)}, u32[]{:S(2)}) copy-start(f32[14,32,128]{2,1,0:T(8,128)S(1)} %collective-permute-done.3.xfirst) | copy-start | bytes 688132
  41.8 0.8 %copy-start.1 = (f32[14,32,128]{2,1,0:T(8,128)}, f32[14,32,128]{2,1,0:T(8,128)S(1)}, u32[]{:S(2)}) copy-start(f32[14,32,128]{2,1,0:T(8,128)S(1)} %collective-permute-done.4.xlast) | copy-start | bytes 688132
